TPU v7x, 32 devices: a whole 2x2x4 slice. The times are simulated.
32 devices in a mesh: seq: 8 (over y, x, core), head: 4 (over z).
Axes of the slice: x: 2, y: 2, z: 4, core: 2. Of those that a mesh axis runs over, the one named last changes fastest.
Arguments:
- queries: bfloat16 [2048, 4096], P(('seq', 'head')), may hold values from -10 to 10
- keys: bfloat16 [2048, 1024], P(('seq', 'head')), may hold values from -10 to 10
- block_pos: int32 [16], replicated, may hold values from 0 to 15, each once
- query_map: float32 [32, 128, 128], P('head'), may hold values from -4 to 4
- key_map: float32 [8, 128, 128], P('head'), may hold values from -4 to 4
Outputs:
- query_map_gradient: float32 [32, 128, 128], P('head')
- key_map_gradient: float32 [8, 128, 128], P('head')
Inputs may be any that keep to these rules, and one draw needn't show every extreme that they name: A permutation: stored block g (token rows g * 128 to (g + 1) * 128 - 1) holds position block block_pos[g]; position blocks below 8 form the first sequence, the others the second.
All inputs are finite; a program needn't handle non-finite values.
Results may differ from a plain program's by a relative error of at most 0.0021.
Values may be sent and summed in bfloat16 or wider, within the bound.
No kernel may reach another device: no remote copies, remote signals or barrier semaphores. Data moves between devices by JAX's collectives and lax.ppermute only.
A program may use at most 64 MiB of HBM per device.

v0:
```python
import math

import jax
import jax.numpy as jnp
from jax import lax
from jax.sharding import PartitionSpec as P

HEAD_SIZE = 128
BLK = 128


HIGHEST = lax.Precision.HIGHEST
NEG_FLOOR = -1e30


def softmax_pair(logits):
    return jnp.concatenate(
        [jax.nn.softmax(logits, axis=-1), jax.nn.softmax(-logits, axis=-1)], axis=-1
    )


def feature_grad(feature, upstream):
    half_width = feature.shape[-1] // 2
    positive, negative = (feature[..., :half_width], feature[..., half_width:])
    grad_positive, grad_negative = (upstream[..., :half_width], upstream[..., half_width:])
    first = positive * (grad_positive - jnp.sum(grad_positive * positive, axis=-1, keepdims=True))
    second = negative * (grad_negative - jnp.sum(grad_negative * negative, axis=-1, keepdims=True))
    return first - second


def row_places(row_index, block_pos, seq_count):
    stored = row_index // BLK
    lookup = stored[:, None] == jnp.arange(block_pos.shape[0], dtype=jnp.int32)[None, :]
    blocks = jnp.sum(jnp.where(lookup, block_pos[None, :], 0), axis=1)
    return (blocks // seq_count, blocks * BLK + row_index % BLK)


def over_blocks(running, portions, step_fn):
    row_count = portions[0].shape[1]
    step_rows = math.gcd(row_count, 512)

    def advance(number, inner_carry):
        slabs = tuple(
            (
                lax.dynamic_slice_in_dim(portion, number * step_rows, step_rows, 1)
                for portion in portions
            )
        )
        return step_fn(inner_carry, slabs, number * step_rows)

    return lax.fori_loop(0, row_count // step_rows, advance, running)


def per_device(queries, keys, block_pos, query_map, key_map):
    local_q, local_k = (
        lax.all_to_all(queries, "head", split_axis=1, concat_axis=0, tiled=True),
        lax.all_to_all(keys, "head", split_axis=1, concat_axis=0, tiled=True),
    )
    seq_count = lax.axis_size("seq")
    seq_rank = lax.axis_index("seq")
    rows_local = local_k.shape[0]
    token_count = rows_local * seq_count
    key_heads = key_map.shape[0]
    group_width = query_map.shape[0] // key_heads
    score_scale = HEAD_SIZE ** (-0.5)
    query_index = seq_rank * rows_local + jnp.arange(rows_local, dtype=jnp.int32)
    query_heads = local_q.reshape(rows_local, key_heads, group_width, HEAD_SIZE).transpose(
        1, 2, 0, 3
    )
    query_wide = query_heads.astype(jnp.float32)
    query_logits = jnp.einsum(
        "vgnd,vgde->vgne",
        query_wide,
        query_map.reshape(key_heads, group_width, HEAD_SIZE, HEAD_SIZE),
        precision=HIGHEST,
    )
    rows_all = group_width * rows_local
    phi_query = softmax_pair(query_logits).reshape(key_heads, rows_all, 2 * HEAD_SIZE)
    phi_query_b = phi_query.astype(jnp.bfloat16)
    query_flat = query_heads.reshape(key_heads, rows_all, HEAD_SIZE)
    query_seq, query_at = row_places(query_index, block_pos, seq_count)
    query_seq = jnp.tile(query_seq, group_width)
    query_at = jnp.tile(query_at, group_width)

    def visible_for(offset, slab_rows):
        key_index = offset + jnp.arange(slab_rows, dtype=jnp.int32)
        key_seq, key_at = row_places(key_index, block_pos, seq_count)
        return (key_seq[None, :] == query_seq[:, None]) & (key_at[None, :] <= query_at[:, None])

    def key_features(key_slab):
        logits = jnp.einsum(
            "vwd,vde->vwe", key_slab.astype(jnp.float32), key_map, precision=HIGHEST
        )
        return softmax_pair(logits)

    def teacher(key_slab):
        return (
            jnp.einsum("vrd,vwd->vrw", query_flat, key_slab, preferred_element_type=jnp.float32)
            * score_scale
        )

    def stats_step(running, slabs, offset):
        key_slab = slabs[0]
        visible = visible_for(offset, key_slab.shape[1])

        def stats_compute_live(current):
            highest, denominator, linear_sum = current
            masked = jnp.where(visible[None], teacher(key_slab), NEG_FLOOR)
            new_high = jnp.maximum(highest, jnp.max(masked, axis=-1))
            exponent = jnp.where(visible[None], jnp.exp(masked - new_high[..., None]), 0.0)
            denominator = denominator * jnp.exp(highest - new_high) + jnp.sum(exponent, axis=-1)
            phi_key_b = key_features(key_slab).astype(jnp.bfloat16)
            linear = jnp.einsum(
                "vrf,vwf->vrw", phi_query_b, phi_key_b, preferred_element_type=jnp.float32
            )
            linear_sum = linear_sum + jnp.sum(jnp.where(visible[None], linear, 0.0), axis=-1)
            return (new_high, denominator, linear_sum)

        return lax.cond(jnp.any(visible), stats_compute_live, lambda current: current, running)

    def grads_step(running, slabs, offset):
        key_slab = slabs[0]
        visible = visible_for(offset, key_slab.shape[1])

        def grads_compute_live(current):
            query_grad, key_weight_grad = current
            masked = jnp.where(visible[None], teacher(key_slab), NEG_FLOOR)
            exponent = jnp.where(visible[None], jnp.exp(masked - highest[..., None]), 0.0)
            teacher_prob = exponent / denominator[..., None]
            phi_key = key_features(key_slab)
            phi_key_b = phi_key.astype(jnp.bfloat16)
            linear = jnp.einsum(
                "vrf,vwf->vrw", phi_query_b, phi_key_b, preferred_element_type=jnp.float32
            )
            weights = (
                jnp.where(visible[None], 1.0 / linear_sum[..., None] - teacher_prob / linear, 0.0)
                / token_count
            ).astype(jnp.bfloat16)
            query_grad = query_grad + jnp.einsum(
                "vrw,vwf->vrf", weights, phi_key_b, preferred_element_type=jnp.float32
            )
            key_grad = jnp.einsum(
                "vrw,vrf->vwf", weights, phi_query_b, preferred_element_type=jnp.float32
            )
            key_logit_grad = feature_grad(phi_key, key_grad)
            key_weight_grad = key_weight_grad + jnp.einsum(
                "vwd,vwe->vde", key_slab.astype(jnp.float32), key_logit_grad, precision=HIGHEST
            )
            return (query_grad, key_weight_grad)

        return lax.cond(jnp.any(visible), grads_compute_live, lambda current: current, running)

    def as_heads(pieces):
        return pieces.reshape(pieces.shape[0], key_heads, -1).transpose(1, 0, 2)

    row_zeros = jnp.zeros((key_heads, rows_all), jnp.float32)
    stats_init = (jnp.full((key_heads, rows_all), NEG_FLOOR, jnp.float32), row_zeros, row_zeros)
    grads_init = (
        jnp.zeros((key_heads, rows_all, 2 * HEAD_SIZE), jnp.float32),
        jnp.zeros((key_heads, HEAD_SIZE, HEAD_SIZE), jnp.float32),
    )
    highest, denominator, linear_sum = over_blocks(
        stats_init, (as_heads(lax.all_gather(local_k, "seq", axis=0, tiled=True)),), stats_step
    )
    query_grad, key_weight_grad = over_blocks(
        grads_init, (as_heads(lax.all_gather(local_k, "seq", axis=0, tiled=True)),), grads_step
    )
    query_logit_grad = feature_grad(phi_query, query_grad).reshape(
        key_heads, group_width, rows_local, HEAD_SIZE
    )
    query_weight_grad = jnp.einsum(
        "vgnd,vgne->vgde", query_wide, query_logit_grad, precision=HIGHEST
    ).reshape(key_heads * group_width, HEAD_SIZE, HEAD_SIZE)
    query_map_gradient, key_map_gradient = lax.psum((query_weight_grad, key_weight_grad), "seq")
    return (query_map_gradient, key_map_gradient)


def solution(mesh):
    in_specs = (
        P(("seq", "head"), None),
        P(("seq", "head"), None),
        P(),
        P("head", None, None),
        P("head", None, None),
    )
    out_specs = (P("head", None, None), P("head", None, None))
    return jax.shard_map(
        per_device, mesh=mesh, in_specs=in_specs, out_specs=out_specs, check_vma=False
    )
```

profile of v0, /device:TPU:0, one launch (start us, length us, event | category | flops | bytes accessed | tf_op | source)
XLA Modules:
  0.0 218.9 jit_solution(3189689803761205006)
XLA Ops:
  8.8 6.3 %all-to-all-start.1 = ((bf16[64,4,256]{2,0,1:T(8,128)(2,1)}), bf16[64,4,256]{2,0,1:T(8,128)(2,1)S(1)}, u32[]{:S(2)}, u32[]{:S(2)}) async-start(bf16[64,4,256]{2,0,1:T(8,128)(2,1)} %bitcast.86), calls=%async_computation.1 | async-start | bytes 262144 | tf_op jit(solution)/shard_map/all_to_all | solution.py:57
  17.0 4.2 %all-to-all-done.1 = bf16[64,4,256]{2,0,1:T(8,128)(2,1)S(1)} async-done(((bf16[64,4,256]{2,0,1:T(8,128)(2,1)}), bf16[64,4,256]{2,0,1:T(8,128)(2,1)S(1)}, u32[]{:S(2)}, u32[]{:S(2)}) %all-to-all-start.1) | async-done | bytes 131104 | tf_op jit(solution)/shard_map/all_to_all | solution.py:57
  21.2 3.5 %all-to-all-start = ((bf16[64,4,1024]{2,0,1:T(8,128)(2,1)}), bf16[64,4,1024]{2,0,1:T(8,128)(2,1)S(1)}, u32[]{:S(2)}, u32[]{:S(2)}) async-start(bf16[64,4,1024]{2,0,1:T(8,128)(2,1)} %bitcast.85), calls=%async_computation | async-start | bytes 1048576 | tf_op jit(solution)/shard_map/all_to_all | solution.py:56
  27.3 10.6 %all-to-all-done = bf16[64,4,1024]{2,0,1:T(8,128)(2,1)S(1)} async-done(((bf16[64,4,1024]{2,0,1:T(8,128)(2,1)}), bf16[64,4,1024]{2,0,1:T(8,128)(2,1)S(1)}, u32[]{:S(2)}, u32[]{:S(2)}) %all-to-all-start) | async-done | bytes 524320 | tf_op jit(solution)/shard_map/all_to_all | solution.py:56
  41.6 3.0 %pad_maximum_fusion.3 = f32[2,4,256,256]{2,3,1,0:T(8,128)} fusion(f32[2,4,256,128]{2,3,1,0:T(8,128)} %fusion.93, f32[2,4,256,128]{2,3,1,0:T(8,128)} %fusion.95), kind=kLoop, calls=%fused_computation.126 | loop fusion | flops 524288 | bytes 4194304 | tf_op jit(solution)/shard_map/concatenate | solution.py:17
  47.8 2.3 %copy.101 = bf16[2,1024,256]{1,2,0:T(8,128)(2,1)} copy(bf16[2,1024,256]{2,1,0:T(8,128)(2,1)} %bitcast_convert_fusion) | data formatting | bytes 2097152
  50.0 2.8 %all-gather.2.cloned.1.call-done = bf16[2048,256]{1,0:T(8,128)(2,1)} async-done(((bf16[256,256]{1,0:T(8,128)(2,1)}), bf16[2048,256]{1,0:T(8,128)(2,1)}) %all-gather.2.cloned.1.call-update) | async-done | bytes 1048592 | tf_op jit(solution)/shard_map/all_gather | solution.py:166
  52.8 2.3 %copy.96 = bf16[2048,256]{0,1:T(8,128)(2,1)} copy(bf16[2048,256]{1,0:T(8,128)(2,1)} %all-gather.2.cloned.1.call-done) | data formatting | bytes 2097152 | tf_op jit(solution)/shard_map/all_gather | solution.py:166
  55.1 2.3 %copy.97 = bf16[2,2048,128]{2,1,0:T(8,128)(2,1)} copy(bf16[2,2048,128]{1,2,0:T(8,128)(2,1)} %bitcast.103) | data formatting | bytes 2097152
  57.4 35.5 %while.40 = (s32[]{:T(128)}, f32[2,1024]{1,0:T(2,128)S(1)}, f32[2,1024]{1,0:T(2,128)S(1)}, f32[2,1024]{1,0:T(2,128)S(1)}, s32[16]{0:T(128)S(1)}, /*index=5*/bf16...) while((s32[]{:T(128)}, f32[2,1024]{1,0:T(2,128)S(1)}, ...), condition=%wide.region_17.18_spmd.clone, body=%wide.region_5.17_spmd.clone.sunk | while | flops 1021495552 | bytes 21834140 | solution.py:51
  59.5 6.8 %conditional.6 = ((f32[2,1024]{1,0:T(2,128)S(1)}, f32[2,1024]{1,0:T(2,128)S(1)}, f32[2,1024]{1,0:T(2,128)S(1)})) conditional(s32[]{:T(128)} %convert_element_type.44, (f32[2,1024]{1,0:T(2,128)S(1)}, f32[2,1024]{1,0:T(2,128)S(1)}, f32[2,1024]{1,0:T(2,128)S(1)}) %tuple.150, (pred[1024,512]{0,1:T(8,128)(4,1)S(1)}, s32[]{:T(128)}, ...), branch_computations={%region_8.8_spmd, %region_9.16_spmd} | conditional | flops 1019351296 | bytes 21258342 | solution.py:119
  68.4 6.8 %conditional.6 = ((f32[2,1024]{1,0:T(2,128)S(1)}, f32[2,1024]{1,0:T(2,128)S(1)}, f32[2,1024]{1,0:T(2,128)S(1)})) conditional(s32[]{:T(128)} %convert_element_type.44, (f32[2,1024]{1,0:T(2,128)S(1)}, f32[2,1024]{1,0:T(2,128)S(1)}, f32[2,1024]{1,0:T(2,128)S(1)}) %tuple.150, (pred[1024,512]{0,1:T(8,128)(4,1)S(1)}, s32[]{:T(128)}, ...), branch_computations={%region_8.8_spmd, %region_9.16_spmd} | conditional | flops 1019351296 | bytes 21258342 | solution.py:119
  77.2 6.8 %conditional.6 = ((f32[2,1024]{1,0:T(2,128)S(1)}, f32[2,1024]{1,0:T(2,128)S(1)}, f32[2,1024]{1,0:T(2,128)S(1)})) conditional(s32[]{:T(128)} %convert_element_type.44, (f32[2,1024]{1,0:T(2,128)S(1)}, f32[2,1024]{1,0:T(2,128)S(1)}, f32[2,1024]{1,0:T(2,128)S(1)}) %tuple.150, (pred[1024,512]{0,1:T(8,128)(4,1)S(1)}, s32[]{:T(128)}, ...), branch_computations={%region_8.8_spmd, %region_9.16_spmd} | conditional | flops 1019351296 | bytes 21258342 | solution.py:119
  86.1 6.8 %conditional.6 = ((f32[2,1024]{1,0:T(2,128)S(1)}, f32[2,1024]{1,0:T(2,128)S(1)}, f32[2,1024]{1,0:T(2,128)S(1)})) conditional(s32[]{:T(128)} %convert_element_type.44, (f32[2,1024]{1,0:T(2,128)S(1)}, f32[2,1024]{1,0:T(2,128)S(1)}, f32[2,1024]{1,0:T(2,128)S(1)}) %tuple.150, (pred[1024,512]{0,1:T(8,128)(4,1)S(1)}, s32[]{:T(128)}, ...), branch_computations={%region_8.8_spmd, %region_9.16_spmd} | conditional | flops 1019351296 | bytes 21258342 | solution.py:119
  93.1 53.8 %while.41 = (s32[]{:T(128)}, f32[2,1024,256]{2,1,0:T(8,128)S(1)}, f32[2,128,128]{2,1,0:T(8,128)S(1)}, s32[16]{0:T(128)S(1)}, f32[2,1024]{1,0:T(2,128)S(1)}, /*in...) while((s32[]{:T(128)}, f32[2,1024,256]{2,1,0:T(8,128)S(1)}, ...), condition=%wide.region_29.30_spmd.clone, body=%wide.region_18.29_spmd.clone.sunk | while | flops 2299869440 | bytes 40643016 | solution.py:51
  95.7 10.8 %conditional.7 = ((f32[2,1024,256]{2,1,0:T(8,128)S(1)}, f32[2,128,128]{2,1,0:T(8,128)S(1)})) conditional(s32[]{:T(128)} %convert_element_type.45, (f32[2,1024,256]{2,1,0:T(8,128)S(1)}, f32[2,128,128]{2,1,0:T(8,128)S(1)}) %tuple.156, (pred[1024,512]{0,1:T(8,128)(4,1)}, f32[2,1024]{1,0:T(2,128)S(1)}, s32[]{:T(128)}, ...), branch_computations={%region_21.21_spmd, %region_22.28_spmd} | conditional | flops 2297725184 | bytes 40067196 | solution.py:151
  100.0 2.5 %fusion.35 = bf16[2,1024,512]{1,2,0:T(8,128)(2,1)S(1)} fusion(f32[2,512,1024]{2,1,0:T(8,128)S(1)} %fusion.53, bf16[2,1024,256]{1,2,0:T(8,128)(2,1)S(1)} %copy-done.1, f32[2,1024]{1,0:T(2,128)S(1)} %get-tuple-element.811, f32[2,1024]{1,0:T(2,128)S(1)} %get-tuple-element.810, f32[2,1024]{1,0:T(2,128)S(1)} %broadcast_divide_fusion.2, ...), kind=kOutput, calls=%fused_computation.40 | convolution fusion | flops 548405248 | bytes 8413184 | tf_op jit(solution)/shard_map/while/body/eval_jaxpr/cond/branch_1_fun/vrf,vwf->vrw/dot_general | solution.py:132
  109.2 10.8 %conditional.7 = ((f32[2,1024,256]{2,1,0:T(8,128)S(1)}, f32[2,128,128]{2,1,0:T(8,128)S(1)})) conditional(s32[]{:T(128)} %convert_element_type.45, (f32[2,1024,256]{2,1,0:T(8,128)S(1)}, f32[2,128,128]{2,1,0:T(8,128)S(1)}) %tuple.156, (pred[1024,512]{0,1:T(8,128)(4,1)}, f32[2,1024]{1,0:T(2,128)S(1)}, s32[]{:T(128)}, ...), branch_computations={%region_21.21_spmd, %region_22.28_spmd} | conditional | flops 2297725184 | bytes 40067196 | solution.py:151
  113.5 2.5 %fusion.35 = bf16[2,1024,512]{1,2,0:T(8,128)(2,1)S(1)} fusion(f32[2,512,1024]{2,1,0:T(8,128)S(1)} %fusion.53, bf16[2,1024,256]{1,2,0:T(8,128)(2,1)S(1)} %copy-done.1, f32[2,1024]{1,0:T(2,128)S(1)} %get-tuple-element.811, f32[2,1024]{1,0:T(2,128)S(1)} %get-tuple-element.810, f32[2,1024]{1,0:T(2,128)S(1)} %broadcast_divide_fusion.2, ...), kind=kOutput, calls=%fused_computation.40 | convolution fusion | flops 548405248 | bytes 8413184 | tf_op jit(solution)/shard_map/while/body/eval_jaxpr/cond/branch_1_fun/vrf,vwf->vrw/dot_general | solution.py:132
  122.7 10.8 %conditional.7 = ((f32[2,1024,256]{2,1,0:T(8,128)S(1)}, f32[2,128,128]{2,1,0:T(8,128)S(1)})) conditional(s32[]{:T(128)} %convert_element_type.45, (f32[2,1024,256]{2,1,0:T(8,128)S(1)}, f32[2,128,128]{2,1,0:T(8,128)S(1)}) %tuple.156, (pred[1024,512]{0,1:T(8,128)(4,1)}, f32[2,1024]{1,0:T(2,128)S(1)}, s32[]{:T(128)}, ...), branch_computations={%region_21.21_spmd, %region_22.28_spmd} | conditional | flops 2297725184 | bytes 40067196 | solution.py:151
  126.9 2.5 %fusion.35 = bf16[2,1024,512]{1,2,0:T(8,128)(2,1)S(1)} fusion(f32[2,512,1024]{2,1,0:T(8,128)S(1)} %fusion.53, bf16[2,1024,256]{1,2,0:T(8,128)(2,1)S(1)} %copy-done.1, f32[2,1024]{1,0:T(2,128)S(1)} %get-tuple-element.811, f32[2,1024]{1,0:T(2,128)S(1)} %get-tuple-element.810, f32[2,1024]{1,0:T(2,128)S(1)} %broadcast_divide_fusion.2, ...), kind=kOutput, calls=%fused_computation.40 | convolution fusion | flops 548405248 | bytes 8413184 | tf_op jit(solution)/shard_map/while/body/eval_jaxpr/cond/branch_1_fun/vrf,vwf->vrw/dot_general | solution.py:132
  136.1 10.8 %conditional.7 = ((f32[2,1024,256]{2,1,0:T(8,128)S(1)}, f32[2,128,128]{2,1,0:T(8,128)S(1)})) conditional(s32[]{:T(128)} %convert_element_type.45, (f32[2,1024,256]{2,1,0:T(8,128)S(1)}, f32[2,128,128]{2,1,0:T(8,128)S(1)}) %tuple.156, (pred[1024,512]{0,1:T(8,128)(4,1)}, f32[2,1024]{1,0:T(2,128)S(1)}, s32[]{:T(128)}, ...), branch_computations={%region_21.21_spmd, %region_22.28_spmd} | conditional | flops 2297725184 | bytes 40067196 | solution.py:151
  140.4 2.5 %fusion.35 = bf16[2,1024,512]{1,2,0:T(8,128)(2,1)S(1)} fusion(f32[2,512,1024]{2,1,0:T(8,128)S(1)} %fusion.53, bf16[2,1024,256]{1,2,0:T(8,128)(2,1)S(1)} %copy-done.1, f32[2,1024]{1,0:T(2,128)S(1)} %get-tuple-element.811, f32[2,1024]{1,0:T(2,128)S(1)} %get-tuple-element.810, f32[2,1024]{1,0:T(2,128)S(1)} %broadcast_divide_fusion.2, ...), kind=kOutput, calls=%fused_computation.40 | convolution fusion | flops 548405248 | bytes 8413184 | tf_op jit(solution)/shard_map/while/body/eval_jaxpr/cond/branch_1_fun/vrf,vwf->vrw/dot_general | solution.py:132
  153.1 55.4 %all-reduce.3.cloned.1.call-done = (f32[8,128,128]{2,1,0:T(8,128)}, f32[2,128,128]{2,1,0:T(8,128)}) async-done(((f32[8,128,128]{2,1,0:T(8,128)}, f32[2,128,128]{2,1,0:T(8,128)}), (f32[8,128,128]{2,1,0:T(8,128)}, f32[2,128,128]{2,1,0:T(8,128)})) %all-reduce.3.cloned.1.call-update) | async-done | bytes 655376 | tf_op jit(solution)/shard_map/psum | solution.py:174
  (206 shorter events, 95.8 us)
Async XLA Ops:
  7.2 31.2 %copy-start = (f32[8,128,128]{2,1,0:T(8,128)S(1)}, f32[8,128,128]{2,1,0:T(8,128)}, u32[]{:S(2)}) copy-start(f32[8,128,128]{2,1,0:T(8,128)} %param.16) | copy-start | bytes 1572868
  8.8 12.4 %all-to-all-start.1 = ((bf16[64,4,256]{2,0,1:T(8,128)(2,1)}), bf16[64,4,256]{2,0,1:T(8,128)(2,1)S(1)}, u32[]{:S(2)}, u32[]{:S(2)}) async-start(bf16[64,4,256]{2,0,1:T(8,128)(2,1)} %bitcast.86), calls=%async_computation.1 | async-start | bytes 262144 | tf_op jit(solution)/shard_map/all_to_all | solution.py:57
  21.2 3.5 %copy-start.8 = (bf16[64,4,256]{2,0,1:T(8,128)(2,1)}, bf16[64,4,256]{2,0,1:T(8,128)(2,1)S(1)}, u32[]{:S(2)}) copy-start(bf16[64,4,256]{2,0,1:T(8,128)(2,1)S(1)} %all-to-all-done.1) | copy-start | bytes 393220
  21.2 16.7 %all-to-all-start = ((bf16[64,4,1024]{2,0,1:T(8,128)(2,1)}), bf16[64,4,1024]{2,0,1:T(8,128)(2,1)S(1)}, u32[]{:S(2)}, u32[]{:S(2)}) async-start(bf16[64,4,1024]{2,0,1:T(8,128)(2,1)} %bitcast.85), calls=%async_computation | async-start | bytes 1048576 | tf_op jit(solution)/shard_map/all_to_all | solution.py:56
  24.7 28.1 %all-gather.2.cloned.1.call-start = ((), (), s32[]{:S(2)}) async-start(), calls=%async_computation.2 | async-start | bytes 1179648 | tf_op jit(solution)/shard_map/all_gather | solution.py:166
  25.4 183.1 %all-reduce.3.cloned.1.call-start = ((), (), s32[]{:S(2)}) async-start(), calls=%async_computation.3 | async-start | bytes 1310720 | tf_op jit(solution)/shard_map/psum | solution.py:174
  38.3 3.3 %copy-start.4 = (bf16[256,2,4,128]{3,2,1,0:T(4,128)(2,1)}, bf16[256,2,4,128]{3,2,1,0:T(4,128)(2,1)S(1)}, u32[]{:S(2)}) copy-start(bf16[256,2,4,128]{3,2,1,0:T(4,128)(2,1)S(1)} %reshape.230) | copy-start | bytes 1572868
  46.5 10.8 %copy-start.2 = (f32[2,4,256,256]{3,2,1,0:T(8,128)}, f32[2,4,256,256]{3,2,1,0:T(8,128)S(1)}, u32[]{:S(2)}) copy-start(f32[2,4,256,256]{3,2,1,0:T(8,128)S(1)} %copy.94) | copy-start | bytes 6291460
  46.5 10.8 %copy-start.9 = (s32[16]{0:T(128)S(1)}, s32[16]{0:T(128)}, u32[]{:S(2)}) copy-start(s32[16]{0:T(128)} %param.15) | copy-start | bytes 196
  59.5 2.6 %copy-start.6 = (bf16[2,1024,256]{2,1,0:T(8,128)(2,1)S(1)}, bf16[2,1024,256]{2,1,0:T(8,128)(2,1)}, u32[]{:S(2)}) copy-start(bf16[2,1024,256]{2,1,0:T(8,128)(2,1)} %get-tuple-element.788) | copy-start | bytes 3145732 | tf_op jit(solution)/shard_map/while/body/eval_jaxpr/cond
  68.4 2.6 %copy-start.6 = (bf16[2,1024,256]{2,1,0:T(8,128)(2,1)S(1)}, bf16[2,1024,256]{2,1,0:T(8,128)(2,1)}, u32[]{:S(2)}) copy-start(bf16[2,1024,256]{2,1,0:T(8,128)(2,1)} %get-tuple-element.788) | copy-start | bytes 3145732 | tf_op jit(solution)/shard_map/while/body/eval_jaxpr/cond
  77.3 2.6 %copy-start.6 = (bf16[2,1024,256]{2,1,0:T(8,128)(2,1)S(1)}, bf16[2,1024,256]{2,1,0:T(8,128)(2,1)}, u32[]{:S(2)}) copy-start(bf16[2,1024,256]{2,1,0:T(8,128)(2,1)} %get-tuple-element.788) | copy-start | bytes 3145732 | tf_op jit(solution)/shard_map/while/body/eval_jaxpr/cond
  86.1 2.6 %copy-start.6 = (bf16[2,1024,256]{2,1,0:T(8,128)(2,1)S(1)}, bf16[2,1024,256]{2,1,0:T(8,128)(2,1)}, u32[]{:S(2)}) copy-start(bf16[2,1024,256]{2,1,0:T(8,128)(2,1)} %get-tuple-element.788) | copy-start | bytes 3145732 | tf_op jit(solution)/shard_map/while/body/eval_jaxpr/cond
  97.1 2.9 %copy-start.1 = (bf16[2,1024,256]{1,2,0:T(8,128)(2,1)S(1)}, bf16[2,1024,256]{1,2,0:T(8,128)(2,1)}, u32[]{:S(2)}) copy-start(bf16[2,1024,256]{1,2,0:T(8,128)(2,1)} %get-tuple-element.813) | copy-start | bytes 3145732 | tf_op jit(solution)/shard_map/while/body/eval_jaxpr/cond
  97.1 2.9 %copy-start.3 = (pred[1024,512]{0,1:T(8,128)(4,1)S(1)}, pred[1024,512]{0,1:T(8,128)(4,1)}, u32[]{:S(2)}) copy-start(pred[1024,512]{0,1:T(8,128)(4,1)} %get-tuple-element.805) | copy-start | bytes 1572868 | tf_op jit(solution)/shard_map/while/body/eval_jaxpr/cond
  110.6 2.9 %copy-start.1 = (bf16[2,1024,256]{1,2,0:T(8,128)(2,1)S(1)}, bf16[2,1024,256]{1,2,0:T(8,128)(2,1)}, u32[]{:S(2)}) copy-start(bf16[2,1024,256]{1,2,0:T(8,128)(2,1)} %get-tuple-element.813) | copy-start | bytes 3145732 | tf_op jit(solution)/shard_map/while/body/eval_jaxpr/cond
  110.6 2.9 %copy-start.3 = (pred[1024,512]{0,1:T(8,128)(4,1)S(1)}, pred[1024,512]{0,1:T(8,128)(4,1)}, u32[]{:S(2)}) copy-start(pred[1024,512]{0,1:T(8,128)(4,1)} %get-tuple-element.805) | copy-start | bytes 1572868 | tf_op jit(solution)/shard_map/while/body/eval_jaxpr/cond
  124.0 2.9 %copy-start.1 = (bf16[2,1024,256]{1,2,0:T(8,128)(2,1)S(1)}, bf16[2,1024,256]{1,2,0:T(8,128)(2,1)}, u32[]{:S(2)}) copy-start(bf16[2,1024,256]{1,2,0:T(8,128)(2,1)} %get-tuple-element.813) | copy-start | bytes 3145732 | tf_op jit(solution)/shard_map/while/body/eval_jaxpr/cond
  124.0 2.9 %copy-start.3 = (pred[1024,512]{0,1:T(8,128)(4,1)S(1)}, pred[1024,512]{0,1:T(8,128)(4,1)}, u32[]{:S(2)}) copy-start(pred[1024,512]{0,1:T(8,128)(4,1)} %get-tuple-element.805) | copy-start | bytes 1572868 | tf_op jit(solution)/shard_map/while/body/eval_jaxpr/cond
  137.5 2.9 %copy-start.1 = (bf16[2,1024,256]{1,2,0:T(8,128)(2,1)S(1)}, bf16[2,1024,256]{1,2,0:T(8,128)(2,1)}, u32[]{:S(2)}) copy-start(bf16[2,1024,256]{1,2,0:T(8,128)(2,1)} %get-tuple-element.813) | copy-start | bytes 3145732 | tf_op jit(solution)/shard_map/while/body/eval_jaxpr/cond
  137.5 2.9 %copy-start.3 = (pred[1024,512]{0,1:T(8,128)(4,1)S(1)}, pred[1024,512]{0,1:T(8,128)(4,1)}, u32[]{:S(2)}) copy-start(pred[1024,512]{0,1:T(8,128)(4,1)} %get-tuple-element.805) | copy-start | bytes 1572868 | tf_op jit(solution)/shard_map/while/body/eval_jaxpr/cond
  146.9 5.2 %copy-start.7 = (f32[2,128,128]{2,1,0:T(8,128)}, f32[2,128,128]{2,1,0:T(8,128)S(1)}, u32[]{:S(2)}) copy-start(f32[2,128,128]{2,1,0:T(8,128)S(1)} %get-tuple-element.842) | copy-start | bytes 393220
  146.9 4.1 %copy-start.5 = (bf16[256,2,4,128]{3,2,1,0:T(4,128)(2,1)S(1)}, bf16[256,2,4,128]{3,2,1,0:T(4,128)(2,1)}, u32[]{:S(2)}) copy-start(bf16[256,2,4,128]{3,2,1,0:T(4,128)(2,1)} %copy-done.4) | copy-start | bytes 1572868
Sparse Core Ops, SparseCore 0:
  28.0 24.7 all-gather.1
  153.3 55.2 all-reduce.2
where the time goes:
time: 220 us; the launch traced here: 219 us
  waiting for transfers between devices  73.7 us (34%)
  matrix products  56.1 us (26%)
  other arithmetic  40.3 us (18%)
  local copies, waits for them, and re-layouts  18.5 us (8%)
  between operations  14.3 us (6%)
  starting transfers between devices  9.9 us (4%)
  loops' own time  6.15 us (3%)
    psum x1, waiting for transfers between devices, per_device(): lax.psum((query_weight_grad, key_weight_grad), 'seq')  55.4 us
    dot_general x8, matrix products, teacher(): jnp.einsum('vrd,vwd->vrw', query_flat, key_slab, preferred_element_type=j...  14.5 us
    dot_general x8, matrix products, key_features(): jnp.einsum('vwd,vde->vwe', key_slab.astype(jnp.float32), key_map, precisi...  11 us
    all_to_all x1, waiting for transfers between devices, per_device(): lax.all_to_all(queries, 'head', split_axis=1, concat_axis=0, tiled=True)  10.6 us
    dot_general x4, matrix products, grads_compute_live(): jnp.einsum('vrf,vwf->vrw', phi_query_b, phi_key_b, preferred_element_type...  9.96 us
    unnamed x19, local copies, waits for them, and re-layouts  9.04 us
    reduce_or x4, other arithmetic, grads_step(): jnp.any(visible)  7.75 us
    all_to_all x1, starting transfers between devices, per_device(): lax.all_to_all(keys, 'head', split_axis=1, concat_axis=0, tiled=True)  6.35 us
  transfers between devices with their start and end apart: 4, of which 4 were waited for; matrix products, arithmetic and copies ran while one was open for 7% of the time, Pallas kernels for 0%

commit v1 on v0

--- a/solution.py
+++ b/solution.py
@@ -1,13 +1,15 @@
+import functools
 import math
 
 import jax
 import jax.numpy as jnp
 from jax import lax
+from jax.experimental import pallas as pl
+from jax.experimental.pallas import tpu as pltpu
 from jax.sharding import PartitionSpec as P
 
 HEAD_SIZE = 128
 BLK = 128
-
 
 HIGHEST = lax.Precision.HIGHEST
 NEG_FLOOR = -1e30
@@ -51,7 +53,7 @@
     return lax.fori_loop(0, row_count // step_rows, advance, running)
 
 
-def per_device(queries, keys, block_pos, query_map, key_map):
+def per_device_general(queries, keys, block_pos, query_map, key_map):
     local_q, local_k = (
         lax.all_to_all(queries, "head", split_axis=1, concat_axis=0, tiled=True),
         lax.all_to_all(keys, "head", split_axis=1, concat_axis=0, tiled=True),
@@ -175,6 +177,237 @@
     return (query_map_gradient, key_map_gradient)
 
 
+NT = (((1,), (1,)), ((), ()))
+F32 = jnp.float32
+BF16 = jnp.bfloat16
+
+
+def nn(left, right):
+    return jnp.dot(left, right, preferred_element_type=F32)
+
+
+def nt(left, right):
+    return lax.dot_general(left, right, NT, preferred_element_type=F32)
+
+
+def bf16_parts(value, count):
+    parts = []
+    for _ in range(count):
+        part = value.astype(BF16)
+        parts.append(part)
+        value = value - part.astype(F32)
+    return jnp.concatenate(parts, axis=0)
+
+
+def fold_parts(value, count):
+    rows = value.shape[0] // count
+    total = value[(count - 1) * rows :]
+    for number in range(count - 2, -1, -1):
+        total = total + value[number * rows : (number + 1) * rows]
+    return total
+
+
+def features_t(logits):
+    up = jnp.exp(logits - jnp.max(logits, axis=0, keepdims=True))
+    down = jnp.exp(jnp.min(logits, axis=0, keepdims=True) - logits)
+    up = up * (1.0 / jnp.sum(up, axis=0, keepdims=True))
+    down = down * (1.0 / jnp.sum(down, axis=0, keepdims=True))
+    return jnp.concatenate([up, down], axis=0)
+
+
+def feature_grad_t(feature, upstream):
+    halves = []
+    for half in (slice(0, HEAD_SIZE), slice(HEAD_SIZE, 2 * HEAD_SIZE)):
+        value, grad = feature[half], upstream[half]
+        halves.append(value * (grad - jnp.sum(grad * value, axis=0, keepdims=True)))
+    return halves[0] - halves[1]
+
+
+def head_kernel(
+    token_count,
+    seq_blocks,
+    pos_ref,
+    which_ref,
+    rows_ref,
+    query_map_ref,
+    key_map_ref,
+    out_ref,
+    stored,
+    query_rows,
+    key_rows,
+    phi_q,
+    phi_k,
+    phi_qb,
+    phi_kb,
+    phi_kb_rows,
+    pair_weights,
+    acc_q,
+    acc_k,
+):
+    del which_ref
+    chunk = rows_ref.shape[1] // 2
+    per_block = BLK // chunk
+    seq_tokens = seq_blocks * BLK
+    sequences = token_count // seq_tokens
+    for number in range(token_count // BLK):
+        stored[pos_ref[number]] = number
+    acc_q[...] = jnp.zeros_like(acc_q)
+    acc_k[...] = jnp.zeros_like(acc_k)
+    query_map_t = bf16_parts(query_map_ref[0].T, 3)
+    key_map_t = bf16_parts(key_map_ref[0].T, 3)
+    lane = lax.broadcasted_iota(jnp.int32, (BLK, BLK), 1)
+    sublane = lax.broadcasted_iota(jnp.int32, (BLK, BLK), 0)
+    unit = jnp.where(lane == sublane, 1.0, 0.0).astype(BF16)
+    visible = sublane <= lane
+    exponent_scale = HEAD_SIZE ** (-0.5) * math.log2(math.e)
+
+    def block_rows(place, half):
+        first = place * per_block
+        return rows_ref[pl.ds(first, per_block), half * chunk : (half + 1) * chunk, :].reshape(
+            BLK, HEAD_SIZE
+        )
+
+    def one_sequence(seq, carry):
+        for at in range(seq_blocks):
+            here = slice(at * BLK, (at + 1) * BLK)
+            place = stored[seq * seq_blocks + at]
+            key_block = block_rows(place, 1)
+            key_rows[here, :] = key_block
+            feature = features_t(fold_parts(nt(key_map_t, key_block), 3))
+            phi_k[:, here] = feature
+            rounded = feature.astype(BF16)
+            phi_kb[:, here] = rounded
+            phi_kb_rows[here, :] = nt(unit, rounded).astype(BF16)
+            query_block = block_rows(place, 0)
+            query_rows[here, :] = query_block
+            feature = features_t(fold_parts(nt(query_map_t, query_block), 3))
+            phi_q[:, here] = feature
+            phi_qb[:, here] = feature.astype(BF16)
+        for at in range(seq_blocks):
+            here = slice(at * BLK, (at + 1) * BLK)
+            live = (at + 1) * BLK
+            query_block = query_rows[here, :]
+            teacher = nt(key_rows[:live, :], query_block)
+            student = nn(phi_kb_rows[:live, :], phi_qb[:, here])
+            last = slice(at * BLK, live)
+            teacher_last = jnp.where(visible, teacher[last], NEG_FLOOR)
+            student_last = jnp.where(visible, student[last], 0.0)
+            highest = jnp.max(teacher_last, axis=0, keepdims=True)
+            linear_sum = jnp.sum(student_last, axis=0, keepdims=True)
+            if at:
+                highest = jnp.maximum(
+                    highest, jnp.max(teacher[: at * BLK], axis=0, keepdims=True)
+                )
+                linear_sum = linear_sum + jnp.sum(student[: at * BLK], axis=0, keepdims=True)
+            exponent_last = jnp.exp2((teacher_last - highest) * exponent_scale)
+            denominator = jnp.sum(exponent_last, axis=0, keepdims=True)
+            if at:
+                exponent = jnp.exp2((teacher[: at * BLK] - highest) * exponent_scale)
+                denominator = denominator + jnp.sum(exponent, axis=0, keepdims=True)
+            base = 1.0 / (linear_sum * token_count)
+            share = 1.0 / (denominator * token_count)
+            weights = jnp.where(
+                visible, base - (exponent_last * share) / student[last], 0.0
+            ).astype(BF16)
+            if at:
+                weights = jnp.concatenate(
+                    [
+                        (base - (exponent * share) / student[: at * BLK]).astype(BF16),
+                        weights,
+                    ],
+                    axis=0,
+                )
+            pair_weights[:live, here] = weights
+            query_grad = nn(phi_kb[:, :live], weights)
+            logit_grad = feature_grad_t(phi_q[:, here], query_grad)
+            acc_q[...] += nn(bf16_parts(logit_grad, 2), query_block)
+        for at in range(seq_blocks):
+            here = slice(at * BLK, (at + 1) * BLK)
+            later = slice(at * BLK, seq_tokens)
+            key_grad = nt(phi_qb[:, later], pair_weights[here, later])
+            logit_grad = feature_grad_t(phi_k[:, here], key_grad)
+            acc_k[...] += nn(bf16_parts(logit_grad, 2), key_rows[here, :])
+        return carry
+
+    lax.fori_loop(0, sequences, one_sequence, 0)
+    out_ref[:HEAD_SIZE, :] = fold_parts(acc_q[...], 2).T.astype(BF16)
+    out_ref[HEAD_SIZE:, :] = bf16_parts(fold_parts(acc_k[...], 2).T, 2)
+
+
+def send_kernel(seq_count, head_count, key_heads, queries_ref, keys_ref, out_ref):
+    rows = queries_ref.shape[0]
+    share = seq_count // key_heads
+    for head in range(head_count):
+        for seq in range(seq_count):
+            target = seq * head_count + head
+            column = (head * seq_count + seq) * HEAD_SIZE
+            out_ref[target, :rows, :] = queries_ref[:, column : column + HEAD_SIZE]
+            column = (head * key_heads + seq // share) * HEAD_SIZE
+            out_ref[target, rows:, :] = keys_ref[:, column : column + HEAD_SIZE]
+
+
+def per_device_head(queries, keys, block_pos, query_map, key_map):
+    seq_count = lax.axis_size("seq")
+    head_count = lax.axis_size("head")
+    key_heads = key_map.shape[0]
+    rows = queries.shape[0]
+    devices = seq_count * head_count
+    token_count = rows * devices
+    sent = pl.pallas_call(
+        functools.partial(send_kernel, seq_count, head_count, key_heads),
+        out_shape=jax.ShapeDtypeStruct((devices, 2 * rows, HEAD_SIZE), BF16),
+    )(queries, keys)
+    arrived = lax.all_to_all(sent, ("seq", "head"), split_axis=0, concat_axis=0, tiled=True)
+    mine = lax.axis_index("seq").astype(jnp.int32)
+    which = jnp.stack([mine, mine // (seq_count // key_heads)])
+    seq_tokens = seq_count * BLK
+    whole = lambda *_: (0, 0, 0)
+    grads = pl.pallas_call(
+        functools.partial(head_kernel, token_count, seq_count),
+        out_shape=jax.ShapeDtypeStruct((3 * HEAD_SIZE, HEAD_SIZE), BF16),
+        grid_spec=pltpu.PrefetchScalarGridSpec(
+            num_scalar_prefetch=2,
+            grid=(1,),
+            in_specs=[
+                pl.BlockSpec(arrived.shape, whole),
+                pl.BlockSpec((1, HEAD_SIZE, HEAD_SIZE), lambda _, pos, which: (which[0], 0, 0)),
+                pl.BlockSpec((1, HEAD_SIZE, HEAD_SIZE), lambda _, pos, which: (which[1], 0, 0)),
+            ],
+            out_specs=pl.BlockSpec((3 * HEAD_SIZE, HEAD_SIZE), lambda *_: (0, 0)),
+            scratch_shapes=[
+                pltpu.SMEM((token_count // BLK,), jnp.int32),
+                pltpu.VMEM((seq_tokens, HEAD_SIZE), BF16),
+                pltpu.VMEM((seq_tokens, HEAD_SIZE), BF16),
+                pltpu.VMEM((2 * HEAD_SIZE, seq_tokens), F32),
+                pltpu.VMEM((2 * HEAD_SIZE, seq_tokens), F32),
+                pltpu.VMEM((2 * HEAD_SIZE, seq_tokens), BF16),
+                pltpu.VMEM((2 * HEAD_SIZE, seq_tokens), BF16),
+                pltpu.VMEM((seq_tokens, 2 * HEAD_SIZE), BF16),
+                pltpu.VMEM((seq_tokens, seq_tokens), BF16),
+                pltpu.VMEM((2 * HEAD_SIZE, HEAD_SIZE), F32),
+                pltpu.VMEM((2 * HEAD_SIZE, HEAD_SIZE), F32),
+            ],
+        ),
+    )(block_pos, which, arrived, query_map, key_map)
+    everyone = lax.all_gather(grads, "seq", axis=0, tiled=False)
+    everyone = everyone.reshape(seq_count, 3, HEAD_SIZE, HEAD_SIZE).astype(F32)
+    key_parts = (everyone[:, 1] + everyone[:, 2]).reshape(
+        key_heads, seq_count // key_heads, HEAD_SIZE, HEAD_SIZE
+    )
+    return everyone[:, 0], jnp.sum(key_parts, axis=1)
+
+
+def per_device(queries, keys, block_pos, query_map, key_map):
+    seq_count = lax.axis_size("seq")
+    one_head_each = (
+        query_map.shape[0] == seq_count
+        and seq_count % key_map.shape[0] == 0
+        and BLK % queries.shape[0] == 0
+    )
+    chosen = per_device_head if one_head_each else per_device_general
+    return chosen(queries, keys, block_pos, query_map, key_map)
+
+
 def solution(mesh):
     in_specs = (
         P(("seq", "head"), None),

time: 220 us -> 69.9 us (0.32)
  matrix products: 56.1 us -> 0 us
  waiting for transfers between devices: 73.7 us -> 24.3 us
  other arithmetic: 40.3 us -> 2.34 us
  Pallas kernels: 0 us -> 22.6 us
  local copies, waits for them, and re-layouts: 18.5 us -> 0.98 us
  between operations: 14.3 us -> 0.66 us
  blocking collectives: 0 us -> 11.4 us
  loops' own time: 6.15 us -> 0 us
  starting transfers between devices: 9.9 us -> 7.33 us
    dot_general x38 -> x0, matrix products: 56.1 us -> none  [the longest x8 14.5 us: teacher(): jnp.einsum('vrd,vwd->vrw', query_flat, key_slab, preferred_element_type=j...]
    psum x1 -> x0, waiting for transfers between devices: 55.4 us -> none  [per_device(): lax.psum((query_weight_grad, key_weight_grad), 'seq')]
    pallas_call x0 -> x2, Pallas kernels: none -> 22.6 us  [the longest x1 20.4 us: per_device_head(): pl.pallas_call(functools.partial(head_kernel, token_count, seq_count), ou...]
    reduce_or x8 -> x0, other arithmetic: 12.8 us -> none  [the longest x4 7.75 us: grads_step(): jnp.any(visible)]
    sub x18 -> x0, other arithmetic: 12.2 us -> none  [the longest x8 4.07 us: softmax_pair(): jax.nn.softmax(-logits, axis=-1)]
    all_gather x0 -> x1, blocking collectives: none -> 11.4 us  [per_device_head(): everyone = lax.all_gather(grads, 'seq', axis=0, tiled=False)]
    all_to_all x2 -> x1, waiting for transfers between devices: 14.8 us -> 24.3 us  [per_device_head(): lax.all_to_all(sent, ('seq', 'head'), split_axis=0, concat_axis=0, tiled=...]
    unnamed x19 -> x2, local copies, waits for them, and re-layouts: 9.04 us -> 0.98 us
  transfers between devices with their start and end apart: 4 -> 1, of which waited for: 4 -> 1; matrix products, arithmetic and copies ran while one was open for 7% -> 1% of each run, Pallas kernels for 0% -> 0%
where the time goes in v1:
time: 69.9 us; the launch traced here: 69.6 us
  waiting for transfers between devices  24.3 us (35%)
  Pallas kernels  22.6 us (32%)
  blocking collectives  11.4 us (16%)
  starting transfers between devices  7.33 us (10%)
  other arithmetic  2.34 us (3%)
  local copies, waits for them, and re-layouts  0.98 us (1%)
    all_to_all x1, waiting for transfers between devices, per_device_head(): lax.all_to_all(sent, ('seq', 'head'), split_axis=0, concat_axis=0, tiled=...  24.3 us
    pallas_call x1, Pallas kernels, per_device_head(): pl.pallas_call(functools.partial(head_kernel, token_count, seq_count), ou...  20.4 us
    all_gather x1, blocking collectives, per_device_head(): everyone = lax.all_gather(grads, 'seq', axis=0, tiled=False)  11.4 us
    all_to_all x1, starting transfers between devices, per_device_head(): lax.all_to_all(sent, ('seq', 'head'), split_axis=0, concat_axis=0, tiled=...  7.33 us
    pallas_call x1, Pallas kernels, per_device_head(): pl.pallas_call(functools.partial(send_kernel, seq_count, head_count, key_...  2.19 us
  transfers between devices with their start and end apart: 1, of which 1 were waited for; matrix products, arithmetic and copies ran while one was open for 1% of the time, Pallas kernels for 0%

profile of v1, /device:TPU:0, one launch (start us, length us, event | category | flops | bytes accessed | tf_op | source)
XLA Modules:
  0.0 69.6 jit_solution(1790535205113437999)
XLA Ops:
  0.6 2.2 %shard_map.68 = bf16[32,128,128]{2,1,0:T(8,128)(2,1)} custom-call(bf16[64,4096]{1,0:T(8,128)(2,1)} %queries_ref.1, bf16[64,1024]{1,0:T(8,128)(2,1)} %keys_ref.1), custom_call_target="tpu_custom_call" | custom-call | tf_op jit(solution)/shard_map/pallas_call | solution.py:356
  2.8 7.3 %all-to-all-start = ((bf16[32,128,128]{2,1,0:T(8,128)(2,1)}), bf16[32,128,128]{2,1,0:T(8,128)(2,1)S(1)}, u32[]{:S(2)}, u32[]{:S(2)}) async-start(bf16[32,128,128]{2,1,0:T(8,128)(2,1)} %shard_map.68), calls=%async_computation | async-start | bytes 2097152 | tf_op jit(solution)/shard_map/all_to_all | solution.py:360
  10.2 0.6 pad_add_fusion.which_ref
  10.8 24.3 %all-to-all-done.rows_ref = bf16[32,128,128]{2,1,0:T(8,128)(2,1)S(1)} async-done(((bf16[32,128,128]{2,1,0:T(8,128)(2,1)}), bf16[32,128,128]{2,1,0:T(8,128)(2,1)S(1)}, u32[]{:S(2)}, u32[]{:S(2)}) %all-to-all-start) | async-done | bytes 1048608 | tf_op jit(solution)/shard_map/all_to_all | solution.py:360
  35.1 0.0 copy-start
  35.1 1.0 %copy-done = bf16[32,128,128]{2,1,0:T(8,128)(2,1)} copy-done((bf16[32,128,128]{2,1,0:T(8,128)(2,1)}, bf16[32,128,128]{2,1,0:T(8,128)(2,1)S(1)}, u32[]{:S(2)}) %copy-start) | copy-done | bytes 1048600
  36.1 20.4 %shard_map.69 = bf16[384,128]{1,0:T(8,128)(2,1)} custom-call(s32[16]{0:T(128)} %pos_ref.1, s32[2]{0:T(128)} %pad_add_fusion.which_ref, bf16[32,128,128]{2,1,0:T(8,128)(2,1)} %copy-done, f32[8,128,128]{2,1,0:T(8,128)} %query_map_ref.1, f32[2,128,128]{2,1,0:T(8,128)} %key_map_ref.1), custom_call_target="tpu_custom_call" | custom-call | tf_op jit(solution)/shard_map/pallas_call | solution.py:365
  56.4 11.4 %all-gather = bf16[3072,128]{1,0:T(8,128)(2,1)S(1)} all-gather(bf16[384,128]{1,0:T(8,128)(2,1)} %shard_map.69), channel_id=2, replica_groups=mesh['seq'=8,'head'=4] {'seq'}, dimensions={0}, use_global_device_ids=true | all-gather | bytes 884736 | tf_op jit(solution)/shard_map/all_gather | solution.py:392
  67.8 0.2 convert.1
  68.0 0.9 %slice_add_fusion = (f32[8,1,128,128]{3,2,1,0:T(8,128)S(1)}, f32[8,128,128]{2,1,0:T(8,128)}) fusion(f32[8,3,128,128]{3,2,1,0:T(8,128)S(1)} %convert.1), kind=kLoop, calls=%fused_computation | loop fusion | flops 131072 | bytes 2621440 | tf_op jit(solution)/shard_map/add | solution.py:394
  68.9 0.7 bitcast_reduce_fusion
Async XLA Ops:
  2.8 32.3 %all-to-all-start = ((bf16[32,128,128]{2,1,0:T(8,128)(2,1)}), bf16[32,128,128]{2,1,0:T(8,128)(2,1)S(1)}, u32[]{:S(2)}, u32[]{:S(2)}) async-start(bf16[32,128,128]{2,1,0:T(8,128)(2,1)} %shard_map.68), calls=%async_computation | async-start | bytes 2097152 | tf_op jit(solution)/shard_map/all_to_all | solution.py:360
  35.1 1.0 %copy-start = (bf16[32,128,128]{2,1,0:T(8,128)(2,1)}, bf16[32,128,128]{2,1,0:T(8,128)(2,1)S(1)}, u32[]{:S(2)}) copy-start(bf16[32,128,128]{2,1,0:T(8,128)(2,1)S(1)} %all-to-all-done.rows_ref) | copy-start | bytes 3145732

commit v2 on v0

--- a/solution.py
+++ b/solution.py
@@ -1,13 +1,15 @@
+import functools
 import math
 
 import jax
 import jax.numpy as jnp
 from jax import lax
+from jax.experimental import pallas as pl
+from jax.experimental.pallas import tpu as pltpu
 from jax.sharding import PartitionSpec as P
 
 HEAD_SIZE = 128
 BLK = 128
-
 
 HIGHEST = lax.Precision.HIGHEST
 NEG_FLOOR = -1e30
@@ -51,7 +53,7 @@
     return lax.fori_loop(0, row_count // step_rows, advance, running)
 
 
-def per_device(queries, keys, block_pos, query_map, key_map):
+def per_device_general(queries, keys, block_pos, query_map, key_map):
     local_q, local_k = (
         lax.all_to_all(queries, "head", split_axis=1, concat_axis=0, tiled=True),
         lax.all_to_all(keys, "head", split_axis=1, concat_axis=0, tiled=True),
@@ -175,6 +177,363 @@
     return (query_map_gradient, key_map_gradient)
 
 
+NT = (((1,), (1,)), ((), ()))
+F32 = jnp.float32
+BF16 = jnp.bfloat16
+
+
+def nn(left, right):
+    return jnp.dot(left, right, preferred_element_type=F32)
+
+
+def nt(left, right):
+    return lax.dot_general(left, right, NT, preferred_element_type=F32)
+
+
+def bf16_parts(value, count):
+    parts = []
+    for _ in range(count):
+        part = value.astype(BF16)
+        parts.append(part)
+        value = value - part.astype(F32)
+    return jnp.concatenate(parts, axis=0)
+
+
+def features_t(logits):
+    up = jnp.exp(logits - jnp.max(logits, axis=0, keepdims=True))
+    down = jnp.exp(jnp.min(logits, axis=0, keepdims=True) - logits)
+    up = up * (1.0 / jnp.sum(up, axis=0, keepdims=True))
+    down = down * (1.0 / jnp.sum(down, axis=0, keepdims=True))
+    return jnp.concatenate([up, down], axis=0)
+
+
+def feature_grad_t(feature, upstream):
+    halves = []
+    for half in (slice(0, HEAD_SIZE), slice(HEAD_SIZE, 2 * HEAD_SIZE)):
+        value, grad = feature[half], upstream[half]
+        halves.append(value * (grad - jnp.sum(grad * value, axis=0, keepdims=True)))
+    return halves[0] - halves[1]
+
+
+def tile_sum(value):
+    return jnp.sum(value.reshape(-1, 8, value.shape[-1]), axis=0)
+
+
+def tile_max(value):
+    return jnp.max(value.reshape(-1, 8, value.shape[-1]), axis=0)
+
+
+def side_parts(value):
+    high = value.astype(BF16)
+    return jnp.concatenate([high, (value - high.astype(F32)).astype(BF16)], axis=1)
+
+
+def map_parts(weights):
+    rest = weights.T
+    parts = []
+    for _ in range(3):
+        parts.append(rest.astype(BF16))
+        rest = rest - parts[-1].astype(F32)
+    return jnp.concatenate(parts[::-1], axis=1)
+
+
+def logits_t(parts, tokens):
+    return nt(parts, jnp.concatenate([tokens] * 3, axis=1))
+
+
+def send_kernel(seq_count, head_count, key_heads, queries_ref, keys_ref, out_ref):
+    rows = queries_ref.shape[0]
+    share = seq_count // key_heads
+    part = rows // share
+    for head in range(head_count):
+        for seq in range(seq_count):
+            target = seq * head_count + head
+            column = (head * seq_count + seq) * HEAD_SIZE
+            out_ref[target, :rows, :] = queries_ref[:, column : column + HEAD_SIZE]
+            column = (head * key_heads + seq // share) * HEAD_SIZE
+            first = seq % share * part
+            out_ref[target, rows:, :] = keys_ref[
+                first : first + part, column : column + HEAD_SIZE
+            ]
+
+
+def query_kernel(rows, mine_ref, arrived_ref, query_map_ref, phi_ref, phi_b_ref):
+    per_block = BLK // rows
+    parts = map_parts(query_map_ref[mine_ref[0]])
+
+    def block_logits(number):
+        tokens = arrived_ref[number * per_block : (number + 1) * per_block, :rows, :]
+        return logits_t(parts, tokens.reshape(BLK, HEAD_SIZE))
+
+    blocks = phi_ref.shape[0]
+    ahead = block_logits(0)
+    for number in range(blocks):
+        logits = ahead
+        if number + 1 < blocks:
+            ahead = block_logits(number + 1)
+        feature = features_t(logits)
+        phi_ref[number] = feature
+        phi_b_ref[number] = feature.astype(BF16)
+
+
+def pair_kernel(
+    token_count,
+    seq_blocks,
+    rows,
+    share,
+    pos_ref,
+    mine_ref,
+    arrived_ref,
+    *refs,
+):
+    key_refs, refs = refs[: share - 1], refs[share - 1 :]
+    (
+        key_map_ref,
+        phi_q,
+        phi_qb,
+        out_ref,
+        stored,
+        key_rows,
+        phi_k,
+        phi_kb,
+        phi_kb_rows,
+        pair_weights,
+        scores,
+        linears,
+        acc_q,
+        acc_k,
+    ) = refs
+    per_block = BLK // rows
+    part = rows // share
+    sequences = token_count // (seq_blocks * BLK)
+    for number in range(token_count // BLK):
+        stored[pos_ref[number]] = number
+    acc_q[...] = jnp.zeros_like(acc_q)
+    acc_k[...] = jnp.zeros_like(acc_k)
+    mine = mine_ref[0] % share
+    parts = map_parts(key_map_ref[mine_ref[0] // share])
+    lane = lax.broadcasted_iota(jnp.int32, (BLK, BLK), 1)
+    sublane = lax.broadcasted_iota(jnp.int32, (BLK, BLK), 0)
+    unit = jnp.where(lane == sublane, 1.0, 0.0).astype(BF16)
+    visible = sublane <= lane
+    exponent_scale = HEAD_SIZE ** (-0.5) * math.log2(math.e)
+
+    def block(at):
+        return slice(at * BLK, (at + 1) * BLK)
+
+    def place(seq, at):
+        return stored[seq * seq_blocks + at]
+
+    def query_block(seq, at):
+        first = place(seq, at) * per_block
+        return arrived_ref[pl.ds(first, per_block), :rows, :].reshape(BLK, HEAD_SIZE)
+
+    def key_logits(seq, at):
+        first = place(seq, at) * per_block
+        for chunk in range(per_block):
+            for other in range(share):
+                start = pl.multiple_of(
+                    at * BLK + chunk * rows + (mine ^ other) * part, part
+                )
+                if other:
+                    piece = key_refs[other - 1][first + chunk]
+                else:
+                    piece = arrived_ref[first + chunk, rows:, :]
+                key_rows[seq, pl.ds(start, part), :] = piece
+        return logits_t(parts, key_rows[seq, block(at), :])
+
+    def key_features(seq, at, logits):
+        feature = features_t(logits)
+        phi_k[seq, :, block(at)] = feature
+        rounded = feature.astype(BF16)
+        phi_kb[seq, :, block(at)] = rounded
+        phi_kb_rows[seq, block(at), :] = nt(unit, rounded).astype(BF16)
+
+    def pair_scores(seq, at):
+        live = (at + 1) * BLK
+        slot = at % 2
+        teacher = nt(key_rows[seq, :live, :], query_block(seq, at))
+        student = nn(phi_kb_rows[seq, :live, :], phi_qb[place(seq, at)])
+        highest = linear_sum = None
+        for number in range(at + 1):
+            here = block(number)
+            score, linear = teacher[here], student[here]
+            linears[seq, slot, here, :] = linear
+            if number == at:
+                score = jnp.where(visible, score, NEG_FLOOR)
+                linear = jnp.where(visible, linear, 0.0)
+            scores[seq, slot, here, :] = score
+            top, total = tile_max(score), tile_sum(linear)
+            highest = top if number == 0 else jnp.maximum(highest, top)
+            linear_sum = total if number == 0 else linear_sum + total
+        return (
+            jnp.max(highest, axis=0, keepdims=True),
+            jnp.sum(linear_sum, axis=0, keepdims=True),
+        )
+
+    def pair_gradients(seq, at, stats):
+        highest, linear_sum = stats
+        slot = at % 2
+        denominator = None
+        for number in range(at + 1):
+            here = block(number)
+            exponent = jnp.exp2((scores[seq, slot, here, :] - highest) * exponent_scale)
+            scores[seq, slot, here, :] = exponent
+            total = tile_sum(exponent)
+            denominator = total if number == 0 else denominator + total
+        denominator = jnp.sum(denominator, axis=0, keepdims=True)
+        base = 1.0 / (linear_sum * token_count)
+        rate = 1.0 / (denominator * token_count)
+        for number in range(at + 1):
+            here = block(number)
+            weights = base - scores[seq, slot, here, :] * rate / linears[seq, slot, here, :]
+            if number == at:
+                weights = jnp.where(visible, weights, 0.0)
+            pair_weights[seq, here, block(at)] = weights.astype(BF16)
+
+    def query_grads(seq, at):
+        live = (at + 1) * BLK
+        upstream = nn(phi_kb[seq, :, :live], pair_weights[seq, :live, block(at)])
+        change = side_parts(feature_grad_t(phi_q[place(seq, at)], upstream))
+        tokens = query_block(seq, at)
+        acc_q[...] += nn(change, jnp.concatenate([tokens, tokens], axis=0))
+
+    def key_grads(seq, at):
+        later = slice(at * BLK, seq_blocks * BLK)
+        phi = jnp.concatenate(
+            [phi_qb[place(seq, number)] for number in range(at, seq_blocks)], axis=1
+        )
+        upstream = nt(phi, pair_weights[seq, block(at), later])
+        change = side_parts(feature_grad_t(phi_k[seq, :, block(at)], upstream))
+        tokens = key_rows[seq, block(at), :]
+        acc_k[...] += nn(change, jnp.concatenate([tokens, tokens], axis=0))
+
+    def feature_steps(seq):
+        ahead = key_logits(seq, 0)
+        for at in range(seq_blocks):
+            logits = ahead
+            if at + 1 < seq_blocks:
+                ahead = key_logits(seq, at + 1)
+            key_features(seq, at, logits)
+            yield
+
+    def pair_steps(seq):
+        ahead = pair_scores(seq, 0)
+        for at in range(seq_blocks):
+            stats = ahead
+            if at + 1 < seq_blocks:
+                ahead = pair_scores(seq, at + 1)
+            pair_gradients(seq, at, stats)
+            if at:
+                query_grads(seq, at - 1)
+            yield
+        query_grads(seq, seq_blocks - 1)
+
+    def key_steps(seq):
+        for at in range(seq_blocks):
+            key_grads(seq, at)
+            yield
+
+    stages = (feature_steps, pair_steps, key_steps)
+    for turn in range(sequences + len(stages) - 1):
+        active = [
+            stage(turn - number)
+            for number, stage in enumerate(stages)
+            if 0 <= turn - number < sequences
+        ]
+        while active:
+            for step in list(active):
+                if next(step, step) is step:
+                    active.remove(step)
+    out_ref[:HEAD_SIZE, :] = acc_q[...].T.astype(BF16)
+    out_ref[HEAD_SIZE:, :] = bf16_parts(acc_k[...].T, 2)
+
+
+def per_device_head(queries, keys, block_pos, query_map, key_map):
+    seq_count = lax.axis_size("seq")
+    head_count = lax.axis_size("head")
+    key_heads = key_map.shape[0]
+    share = seq_count // key_heads
+    rows = queries.shape[0]
+    part = rows // share
+    devices = seq_count * head_count
+    token_count = rows * devices
+    blocks = token_count // BLK
+    seq_tokens = seq_count * BLK
+    sequences = token_count // seq_tokens
+    vmem = pl.BlockSpec(memory_space=pltpu.VMEM)
+    smem = pl.BlockSpec(memory_space=pltpu.SMEM)
+    sent = pl.pallas_call(
+        functools.partial(send_kernel, seq_count, head_count, key_heads),
+        out_shape=jax.ShapeDtypeStruct((devices, rows + part, HEAD_SIZE), BF16),
+        compiler_params=pltpu.CompilerParams(vmem_limit_bytes=8 << 20),
+    )(queries, keys)
+    arrived = lax.all_to_all(sent, ("seq", "head"), split_axis=0, concat_axis=0, tiled=True)
+    mine = lax.axis_index("seq").astype(jnp.int32).reshape(1)
+
+    def swap(piece, bit):
+        return lax.ppermute(piece, "seq", [(i, i ^ bit) for i in range(seq_count)])
+
+    pieces = [arrived[:, rows:, :]]
+    for other in range(1, share):
+        bit = other & -other
+        pieces.append(swap(pieces[other - bit], bit))
+    phi, phi_b = pl.pallas_call(
+        functools.partial(query_kernel, rows),
+        out_shape=(
+            jax.ShapeDtypeStruct((blocks, 2 * HEAD_SIZE, BLK), F32),
+            jax.ShapeDtypeStruct((blocks, 2 * HEAD_SIZE, BLK), BF16),
+        ),
+        in_specs=[smem, vmem, vmem],
+        out_specs=(vmem, vmem),
+        compiler_params=pltpu.CompilerParams(vmem_limit_bytes=16 << 20),
+        cost_estimate=pl.CostEstimate(
+            flops=token_count * HEAD_SIZE * HEAD_SIZE * 6,
+            bytes_accessed=token_count * HEAD_SIZE * 20,
+            transcendentals=token_count * HEAD_SIZE * 2,
+        ),
+    )(mine, arrived, query_map)
+    grads = pl.pallas_call(
+        functools.partial(pair_kernel, token_count, seq_count, rows, share),
+        out_shape=jax.ShapeDtypeStruct((3 * HEAD_SIZE, HEAD_SIZE), BF16),
+        in_specs=[smem, smem] + [vmem] * (share + 3),
+        out_specs=vmem,
+        scratch_shapes=[
+            pltpu.SMEM((blocks,), jnp.int32),
+            pltpu.VMEM((sequences, seq_tokens, HEAD_SIZE), BF16),
+            pltpu.VMEM((sequences, 2 * HEAD_SIZE, seq_tokens), F32),
+            pltpu.VMEM((sequences, 2 * HEAD_SIZE, seq_tokens), BF16),
+            pltpu.VMEM((sequences, seq_tokens, 2 * HEAD_SIZE), BF16),
+            pltpu.VMEM((sequences, seq_tokens, seq_tokens), BF16),
+            pltpu.VMEM((sequences, 2, seq_tokens, BLK), F32),
+            pltpu.VMEM((sequences, 2, seq_tokens, BLK), F32),
+            pltpu.VMEM((HEAD_SIZE, HEAD_SIZE), F32),
+            pltpu.VMEM((HEAD_SIZE, HEAD_SIZE), F32),
+        ],
+        compiler_params=pltpu.CompilerParams(vmem_limit_bytes=32 << 20),
+    )(block_pos, mine, arrived, *pieces[1:], key_map, phi, phi_b)
+    everyone = lax.all_gather(grads, "seq", axis=0, tiled=False)
+    everyone = everyone.reshape(seq_count, 3, HEAD_SIZE, HEAD_SIZE).astype(F32)
+    key_sums = (everyone[:, 1] + everyone[:, 2]).reshape(
+        key_heads, share, HEAD_SIZE, HEAD_SIZE
+    )
+    return everyone[:, 0], jnp.sum(key_sums, axis=1)
+
+
+def per_device(queries, keys, block_pos, query_map, key_map):
+    seq_count = lax.axis_size("seq")
+    share = seq_count // key_map.shape[0]
+    one_head_each = (
+        query_map.shape[0] == seq_count
+        and seq_count == share * key_map.shape[0]
+        and share & (share - 1) == 0
+        and BLK % queries.shape[0] == 0
+        and queries.shape[0] % (16 * share) == 0
+    )
+    chosen = per_device_head if one_head_each else per_device_general
+    return chosen(queries, keys, block_pos, query_map, key_map)
+
+
 def solution(mesh):
     in_specs = (
         P(("seq", "head"), None),

time: 220 us -> 58.9 us (0.27)
  waiting for transfers between devices: 73.7 us -> 3.21 us
  matrix products: 56.1 us -> 0 us
  other arithmetic: 40.3 us -> 1.74 us
  blocking collectives: 0 us -> 34.3 us
  local copies, waits for them, and re-layouts: 18.5 us -> 1.96 us
  between operations: 14.3 us -> 0.7 us
  Pallas kernels: 0 us -> 13.6 us
  starting transfers between devices: 9.9 us -> 3.11 us
  loops' own time: 6.15 us -> 0 us
    dot_general x38 -> x0, matrix products: 56.1 us -> none  [the longest x8 14.5 us: teacher(): jnp.einsum('vrd,vwd->vrw', query_flat, key_slab, preferred_element_type=j...]
    psum x1 -> x0, waiting for transfers between devices: 55.4 us -> none  [per_device(): lax.psum((query_weight_grad, key_weight_grad), 'seq')]
    all_to_all x0 -> x1, blocking collectives: none -> 23.9 us  [per_device_head(): lax.all_to_all(sent, ('seq', 'head'), split_axis=0, concat_axis=0, tiled=...]
    all_to_all x2 -> x0, waiting for transfers between devices: 14.8 us -> none  [the longest x1 10.6 us: per_device(): lax.all_to_all(queries, 'head', split_axis=1, concat_axis=0, tiled=True)]
    pallas_call x0 -> x3, Pallas kernels: none -> 13.6 us  [the longest x1 12.6 us: per_device_head(): pl.pallas_call(functools.partial(pair_kernel, token_count, seq_count, row...]
    reduce_or x8 -> x0, other arithmetic: 12.8 us -> none  [the longest x4 7.75 us: grads_step(): jnp.any(visible)]
    sub x18 -> x0, other arithmetic: 12.2 us -> none  [the longest x8 4.07 us: softmax_pair(): jax.nn.softmax(-logits, axis=-1)]
    all_gather x0 -> x1, blocking collectives: none -> 10.4 us  [per_device_head(): everyone = lax.all_gather(grads, 'seq', axis=0, tiled=False)]
  transfers between devices with their start and end apart: 4 -> 3, of which waited for: 4 -> 2; matrix products, arithmetic and copies ran while one was open for 7% -> 0% of each run, Pallas kernels for 0% -> 2%
where the time goes in v2:
time: 58.9 us; the launch traced here: 58.7 us
  blocking collectives  34.3 us (58%)
  Pallas kernels  13.6 us (23%)
  waiting for transfers between devices  3.21 us (5%)
  starting transfers between devices  3.11 us (5%)
  local copies, waits for them, and re-layouts  1.96 us (3%)
  other arithmetic  1.74 us (3%)
  between operations  0.7 us (1%)
    all_to_all x1, blocking collectives, per_device_head(): lax.all_to_all(sent, ('seq', 'head'), split_axis=0, concat_axis=0, tiled=...  23.9 us
    pallas_call x1, Pallas kernels, per_device_head(): pl.pallas_call(functools.partial(pair_kernel, token_count, seq_count, row...  12.6 us
    all_gather x1, blocking collectives, per_device_head(): everyone = lax.all_gather(grads, 'seq', axis=0, tiled=False)  10.4 us
    ppermute x3, waiting for transfers between devices, swap(): return lax.ppermute(piece, 'seq', [(i, i ^ bit) for i in range(seq_count)])  3.21 us
    ppermute x3, starting transfers between devices, swap(): return lax.ppermute(piece, 'seq', [(i, i ^ bit) for i in range(seq_count)])  3.11 us
    unnamed x10, local copies, waits for them, and re-layouts  1.95 us
  transfers between devices with their start and end apart: 3, of which 2 were waited for; matrix products, arithmetic and copies ran while one was open for 0% of the time, Pallas kernels for 2%

profile of v2, /device:TPU:0, one launch (start us, length us, event | category | flops | bytes accessed | tf_op | source)
XLA Modules:
  0.0 58.7 jit_solution(16582195608252896863)
XLA Ops:
  0.6 0.0 copy-start
  0.6 1.0 %copy-done = bf16[64,4096]{1,0:T(8,128)(2,1)S(1)} copy-done((bf16[64,4096]{1,0:T(8,128)(2,1)S(1)}, bf16[64,4096]{1,0:T(8,128)(2,1)}, u32[]{:S(2)}) %copy-start) | copy-done | bytes 524312
  1.7 0.0 copy-start.2
  1.7 0.9 %copy-done.2 = bf16[64,1024]{1,0:T(8,128)(2,1)S(1)} copy-done((bf16[64,1024]{1,0:T(8,128)(2,1)S(1)}, bf16[64,1024]{1,0:T(8,128)(2,1)}, u32[]{:S(2)}) %copy-start.2) | copy-done | bytes 131096
  2.6 0.0 copy-start.1
  2.6 0.1 shard_map.68
  2.7 0.0 copy-start.3
  2.7 0.0 copy-start.4
  2.7 23.9 %all_to_all.5.arrived_ref = bf16[32,80,128]{2,1,0:T(8,128)(2,1)S(1)} all-to-all(bf16[32,80,128]{2,1,0:T(8,128)(2,1)S(1)} %shard_map.68), channel_id=1, replica_groups=mesh['seq'=8,'head'=4] {'seq','head'}, dimensions={0} | all-to-all | bytes 1310720 | tf_op jit(solution)/shard_map/all_to_all | solution.py:471
  26.7 1.6 %collective-permute-start.1 = (bf16[32,16,128]{2,1,0:T(8,128)(2,1)S(1)}, bf16[32,16,128]{2,1,0:T(8,128)(2,1)S(1)}, u32[]{:S(2)}, u32[]{:S(2)}) collective-permute-start(bf16[32,16,128]{2,1,0:T(8,128)(2,1)S(1)} %slice.16), channel_id=1, source_target_pairs={{0,8},{4,12},{8,0},{12,4},{16,24},{20,28},{24,16},{28,20},{1,9},{5... | collective-permute-start | bytes 393224 | tf_op jit(solution)/shard_map/ppermute | solution.py:475
  28.2 1.2 %collective-permute-start = (bf16[32,16,128]{2,1,0:T(8,128)(2,1)S(1)}, bf16[32,16,128]{2,1,0:T(8,128)(2,1)S(1)}, u32[]{:S(2)}, u32[]{:S(2)}) collective-permute-start(bf16[32,16,128]{2,1,0:T(8,128)(2,1)S(1)} %slice.16), channel_id=1, source_target_pairs={{0,4},{4,0},{8,12},{12,8},{16,20},{20,16},{24,28},{28,24},{1,5},{5... | collective-permute-start | bytes 393224 | tf_op jit(solution)/shard_map/ppermute | solution.py:475
  29.4 3.2 %collective-permute-done.1.refs_1_ = bf16[32,16,128]{2,1,0:T(8,128)(2,1)S(1)} collective-permute-done((bf16[32,16,128]{2,1,0:T(8,128)(2,1)S(1)}, bf16[32,16,128]{2,1,0:T(8,128)(2,1)S(1)}, u32[]{:S(2)}, u32[]{:S(2)}) %collective-permute-start.1) | collective-permute-done | bytes 131104 | tf_op jit(solution)/shard_map/ppermute | solution.py:475
  32.6 0.3 collective-permute-start.2
  32.9 0.0 copy-done.1
  32.9 0.9 %shard_map.69 = (f32[16,256,128]{2,1,0:T(8,128)S(1)}, bf16[16,256,128]{2,1,0:T(8,128)(2,1)S(1)}) custom-call(s32[1]{0:T(128)} %bitcast.mine_ref, bf16[32,80,128]{2,1,0:T(8,128)(2,1)S(1)} %all_to_all.5.arrived_ref, f32[8,128,128]{2,1,0:T(8,128)S(1)} %copy-done.1), custom_call_target="tpu_custom_call" | custom-call | flops 201326592 | bytes 5242880 | tf_op jit(solution)/shard_map/pallas_call | solution.py:481
  33.9 0.0 collective-permute-done.refs_0_
  33.9 0.1 collective-permute-done.2.refs_2_
  33.9 0.0 copy-done.3
  33.9 0.0 copy-done.4
  33.9 12.6 %shard_map.70 = bf16[384,128]{1,0:T(8,128)(2,1)S(1)} custom-call(s32[16]{0:T(128)S(1)} %copy-done.4, s32[1]{0:T(128)} %bitcast.mine_ref, bf16[32,80,128]{2,1,0:T(8,128)(2,1)S(1)} %all_to_all.5.arrived_ref, bf16[32,16,128]{2,1,0:T(8,128)(2,1)S(1)} %collective-permute-done.refs_0_, bf16[32,16,128]{2,1,0:T(8,128)(2,1)S(1)} %collective-permute-done.1.refs_1_, ...), custom_call_target="tpu_custom_call" | custom-call | tf_op jit(solution)/shard_map/pallas_call | solution.py:496
  46.5 10.4 %all-gather = bf16[3072,128]{1,0:T(8,128)(2,1)S(1)} all-gather(bf16[384,128]{1,0:T(8,128)(2,1)S(1)} %shard_map.70), channel_id=2, replica_groups=mesh['seq'=8,'head'=4] {'seq'}, dimensions={0}, use_global_device_ids=true | all-gather | bytes 884736 | tf_op jit(solution)/shard_map/all_gather | solution.py:515
  56.9 0.2 convert.1
  57.1 0.9 %slice_add_fusion = (f32[8,1,128,128]{3,2,1,0:T(8,128)S(1)}, f32[8,128,128]{2,1,0:T(8,128)}) fusion(f32[8,3,128,128]{3,2,1,0:T(8,128)S(1)} %convert.1), kind=kLoop, calls=%fused_computation | loop fusion | flops 131072 | bytes 2621440 | tf_op jit(solution)/shard_map/add | solution.py:517
  58.0 0.7 %bitcast_reduce_fusion = f32[2,128,128]{2,1,0:T(8,128)} fusion(f32[2,4,128,128]{3,2,1,0:T(8,128)S(1)} %bitcast.11), kind=kLoop, calls=%fused_computation.2 | loop fusion | flops 98304 | bytes 655360 | tf_op jit(solution)/shard_map/reduce_sum | solution.py:520
  (1 shorter events, 0.0 us)
Async XLA Ops:
  0.6 1.0 %copy-start = (bf16[64,4096]{1,0:T(8,128)(2,1)S(1)}, bf16[64,4096]{1,0:T(8,128)(2,1)}, u32[]{:S(2)}) copy-start(bf16[64,4096]{1,0:T(8,128)(2,1)} %queries_ref.1) | copy-start | bytes 1572868
  1.7 0.9 %copy-start.2 = (bf16[64,1024]{1,0:T(8,128)(2,1)S(1)}, bf16[64,1024]{1,0:T(8,128)(2,1)}, u32[]{:S(2)}) copy-start(bf16[64,1024]{1,0:T(8,128)(2,1)} %keys_ref.1) | copy-start | bytes 393220
  2.6 30.3 %copy-start.1 = (f32[8,128,128]{2,1,0:T(8,128)S(1)}, f32[8,128,128]{2,1,0:T(8,128)}, u32[]{:S(2)}) copy-start(f32[8,128,128]{2,1,0:T(8,128)} %query_map_ref.1) | copy-start | bytes 1572868
  2.7 31.2 %copy-start.3 = (f32[2,128,128]{2,1,0:T(8,128)S(1)}, f32[2,128,128]{2,1,0:T(8,128)}, u32[]{:S(2)}) copy-start(f32[2,128,128]{2,1,0:T(8,128)} %refs_3_.1) | copy-start | bytes 393220
  2.7 31.2 %copy-start.4 = (s32[16]{0:T(128)S(1)}, s32[16]{0:T(128)}, u32[]{:S(2)}) copy-start(s32[16]{0:T(128)} %pos_ref.1) | copy-start | bytes 196
  26.7 5.9 %collective-permute-start.1 = (bf16[32,16,128]{2,1,0:T(8,128)(2,1)S(1)}, bf16[32,16,128]{2,1,0:T(8,128)(2,1)S(1)}, u32[]{:S(2)}, u32[]{:S(2)}) collective-permute-start(bf16[32,16,128]{2,1,0:T(8,128)(2,1)S(1)} %slice.16), channel_id=1, source_target_pairs={{0,8},{4,12},{8,0},{12,4},{16,24},{20,28},{24,16},{28,20},{1,9},{5... | collective-permute-start | bytes 393224 | tf_op jit(solution)/shard_map/ppermute | solution.py:475
  28.2 5.6 %collective-permute-start = (bf16[32,16,128]{2,1,0:T(8,128)(2,1)S(1)}, bf16[32,16,128]{2,1,0:T(8,128)(2,1)S(1)}, u32[]{:S(2)}, u32[]{:S(2)}) collective-permute-start(bf16[32,16,128]{2,1,0:T(8,128)(2,1)S(1)} %slice.16), channel_id=1, source_target_pairs={{0,4},{4,0},{8,12},{12,8},{16,20},{20,16},{24,28},{28,24},{1,5},{5... | collective-permute-start | bytes 393224 | tf_op jit(solution)/shard_map/ppermute | solution.py:475
  32.6 1.3 %collective-permute-start.2 = (bf16[32,16,128]{2,1,0:T(8,128)(2,1)S(1)}, bf16[32,16,128]{2,1,0:T(8,128)(2,1)S(1)}, u32[]{:S(2)}, u32[]{:S(2)}) collective-permute-start(bf16[32,16,128]{2,1,0:T(8,128)(2,1)S(1)} %collective-permute-done.1.refs_1_), channel_id=1, source_target_pairs={{0,4},{4,0},{8,12},{12,8},{16,20},{20,16},{24,28},{28,24},{1,5},{5... | collective-permute-start | bytes 393224 | tf_op jit(solution)/shard_map/ppermute | solution.py:475

commit v3 on v2

--- a/solution.py
+++ b/solution.py
@@ -241,23 +241,38 @@
     return nt(parts, jnp.concatenate([tokens] * 3, axis=1))
 
 
-def send_kernel(seq_count, head_count, key_heads, queries_ref, keys_ref, out_ref):
+def send_kernel(seq_count, head_count, key_heads, queries_ref, keys_ref, out_ref, sems):
     rows = queries_ref.shape[0]
     share = seq_count // key_heads
     part = rows // share
+    copies = []
     for head in range(head_count):
         for seq in range(seq_count):
             target = seq * head_count + head
             column = (head * seq_count + seq) * HEAD_SIZE
-            out_ref[target, :rows, :] = queries_ref[:, column : column + HEAD_SIZE]
+            copies.append(
+                pltpu.make_async_copy(
+                    queries_ref.at[:, column : column + HEAD_SIZE],
+                    out_ref.at[target, :rows, :],
+                    sems.at[0, target],
+                )
+            )
             column = (head * key_heads + seq // share) * HEAD_SIZE
             first = seq % share * part
-            out_ref[target, rows:, :] = keys_ref[
-                first : first + part, column : column + HEAD_SIZE
-            ]
-
-
-def query_kernel(rows, mine_ref, arrived_ref, query_map_ref, phi_ref, phi_b_ref):
+            copies.append(
+                pltpu.make_async_copy(
+                    keys_ref.at[first : first + part, column : column + HEAD_SIZE],
+                    out_ref.at[target, rows:, :],
+                    sems.at[1, target],
+                )
+            )
+    for copy in copies:
+        copy.start()
+    for copy in copies:
+        copy.wait()
+
+
+def query_kernel(rows, mine_ref, arrived_ref, query_map_ref, phi_ref):
     per_block = BLK // rows
     parts = map_parts(query_map_ref[mine_ref[0]])
 
@@ -271,9 +286,7 @@
         logits = ahead
         if number + 1 < blocks:
             ahead = block_logits(number + 1)
-        feature = features_t(logits)
-        phi_ref[number] = feature
-        phi_b_ref[number] = feature.astype(BF16)
+        phi_ref[number] = features_t(logits)
 
 
 def pair_kernel(
@@ -290,10 +303,11 @@
     (
         key_map_ref,
         phi_q,
-        phi_qb,
         out_ref,
         stored,
         key_rows,
+        query_rows,
+        phi_qb,
         phi_k,
         phi_kb,
         phi_kb_rows,
@@ -310,6 +324,14 @@
         stored[pos_ref[number]] = number
     acc_q[...] = jnp.zeros_like(acc_q)
     acc_k[...] = jnp.zeros_like(acc_k)
+    width = 2 if seq_blocks % 2 == 0 else 1
+    tiles = seq_blocks // width
+    for seq in range(sequences):
+        for at in range(0, seq_blocks, width):
+            if width > 1:
+                pair_weights[seq, (at + 1) * BLK : (at + 2) * BLK, at * BLK : (at + 1) * BLK] = (
+                    jnp.zeros((BLK, BLK), BF16)
+                )
     mine = mine_ref[0] % share
     parts = map_parts(key_map_ref[mine_ref[0] // share])
     lane = lax.broadcasted_iota(jnp.int32, (BLK, BLK), 1)
@@ -321,14 +343,19 @@
     def block(at):
         return slice(at * BLK, (at + 1) * BLK)
 
+    def span(tile):
+        return slice(tile * width * BLK, (tile + 1) * width * BLK)
+
     def place(seq, at):
         return stored[seq * seq_blocks + at]
 
-    def query_block(seq, at):
+    def load_queries(seq, at):
         first = place(seq, at) * per_block
-        return arrived_ref[pl.ds(first, per_block), :rows, :].reshape(BLK, HEAD_SIZE)
-
-    def key_logits(seq, at):
+        tokens = arrived_ref[pl.ds(first, per_block), :rows, :]
+        query_rows[seq, block(at), :] = tokens.reshape(BLK, HEAD_SIZE)
+        phi_qb[seq, :, block(at)] = phi_q[place(seq, at)].astype(BF16)
+
+    def load_keys(seq, at):
         first = place(seq, at) * per_block
         for chunk in range(per_block):
             for other in range(share):
@@ -340,100 +367,134 @@
                 else:
                     piece = arrived_ref[first + chunk, rows:, :]
                 key_rows[seq, pl.ds(start, part), :] = piece
+
+    def key_logits(seq, at):
         return logits_t(parts, key_rows[seq, block(at), :])
 
     def key_features(seq, at, logits):
         feature = features_t(logits)
         phi_k[seq, :, block(at)] = feature
-        rounded = feature.astype(BF16)
-        phi_kb[seq, :, block(at)] = rounded
-        phi_kb_rows[seq, block(at), :] = nt(unit, rounded).astype(BF16)
-
-    def pair_scores(seq, at):
-        live = (at + 1) * BLK
-        slot = at % 2
-        teacher = nt(key_rows[seq, :live, :], query_block(seq, at))
-        student = nn(phi_kb_rows[seq, :live, :], phi_qb[place(seq, at)])
-        highest = linear_sum = None
-        for number in range(at + 1):
-            here = block(number)
-            score, linear = teacher[here], student[here]
-            linears[seq, slot, here, :] = linear
-            if number == at:
-                score = jnp.where(visible, score, NEG_FLOOR)
-                linear = jnp.where(visible, linear, 0.0)
-            scores[seq, slot, here, :] = score
-            top, total = tile_max(score), tile_sum(linear)
-            highest = top if number == 0 else jnp.maximum(highest, top)
-            linear_sum = total if number == 0 else linear_sum + total
-        return (
-            jnp.max(highest, axis=0, keepdims=True),
-            jnp.sum(linear_sum, axis=0, keepdims=True),
-        )
-
-    def pair_gradients(seq, at, stats):
+        phi_kb[seq, :, block(at)] = feature.astype(BF16)
+
+    def turn_features(seq, at):
+        phi_kb_rows[seq, block(at), :] = nt(unit, phi_kb[seq, :, block(at)]).astype(BF16)
+
+    def pair_scores(seq, tile):
+        here = span(tile)
+        slot = tile % 2
+        teacher = nt(key_rows[seq, : here.stop, :], query_rows[seq, here, :])
+        student = nn(phi_kb_rows[seq, : here.stop, :], phi_qb[seq, :, here])
+        stats = []
+        for half in range(width):
+            at = tile * width + half
+            highest = linear_sum = None
+            for number in range(at + 1):
+                score = teacher[block(number), block(half)]
+                linear = student[block(number), block(half)]
+                linears[seq, slot, block(number), block(half)] = linear
+                if number == at:
+                    score = jnp.where(visible, score, NEG_FLOOR)
+                    linear = jnp.where(visible, linear, 0.0)
+                scores[seq, slot, block(number), block(half)] = score
+                top, total = tile_max(score), tile_sum(linear)
+                highest = top if number == 0 else jnp.maximum(highest, top)
+                linear_sum = total if number == 0 else linear_sum + total
+            stats.append(
+                (
+                    jnp.max(highest, axis=0, keepdims=True),
+                    jnp.sum(linear_sum, axis=0, keepdims=True),
+                )
+            )
+        return stats
+
+    def pair_gradients(seq, tile, half, stats):
         highest, linear_sum = stats
-        slot = at % 2
+        slot = tile % 2
+        at = tile * width + half
         denominator = None
         for number in range(at + 1):
-            here = block(number)
-            exponent = jnp.exp2((scores[seq, slot, here, :] - highest) * exponent_scale)
-            scores[seq, slot, here, :] = exponent
+            score = scores[seq, slot, block(number), block(half)]
+            exponent = jnp.exp2((score - highest) * exponent_scale)
+            scores[seq, slot, block(number), block(half)] = exponent
             total = tile_sum(exponent)
             denominator = total if number == 0 else denominator + total
         denominator = jnp.sum(denominator, axis=0, keepdims=True)
         base = 1.0 / (linear_sum * token_count)
         rate = 1.0 / (denominator * token_count)
         for number in range(at + 1):
-            here = block(number)
-            weights = base - scores[seq, slot, here, :] * rate / linears[seq, slot, here, :]
+            exponent = scores[seq, slot, block(number), block(half)]
+            weights = base - exponent * rate / linears[seq, slot, block(number), block(half)]
             if number == at:
                 weights = jnp.where(visible, weights, 0.0)
-            pair_weights[seq, here, block(at)] = weights.astype(BF16)
-
-    def query_grads(seq, at):
-        live = (at + 1) * BLK
-        upstream = nn(phi_kb[seq, :, :live], pair_weights[seq, :live, block(at)])
-        change = side_parts(feature_grad_t(phi_q[place(seq, at)], upstream))
-        tokens = query_block(seq, at)
-        acc_q[...] += nn(change, jnp.concatenate([tokens, tokens], axis=0))
-
-    def key_grads(seq, at):
-        later = slice(at * BLK, seq_blocks * BLK)
-        phi = jnp.concatenate(
-            [phi_qb[place(seq, number)] for number in range(at, seq_blocks)], axis=1
-        )
-        upstream = nt(phi, pair_weights[seq, block(at), later])
-        change = side_parts(feature_grad_t(phi_k[seq, :, block(at)], upstream))
-        tokens = key_rows[seq, block(at), :]
-        acc_k[...] += nn(change, jnp.concatenate([tokens, tokens], axis=0))
+            pair_weights[seq, block(number), block(at)] = weights.astype(BF16)
+
+    def map_change(phis, upstream, tokens):
+        changes = [
+            side_parts(feature_grad_t(phi, upstream[:, block(half)]))
+            for half, phi in enumerate(phis)
+        ]
+        twice = [tokens[block(half)] for half in range(width) for _ in range(2)]
+        return nn(jnp.concatenate(changes, axis=1), jnp.concatenate(twice, axis=0))
+
+    def query_upstream(seq, tile):
+        here = span(tile)
+        return nn(phi_kb[seq, :, : here.stop], pair_weights[seq, : here.stop, here])
+
+    def query_change(seq, tile, upstream):
+        phis = [phi_q[place(seq, tile * width + half)] for half in range(width)]
+        acc_q[...] += map_change(phis, upstream, query_rows[seq, span(tile), :])
+
+    def key_upstream(seq, tile):
+        later = slice(tile * width * BLK, seq_blocks * BLK)
+        return nt(phi_qb[seq, :, later], pair_weights[seq, span(tile), later])
+
+    def key_change(seq, tile, upstream):
+        phis = [phi_k[seq, :, block(tile * width + half)] for half in range(width)]
+        acc_k[...] += map_change(phis, upstream, key_rows[seq, span(tile), :])
 
     def feature_steps(seq):
-        ahead = key_logits(seq, 0)
+        ahead = [key_logits(seq, at) for at in range(min(3, seq_blocks))]
         for at in range(seq_blocks):
-            logits = ahead
-            if at + 1 < seq_blocks:
-                ahead = key_logits(seq, at + 1)
-            key_features(seq, at, logits)
+            if at + len(ahead) < seq_blocks:
+                ahead.append(key_logits(seq, at + len(ahead)))
+            key_features(seq, at, ahead.pop(0))
+            if at > 1:
+                turn_features(seq, at - 2)
             yield
+        for at in range(max(seq_blocks - 2, 0), seq_blocks):
+            turn_features(seq, at)
 
     def pair_steps(seq):
         ahead = pair_scores(seq, 0)
+        behind = None
+        for tile in range(tiles):
+            stats = ahead
+            if tile + 1 < tiles:
+                ahead = pair_scores(seq, tile + 1)
+            for half in range(width):
+                pair_gradients(seq, tile, half, stats[half])
+                yield
+            upstream = query_upstream(seq, tile)
+            if tile:
+                query_change(seq, tile - 1, behind)
+            behind = upstream
+        yield
+        query_change(seq, tiles - 1, behind)
+
+    def key_steps(seq):
+        ahead = key_upstream(seq, 0)
+        yield
+        for tile in range(tiles):
+            upstream = ahead
+            if tile + 1 < tiles:
+                ahead = key_upstream(seq, tile + 1)
+            key_change(seq, tile, upstream)
+            yield
+
+    for seq in range(sequences):
         for at in range(seq_blocks):
-            stats = ahead
-            if at + 1 < seq_blocks:
-                ahead = pair_scores(seq, at + 1)
-            pair_gradients(seq, at, stats)
-            if at:
-                query_grads(seq, at - 1)
-            yield
-        query_grads(seq, seq_blocks - 1)
-
-    def key_steps(seq):
-        for at in range(seq_blocks):
-            key_grads(seq, at)
-            yield
-
+            load_keys(seq, at)
+            load_queries(seq, at)
     stages = (feature_steps, pair_steps, key_steps)
     for turn in range(sequences + len(stages) - 1):
         active = [
@@ -466,7 +527,10 @@
     sent = pl.pallas_call(
         functools.partial(send_kernel, seq_count, head_count, key_heads),
         out_shape=jax.ShapeDtypeStruct((devices, rows + part, HEAD_SIZE), BF16),
-        compiler_params=pltpu.CompilerParams(vmem_limit_bytes=8 << 20),
+        in_specs=[pl.BlockSpec(memory_space=pltpu.HBM)] * 2,
+        out_specs=vmem,
+        scratch_shapes=[pltpu.SemaphoreType.DMA((2, devices))],
+        compiler_params=pltpu.CompilerParams(vmem_limit_bytes=60 << 20),
     )(queries, keys)
     arrived = lax.all_to_all(sent, ("seq", "head"), split_axis=0, concat_axis=0, tiled=True)
     mine = lax.axis_index("seq").astype(jnp.int32).reshape(1)
@@ -474,18 +538,11 @@
     def swap(piece, bit):
         return lax.ppermute(piece, "seq", [(i, i ^ bit) for i in range(seq_count)])
 
-    pieces = [arrived[:, rows:, :]]
-    for other in range(1, share):
-        bit = other & -other
-        pieces.append(swap(pieces[other - bit], bit))
-    phi, phi_b = pl.pallas_call(
+    phi = pl.pallas_call(
         functools.partial(query_kernel, rows),
-        out_shape=(
-            jax.ShapeDtypeStruct((blocks, 2 * HEAD_SIZE, BLK), F32),
-            jax.ShapeDtypeStruct((blocks, 2 * HEAD_SIZE, BLK), BF16),
-        ),
+        out_shape=jax.ShapeDtypeStruct((blocks, 2 * HEAD_SIZE, BLK), F32),
         in_specs=[smem, vmem, vmem],
-        out_specs=(vmem, vmem),
+        out_specs=vmem,
         compiler_params=pltpu.CompilerParams(vmem_limit_bytes=16 << 20),
         cost_estimate=pl.CostEstimate(
             flops=token_count * HEAD_SIZE * HEAD_SIZE * 6,
@@ -493,25 +550,34 @@
             transcendentals=token_count * HEAD_SIZE * 2,
         ),
     )(mine, arrived, query_map)
+    pieces = {0: arrived[:, rows:, :]}
+    for number in range(share.bit_length() - 1):
+        bit = share >> (number + 1)
+        if number and number == share.bit_length() - 2:
+            pieces, phi = lax.optimization_barrier((pieces, phi))
+        pieces |= {other + bit: swap(piece, bit) for other, piece in pieces.items()}
+    pieces = [pieces[other] for other in range(share)]
     grads = pl.pallas_call(
         functools.partial(pair_kernel, token_count, seq_count, rows, share),
         out_shape=jax.ShapeDtypeStruct((3 * HEAD_SIZE, HEAD_SIZE), BF16),
-        in_specs=[smem, smem] + [vmem] * (share + 3),
+        in_specs=[smem, smem] + [vmem] * (share + 2),
         out_specs=vmem,
         scratch_shapes=[
             pltpu.SMEM((blocks,), jnp.int32),
             pltpu.VMEM((sequences, seq_tokens, HEAD_SIZE), BF16),
+            pltpu.VMEM((sequences, seq_tokens, HEAD_SIZE), BF16),
+            pltpu.VMEM((sequences, 2 * HEAD_SIZE, seq_tokens), BF16),
             pltpu.VMEM((sequences, 2 * HEAD_SIZE, seq_tokens), F32),
             pltpu.VMEM((sequences, 2 * HEAD_SIZE, seq_tokens), BF16),
             pltpu.VMEM((sequences, seq_tokens, 2 * HEAD_SIZE), BF16),
             pltpu.VMEM((sequences, seq_tokens, seq_tokens), BF16),
-            pltpu.VMEM((sequences, 2, seq_tokens, BLK), F32),
-            pltpu.VMEM((sequences, 2, seq_tokens, BLK), F32),
+            pltpu.VMEM((sequences, 2, seq_tokens, 2 * BLK), F32),
+            pltpu.VMEM((sequences, 2, seq_tokens, 2 * BLK), F32),
             pltpu.VMEM((HEAD_SIZE, HEAD_SIZE), F32),
             pltpu.VMEM((HEAD_SIZE, HEAD_SIZE), F32),
         ],
         compiler_params=pltpu.CompilerParams(vmem_limit_bytes=32 << 20),
-    )(block_pos, mine, arrived, *pieces[1:], key_map, phi, phi_b)
+    )(block_pos, mine, arrived, *pieces[1:], key_map, phi)
     everyone = lax.all_gather(grads, "seq", axis=0, tiled=False)
     everyone = everyone.reshape(seq_count, 3, HEAD_SIZE, HEAD_SIZE).astype(F32)
     key_sums = (everyone[:, 1] + everyone[:, 2]).reshape(

time: 58.9 us -> 55.9 us (0.949)
  local copies, waits for them, and re-layouts: 1.96 us -> 0.02 us
  Pallas kernels: 13.6 us -> 12 us
  waiting for transfers between devices: 3.21 us -> 4.65 us
  starting transfers between devices: 3.11 us -> 2.06 us
    pallas_call x1, Pallas kernels: 12.6 us -> 8.51 us  [per_device_head(): pl.pallas_call(functools.partial(pair_kernel, token_count, seq_count, row...]
    pallas_call x1, Pallas kernels: 0.11 us -> 2.59 us  [per_device_head(): pl.pallas_call(functools.partial(send_kernel, seq_count, head_count, key_...]
    unnamed x10 -> x6, local copies, waits for them, and re-layouts: 1.95 us -> 0.01 us
    ppermute x3, waiting for transfers between devices: 3.21 us -> 4.65 us  [swap(): return lax.ppermute(piece, 'seq', [(i, i ^ bit) for i in range(seq_count)])]
    ppermute x3, starting transfers between devices: 3.11 us -> 2.06 us  [swap(): return lax.ppermute(piece, 'seq', [(i, i ^ bit) for i in range(seq_count)])]
  transfers between devices with their start and end apart: 3 -> 3, of which waited for: 2 -> 3; matrix products, arithmetic and copies ran while one was open for 0% -> 0% of each run, Pallas kernels for 2% -> 2%
where the time goes in v3:
time: 55.9 us; the launch traced here: 55.6 us
  blocking collectives  34.5 us (62%)
  Pallas kernels  12 us (21%)
  waiting for transfers between devices  4.65 us (8%)
  starting transfers between devices  2.06 us (4%)
  other arithmetic  1.73 us (3%)
  between operations  0.68 us (1%)
    all_to_all x1, blocking collectives, per_device_head(): lax.all_to_all(sent, ('seq', 'head'), split_axis=0, concat_axis=0, tiled=...  24.1 us
    all_gather x1, blocking collectives, per_device_head(): everyone = lax.all_gather(grads, 'seq', axis=0, tiled=False)  10.4 us
    pallas_call x1, Pallas kernels, per_device_head(): pl.pallas_call(functools.partial(pair_kernel, token_count, seq_count, row...  8.51 us
    ppermute x3, waiting for transfers between devices, swap(): return lax.ppermute(piece, 'seq', [(i, i ^ bit) for i in range(seq_count)])  4.65 us
    pallas_call x1, Pallas kernels, per_device_head(): pl.pallas_call(functools.partial(send_kernel, seq_count, head_count, key_...  2.59 us
    ppermute x3, starting transfers between devices, swap(): return lax.ppermute(piece, 'seq', [(i, i ^ bit) for i in range(seq_count)])  2.06 us
  transfers between devices with their start and end apart: 3, of which 3 were waited for; matrix products, arithmetic and copies ran while one was open for 0% of the time, Pallas kernels for 2%

profile of v3, /device:TPU:0, one launch (start us, length us, event | category | flops | bytes accessed | tf_op | source)
XLA Modules:
  0.0 55.6 jit_solution(7354909146398205844)
XLA Ops:
  0.6 0.0 copy-start
  0.6 2.6 %shard_map.68 = bf16[32,80,128]{2,1,0:T(8,128)(2,1)} custom-call(bf16[64,4096]{1,0:T(8,128)(2,1)} %queries_ref.1, bf16[64,1024]{1,0:T(8,128)(2,1)} %keys_ref.1), custom_call_target="tpu_custom_call" | custom-call | tf_op jit(solution)/shard_map/pallas_call | solution.py:527
  3.2 24.1 %all_to_all.5.arrived_ref = bf16[32,80,128]{2,1,0:T(8,128)(2,1)S(1)} all-to-all(bf16[32,80,128]{2,1,0:T(8,128)(2,1)} %shard_map.68), channel_id=1, replica_groups=mesh['seq'=8,'head'=4] {'seq','head'}, dimensions={0} | all-to-all | bytes 1310720 | tf_op jit(solution)/shard_map/all_to_all | solution.py:535
  27.4 1.6 %collective-permute-start = (bf16[32,16,128]{2,1,0:T(8,128)(2,1)S(1)}, bf16[32,16,128]{2,1,0:T(8,128)(2,1)S(1)}, u32[]{:S(2)}, u32[]{:S(2)}) collective-permute-start(bf16[32,16,128]{2,1,0:T(8,128)(2,1)S(1)} %slice.16), channel_id=1, source_target_pairs={{0,8},{4,12},{8,0},{12,4},{16,24},{20,28},{24,16},{28,20},{1,9},{5... | collective-permute-start | bytes 393224 | tf_op jit(solution)/shard_map/ppermute | solution.py:539
  28.9 0.0 copy-done
  28.9 0.0 copy-start.1
  28.9 0.0 copy-start.2
  28.9 0.9 %shard_map.69.refs_4_ = f32[16,256,128]{2,1,0:T(8,128)S(1)} custom-call(s32[1]{0:T(128)} %bitcast.mine_ref, bf16[32,80,128]{2,1,0:T(8,128)(2,1)S(1)} %all_to_all.5.arrived_ref, f32[8,128,128]{2,1,0:T(8,128)S(1)} %copy-done), custom_call_target="tpu_custom_call" | custom-call | flops 201326592 | bytes 5242880 | tf_op jit(solution)/shard_map/pallas_call | solution.py:541
  29.8 3.5 %collective-permute-done.refs_1_ = bf16[32,16,128]{2,1,0:T(8,128)(2,1)S(1)} collective-permute-done((bf16[32,16,128]{2,1,0:T(8,128)(2,1)S(1)}, bf16[32,16,128]{2,1,0:T(8,128)(2,1)S(1)}, u32[]{:S(2)}, u32[]{:S(2)}) %collective-permute-start) | collective-permute-done | bytes 131104 | tf_op jit(solution)/shard_map/ppermute | solution.py:539
  33.3 0.3 collective-permute-start.1
  33.6 0.2 collective-permute-start.2
  33.8 0.8 %collective-permute-done.1.refs_0_ = bf16[32,16,128]{2,1,0:T(8,128)(2,1)S(1)} collective-permute-done((bf16[32,16,128]{2,1,0:T(8,128)(2,1)S(1)}, bf16[32,16,128]{2,1,0:T(8,128)(2,1)S(1)}, u32[]{:S(2)}, u32[]{:S(2)}) %collective-permute-start.1) | collective-permute-done | bytes 131104 | tf_op jit(solution)/shard_map/ppermute | solution.py:539
  34.6 0.3 collective-permute-done.2.refs_2_
  35.0 0.0 copy-done.1
  35.0 0.0 copy-done.2
  35.0 8.5 %shard_map.70 = bf16[384,128]{1,0:T(8,128)(2,1)S(1)} custom-call(s32[16]{0:T(128)S(1)} %copy-done.2, s32[1]{0:T(128)} %bitcast.mine_ref, bf16[32,80,128]{2,1,0:T(8,128)(2,1)S(1)} %all_to_all.5.arrived_ref, bf16[32,16,128]{2,1,0:T(8,128)(2,1)S(1)} %collective-permute-done.1.refs_0_, bf16[32,16,128]{2,1,0:T(8,128)(2,1)S(1)} %collective-permute-done.refs_1_, ...), custom_call_target="tpu_custom_call" | custom-call | tf_op jit(solution)/shard_map/pallas_call | solution.py:560
  43.5 10.4 %all-gather = bf16[3072,128]{1,0:T(8,128)(2,1)S(1)} all-gather(bf16[384,128]{1,0:T(8,128)(2,1)S(1)} %shard_map.70), channel_id=2, replica_groups=mesh['seq'=8,'head'=4] {'seq'}, dimensions={0}, use_global_device_ids=true | all-gather | bytes 884736 | tf_op jit(solution)/shard_map/all_gather | solution.py:581
  53.9 0.2 convert.1
  54.1 0.9 %slice_add_fusion = (f32[8,1,128,128]{3,2,1,0:T(8,128)S(1)}, f32[8,128,128]{2,1,0:T(8,128)}) fusion(f32[8,3,128,128]{3,2,1,0:T(8,128)S(1)} %convert.1), kind=kLoop, calls=%fused_computation | loop fusion | flops 131072 | bytes 2621440 | tf_op jit(solution)/shard_map/add | solution.py:583
  55.0 0.7 %bitcast_reduce_fusion = f32[2,128,128]{2,1,0:T(8,128)} fusion(f32[2,4,128,128]{3,2,1,0:T(8,128)S(1)} %bitcast.11), kind=kLoop, calls=%fused_computation.2 | loop fusion | flops 98304 | bytes 655360 | tf_op jit(solution)/shard_map/reduce_sum | solution.py:586
  (1 shorter events, 0.0 us)
Async XLA Ops:
  0.6 28.3 %copy-start = (f32[8,128,128]{2,1,0:T(8,128)S(1)}, f32[8,128,128]{2,1,0:T(8,128)}, u32[]{:S(2)}) copy-start(f32[8,128,128]{2,1,0:T(8,128)} %query_map_ref.1) | copy-start | bytes 1572868
  27.4 5.9 %collective-permute-start = (bf16[32,16,128]{2,1,0:T(8,128)(2,1)S(1)}, bf16[32,16,128]{2,1,0:T(8,128)(2,1)S(1)}, u32[]{:S(2)}, u32[]{:S(2)}) collective-permute-start(bf16[32,16,128]{2,1,0:T(8,128)(2,1)S(1)} %slice.16), channel_id=1, source_target_pairs={{0,8},{4,12},{8,0},{12,4},{16,24},{20,28},{24,16},{28,20},{1,9},{5... | collective-permute-start | bytes 393224 | tf_op jit(solution)/shard_map/ppermute | solution.py:539
  28.9 6.1 %copy-start.1 = (f32[2,128,128]{2,1,0:T(8,128)S(1)}, f32[2,128,128]{2,1,0:T(8,128)}, u32[]{:S(2)}) copy-start(f32[2,128,128]{2,1,0:T(8,128)} %refs_3_.1) | copy-start | bytes 393220
  28.9 6.1 %copy-start.2 = (s32[16]{0:T(128)S(1)}, s32[16]{0:T(128)}, u32[]{:S(2)}) copy-start(s32[16]{0:T(128)} %pos_ref.1) | copy-start | bytes 196
  33.3 1.3 %collective-permute-start.1 = (bf16[32,16,128]{2,1,0:T(8,128)(2,1)S(1)}, bf16[32,16,128]{2,1,0:T(8,128)(2,1)S(1)}, u32[]{:S(2)}, u32[]{:S(2)}) collective-permute-start(bf16[32,16,128]{2,1,0:T(8,128)(2,1)S(1)} %slice.16), channel_id=1, source_target_pairs={{0,4},{4,0},{8,12},{12,8},{16,20},{20,16},{24,28},{28,24},{1,5},{5... | collective-permute-start | bytes 393224 | tf_op jit(solution)/shard_map/ppermute | solution.py:539
  33.6 1.3 %collective-permute-start.2 = (bf16[32,16,128]{2,1,0:T(8,128)(2,1)S(1)}, bf16[32,16,128]{2,1,0:T(8,128)(2,1)S(1)}, u32[]{:S(2)}, u32[]{:S(2)}) collective-permute-start(bf16[32,16,128]{2,1,0:T(8,128)(2,1)S(1)} %collective-permute-done.refs_1_), channel_id=1, source_target_pairs={{0,4},{4,0},{8,12},{12,8},{16,20},{20,16},{24,28},{28,24},{1,5},{5... | collective-permute-start | bytes 393224 | tf_op jit(solution)/shard_map/ppermute | solution.py:539

commit v4 on v3

--- a/solution.py
+++ b/solution.py
@@ -241,40 +241,46 @@
     return nt(parts, jnp.concatenate([tokens] * 3, axis=1))
 
 
-def send_kernel(seq_count, head_count, key_heads, queries_ref, keys_ref, out_ref, sems):
+def send_kernel(
+    seq_count, head_count, key_heads, spread, queries_ref, keys_ref, out_ref, buffer, sems
+):
     rows = queries_ref.shape[0]
     share = seq_count // key_heads
-    part = rows // share
-    copies = []
+    part = rows // spread
+    arriving, leaving = [], []
     for head in range(head_count):
         for seq in range(seq_count):
             target = seq * head_count + head
             column = (head * seq_count + seq) * HEAD_SIZE
-            copies.append(
-                pltpu.make_async_copy(
-                    queries_ref.at[:, column : column + HEAD_SIZE],
-                    out_ref.at[target, :rows, :],
-                    sems.at[0, target],
-                )
+            query_copy = pltpu.make_async_copy(
+                queries_ref.at[:, column : column + HEAD_SIZE],
+                buffer.at[target, :rows, :],
+                sems.at[0, target],
             )
             column = (head * key_heads + seq // share) * HEAD_SIZE
-            first = seq % share * part
-            copies.append(
-                pltpu.make_async_copy(
-                    keys_ref.at[first : first + part, column : column + HEAD_SIZE],
-                    out_ref.at[target, rows:, :],
-                    sems.at[1, target],
-                )
-            )
-    for copy in copies:
+            first = seq % spread * part
+            key_copy = pltpu.make_async_copy(
+                keys_ref.at[first : first + part, column : column + HEAD_SIZE],
+                buffer.at[target, rows:, :],
+                sems.at[1, target],
+            )
+            query_copy.start()
+            key_copy.start()
+            arriving.append((query_copy, key_copy))
+            leaving.append(
+                pltpu.make_async_copy(buffer.at[target], out_ref.at[target], sems.at[2, target])
+            )
+    for copies, copy in zip(arriving, leaving):
+        for earlier in copies:
+            earlier.wait()
         copy.start()
-    for copy in copies:
+    for copy in leaving:
         copy.wait()
 
 
-def query_kernel(rows, mine_ref, arrived_ref, query_map_ref, phi_ref):
+def query_kernel(rows, arrived_ref, query_map_ref, phi_ref):
     per_block = BLK // rows
-    parts = map_parts(query_map_ref[mine_ref[0]])
+    parts = map_parts(query_map_ref[lax.axis_index("seq")])
 
     def block_logits(number):
         tokens = arrived_ref[number * per_block : (number + 1) * per_block, :rows, :]
@@ -294,12 +300,12 @@
     seq_blocks,
     rows,
     share,
+    spread,
     pos_ref,
-    mine_ref,
     arrived_ref,
     *refs,
 ):
-    key_refs, refs = refs[: share - 1], refs[share - 1 :]
+    key_refs, refs = refs[: spread - 1], refs[spread - 1 :]
     (
         key_map_ref,
         phi_q,
@@ -318,7 +324,7 @@
         acc_k,
     ) = refs
     per_block = BLK // rows
-    part = rows // share
+    part = rows // spread
     sequences = token_count // (seq_blocks * BLK)
     for number in range(token_count // BLK):
         stored[pos_ref[number]] = number
@@ -332,8 +338,9 @@
                 pair_weights[seq, (at + 1) * BLK : (at + 2) * BLK, at * BLK : (at + 1) * BLK] = (
                     jnp.zeros((BLK, BLK), BF16)
                 )
-    mine = mine_ref[0] % share
-    parts = map_parts(key_map_ref[mine_ref[0] // share])
+    mine = lax.axis_index("seq")
+    parts = map_parts(key_map_ref[lax.div(mine, share)])
+    mine = lax.rem(mine, spread)
     lane = lax.broadcasted_iota(jnp.int32, (BLK, BLK), 1)
     sublane = lax.broadcasted_iota(jnp.int32, (BLK, BLK), 0)
     unit = jnp.where(lane == sublane, 1.0, 0.0).astype(BF16)
@@ -358,7 +365,7 @@
     def load_keys(seq, at):
         first = place(seq, at) * per_block
         for chunk in range(per_block):
-            for other in range(share):
+            for other in range(spread):
                 start = pl.multiple_of(
                     at * BLK + chunk * rows + (mine ^ other) * part, part
                 )
@@ -516,7 +523,8 @@
     key_heads = key_map.shape[0]
     share = seq_count // key_heads
     rows = queries.shape[0]
-    part = rows // share
+    spread = math.gcd(share, 2)
+    part = rows // spread
     devices = seq_count * head_count
     token_count = rows * devices
     blocks = token_count // BLK
@@ -524,24 +532,26 @@
     sequences = token_count // seq_tokens
     vmem = pl.BlockSpec(memory_space=pltpu.VMEM)
     smem = pl.BlockSpec(memory_space=pltpu.SMEM)
+    sent_shape = (devices, rows + part, HEAD_SIZE)
     sent = pl.pallas_call(
-        functools.partial(send_kernel, seq_count, head_count, key_heads),
-        out_shape=jax.ShapeDtypeStruct((devices, rows + part, HEAD_SIZE), BF16),
-        in_specs=[pl.BlockSpec(memory_space=pltpu.HBM)] * 2,
-        out_specs=vmem,
-        scratch_shapes=[pltpu.SemaphoreType.DMA((2, devices))],
+        functools.partial(send_kernel, seq_count, head_count, key_heads, spread),
+        out_shape=jax.ShapeDtypeStruct(sent_shape, BF16),
+        in_specs=[pl.BlockSpec(memory_space=pl.ANY)] * 2,
+        out_specs=pl.BlockSpec(memory_space=pl.ANY),
+        scratch_shapes=[
+            pltpu.VMEM(sent_shape, BF16),
+            pltpu.SemaphoreType.DMA((3, devices)),
+        ],
         compiler_params=pltpu.CompilerParams(vmem_limit_bytes=60 << 20),
     )(queries, keys)
     arrived = lax.all_to_all(sent, ("seq", "head"), split_axis=0, concat_axis=0, tiled=True)
-    mine = lax.axis_index("seq").astype(jnp.int32).reshape(1)
-
     def swap(piece, bit):
         return lax.ppermute(piece, "seq", [(i, i ^ bit) for i in range(seq_count)])
 
     phi = pl.pallas_call(
         functools.partial(query_kernel, rows),
         out_shape=jax.ShapeDtypeStruct((blocks, 2 * HEAD_SIZE, BLK), F32),
-        in_specs=[smem, vmem, vmem],
+        in_specs=[vmem, vmem],
         out_specs=vmem,
         compiler_params=pltpu.CompilerParams(vmem_limit_bytes=16 << 20),
         cost_estimate=pl.CostEstimate(
@@ -549,18 +559,14 @@
             bytes_accessed=token_count * HEAD_SIZE * 20,
             transcendentals=token_count * HEAD_SIZE * 2,
         ),
-    )(mine, arrived, query_map)
-    pieces = {0: arrived[:, rows:, :]}
-    for number in range(share.bit_length() - 1):
-        bit = share >> (number + 1)
-        if number and number == share.bit_length() - 2:
-            pieces, phi = lax.optimization_barrier((pieces, phi))
-        pieces |= {other + bit: swap(piece, bit) for other, piece in pieces.items()}
-    pieces = [pieces[other] for other in range(share)]
+    )(arrived, query_map)
+    pieces = [arrived[:, rows:, :]]
+    for other in range(1, spread):
+        pieces.append(swap(pieces[0], other))
     grads = pl.pallas_call(
-        functools.partial(pair_kernel, token_count, seq_count, rows, share),
+        functools.partial(pair_kernel, token_count, seq_count, rows, share, spread),
         out_shape=jax.ShapeDtypeStruct((3 * HEAD_SIZE, HEAD_SIZE), BF16),
-        in_specs=[smem, smem] + [vmem] * (share + 2),
+        in_specs=[smem] + [vmem] * (spread + 2),
         out_specs=vmem,
         scratch_shapes=[
             pltpu.SMEM((blocks,), jnp.int32),
@@ -577,7 +583,7 @@
             pltpu.VMEM((HEAD_SIZE, HEAD_SIZE), F32),
         ],
         compiler_params=pltpu.CompilerParams(vmem_limit_bytes=32 << 20),
-    )(block_pos, mine, arrived, *pieces[1:], key_map, phi)
+    )(block_pos, arrived, *pieces[1:], key_map, phi)
     everyone = lax.all_gather(grads, "seq", axis=0, tiled=False)
     everyone = everyone.reshape(seq_count, 3, HEAD_SIZE, HEAD_SIZE).astype(F32)
     key_sums = (everyone[:, 1] + everyone[:, 2]).reshape(
@@ -592,9 +598,8 @@
     one_head_each = (
         query_map.shape[0] == seq_count
         and seq_count == share * key_map.shape[0]
-        and share & (share - 1) == 0
         and BLK % queries.shape[0] == 0
-        and queries.shape[0] % (16 * share) == 0
+        and queries.shape[0] % 32 == 0
     )
     chosen = per_device_head if one_head_each else per_device_general
     return chosen(queries, keys, block_pos, query_map, key_map)

time: 55.9 us -> 53.9 us (0.964)
  waiting for transfers between devices: 4.65 us -> 0.26 us
  blocking collectives: 34.5 us -> 37.2 us
    ppermute x3 -> x1, waiting for transfers between devices: 4.65 us -> 0.26 us  [swap(): return lax.ppermute(piece, 'seq', [(i, i ^ bit) for i in range(seq_count)])]
    all_to_all x1, blocking collectives: 24.1 us -> 26.8 us  [per_device_head(): lax.all_to_all(sent, ('seq', 'head'), split_axis=0, concat_axis=0, tiled=...]
    ppermute x3 -> x1, starting transfers between devices: 2.06 us -> 1.63 us  [swap(): return lax.ppermute(piece, 'seq', [(i, i ^ bit) for i in range(seq_count)])]
  transfers between devices with their start and end apart: 3 -> 1, of which waited for: 3 -> 1; matrix products, arithmetic and copies ran while one was open for 0% -> 0% of each run, Pallas kernels for 2% -> 2%
where the time goes in v4:
time: 53.9 us; the launch traced here: 53.7 us
  blocking collectives  37.2 us (69%)
  Pallas kernels  12.1 us (22%)
  other arithmetic  1.74 us (3%)
  starting transfers between devices  1.63 us (3%)
  between operations  0.69 us (1%)
    all_to_all x1, blocking collectives, per_device_head(): lax.all_to_all(sent, ('seq', 'head'), split_axis=0, concat_axis=0, tiled=...  26.8 us
    all_gather x1, blocking collectives, per_device_head(): everyone = lax.all_gather(grads, 'seq', axis=0, tiled=False)  10.4 us
    pallas_call x1, Pallas kernels, per_device_head(): pl.pallas_call(functools.partial(pair_kernel, token_count, seq_count, row...  8.53 us
    pallas_call x1, Pallas kernels, per_device_head(): pl.pallas_call(functools.partial(send_kernel, seq_count, head_count, key_...  2.7 us
    ppermute x1, starting transfers between devices, swap(): return lax.ppermute(piece, 'seq', [(i, i ^ bit) for i in range(seq_count)])  1.63 us
  transfers between devices with their start and end apart: 1, of which 1 were waited for; matrix products, arithmetic and copies ran while one was open for 0% of the time, Pallas kernels for 2%

profile of v4, /device:TPU:0, one launch (start us, length us, event | category | flops | bytes accessed | tf_op | source)
XLA Modules:
  0.0 53.7 jit_solution(5762056690918769388)
XLA Ops:
  0.6 0.0 copy-start
  0.6 2.7 %shard_map.68 = bf16[32,96,128]{2,1,0:T(8,128)(2,1)} custom-call(bf16[64,4096]{1,0:T(8,128)(2,1)} %queries_ref.1, bf16[64,1024]{1,0:T(8,128)(2,1)} %keys_ref.1), custom_call_target="tpu_custom_call" | custom-call | tf_op jit(solution)/shard_map/pallas_call | solution.py:536
  3.3 26.8 %all_to_all.5.arrived_ref = bf16[32,96,128]{2,1,0:T(8,128)(2,1)S(1)} all-to-all(bf16[32,96,128]{2,1,0:T(8,128)(2,1)} %shard_map.68), channel_id=1, replica_groups=mesh['seq'=8,'head'=4] {'seq','head'}, dimensions={0} | all-to-all | bytes 1572864 | tf_op jit(solution)/shard_map/all_to_all | solution.py:547
  30.2 0.0 copy-start.1
  30.2 0.0 copy-start.2
  30.2 1.6 %collective-permute-start = (bf16[32,32,128]{2,1,0:T(8,128)(2,1)S(1)}, bf16[32,32,128]{2,1,0:T(8,128)(2,1)S(1)}, u32[]{:S(2)}, u32[]{:S(2)}) collective-permute-start(bf16[32,32,128]{2,1,0:T(8,128)(2,1)S(1)} %slice.16), channel_id=1, source_target_pairs={{0,4},{4,0},{8,12},{12,8},{16,20},{20,16},{24,28},{28,24},{1,5},{5... | collective-permute-start | bytes 786440 | tf_op jit(solution)/shard_map/ppermute | solution.py:549
  31.8 0.0 copy-done
  31.9 0.9 %shard_map.69.refs_2_ = f32[16,256,128]{2,1,0:T(8,128)S(1)} custom-call(bf16[32,96,128]{2,1,0:T(8,128)(2,1)S(1)} %all_to_all.5.arrived_ref, f32[8,128,128]{2,1,0:T(8,128)S(1)} %copy-done), custom_call_target="tpu_custom_call" | custom-call | flops 201326592 | bytes 5242880 | tf_op jit(solution)/shard_map/pallas_call | solution.py:551
  32.7 0.3 collective-permute-done.refs_0_
  33.0 0.0 copy-done.1
  33.0 0.0 copy-done.2
  33.0 8.5 %shard_map.70 = bf16[384,128]{1,0:T(8,128)(2,1)S(1)} custom-call(s32[16]{0:T(128)S(1)} %copy-done.2, bf16[32,96,128]{2,1,0:T(8,128)(2,1)S(1)} %all_to_all.5.arrived_ref, bf16[32,32,128]{2,1,0:T(8,128)(2,1)S(1)} %collective-permute-done.refs_0_, f32[2,128,128]{2,1,0:T(8,128)S(1)} %copy-done.1, f32[16,256,128]{2,1,0:T(8,128)S(1)} %shard_map.69.refs_2_), custom_call_target="tpu_custom_call" | custom-call | tf_op jit(solution)/shard_map/pallas_call | solution.py:566
  41.5 10.4 %all-gather = bf16[3072,128]{1,0:T(8,128)(2,1)S(1)} all-gather(bf16[384,128]{1,0:T(8,128)(2,1)S(1)} %shard_map.70), channel_id=2, replica_groups=mesh['seq'=8,'head'=4] {'seq'}, dimensions={0}, use_global_device_ids=true | all-gather | bytes 884736 | tf_op jit(solution)/shard_map/all_gather | solution.py:587
  51.9 0.2 convert.1
  52.1 0.9 %slice_add_fusion = (f32[8,1,128,128]{3,2,1,0:T(8,128)S(1)}, f32[8,128,128]{2,1,0:T(8,128)}) fusion(f32[8,3,128,128]{3,2,1,0:T(8,128)S(1)} %convert.1), kind=kLoop, calls=%fused_computation | loop fusion | flops 131072 | bytes 2621440 | tf_op jit(solution)/shard_map/add | solution.py:589
  53.0 0.7 %bitcast_reduce_fusion = f32[2,128,128]{2,1,0:T(8,128)} fusion(f32[2,4,128,128]{3,2,1,0:T(8,128)S(1)} %bitcast.10), kind=kLoop, calls=%fused_computation.2 | loop fusion | flops 98304 | bytes 655360 | tf_op jit(solution)/shard_map/reduce_sum | solution.py:592
  (1 shorter events, 0.0 us)
Async XLA Ops:
  0.6 31.2 %copy-start = (f32[8,128,128]{2,1,0:T(8,128)S(1)}, f32[8,128,128]{2,1,0:T(8,128)}, u32[]{:S(2)}) copy-start(f32[8,128,128]{2,1,0:T(8,128)} %query_map_ref.1) | copy-start | bytes 1572868
  30.2 2.8 %copy-start.1 = (f32[2,128,128]{2,1,0:T(8,128)S(1)}, f32[2,128,128]{2,1,0:T(8,128)}, u32[]{:S(2)}) copy-start(f32[2,128,128]{2,1,0:T(8,128)} %refs_1_.1) | copy-start | bytes 393220
  30.2 2.8 %copy-start.2 = (s32[16]{0:T(128)S(1)}, s32[16]{0:T(128)}, u32[]{:S(2)}) copy-start(s32[16]{0:T(128)} %pos_ref.1) | copy-start | bytes 196
  30.2 2.8 %collective-permute-start = (bf16[32,32,128]{2,1,0:T(8,128)(2,1)S(1)}, bf16[32,32,128]{2,1,0:T(8,128)(2,1)S(1)}, u32[]{:S(2)}, u32[]{:S(2)}) collective-permute-start(bf16[32,32,128]{2,1,0:T(8,128)(2,1)S(1)} %slice.16), channel_id=1, source_target_pairs={{0,4},{4,0},{8,12},{12,8},{16,20},{20,16},{24,28},{28,24},{1,5},{5... | collective-permute-start | bytes 786440 | tf_op jit(solution)/shard_map/ppermute | solution.py:549

commit v5 on v4

--- a/solution.py
+++ b/solution.py
@@ -7,6 +7,7 @@
 from jax.experimental import pallas as pl
 from jax.experimental.pallas import tpu as pltpu
 from jax.sharding import PartitionSpec as P
+
 
 HEAD_SIZE = 128
 BLK = 128
@@ -241,41 +242,30 @@
     return nt(parts, jnp.concatenate([tokens] * 3, axis=1))
 
 
-def send_kernel(
-    seq_count, head_count, key_heads, spread, queries_ref, keys_ref, out_ref, buffer, sems
-):
-    rows = queries_ref.shape[0]
-    share = seq_count // key_heads
-    part = rows // spread
-    arriving, leaving = [], []
+def key_send_kernel(keys_ref, *out_refs):
+    head = lax.axis_index("head")
+    key_heads = out_refs[0].shape[0]
+    for other, out_ref in enumerate(out_refs):
+        for number in range(key_heads):
+            column = ((head ^ other) * key_heads + number) * HEAD_SIZE
+            column = pl.multiple_of(column, HEAD_SIZE)
+            out_ref[number] = keys_ref[:, pl.ds(column, HEAD_SIZE)]
+
+
+def query_send_kernel(seq_count, head_count, queries_ref, out_ref):
     for head in range(head_count):
         for seq in range(seq_count):
-            target = seq * head_count + head
             column = (head * seq_count + seq) * HEAD_SIZE
-            query_copy = pltpu.make_async_copy(
-                queries_ref.at[:, column : column + HEAD_SIZE],
-                buffer.at[target, :rows, :],
-                sems.at[0, target],
-            )
-            column = (head * key_heads + seq // share) * HEAD_SIZE
-            first = seq % spread * part
-            key_copy = pltpu.make_async_copy(
-                keys_ref.at[first : first + part, column : column + HEAD_SIZE],
-                buffer.at[target, rows:, :],
-                sems.at[1, target],
-            )
-            query_copy.start()
-            key_copy.start()
-            arriving.append((query_copy, key_copy))
-            leaving.append(
-                pltpu.make_async_copy(buffer.at[target], out_ref.at[target], sems.at[2, target])
-            )
-    for copies, copy in zip(arriving, leaving):
-        for earlier in copies:
-            earlier.wait()
-        copy.start()
-    for copy in leaving:
-        copy.wait()
+            out_ref[seq * head_count + head] = queries_ref[:, column : column + HEAD_SIZE]
+
+
+def key_turn_kernel(share, *refs):
+    key_heads = refs[0].shape[0]
+    in_refs, out_refs = refs[:-key_heads], refs[-key_heads:]
+    mine = lax.div(lax.axis_index("seq"), share)
+    for other, out_ref in enumerate(out_refs):
+        for number, in_ref in enumerate(in_refs):
+            out_ref[number] = in_ref[mine ^ other]
 
 
 def query_kernel(rows, arrived_ref, query_map_ref, phi_ref):
@@ -283,7 +273,7 @@
     parts = map_parts(query_map_ref[lax.axis_index("seq")])
 
     def block_logits(number):
-        tokens = arrived_ref[number * per_block : (number + 1) * per_block, :rows, :]
+        tokens = arrived_ref[number * per_block : (number + 1) * per_block]
         return logits_t(parts, tokens.reshape(BLK, HEAD_SIZE))
 
     blocks = phi_ref.shape[0]
@@ -300,12 +290,12 @@
     seq_blocks,
     rows,
     share,
-    spread,
     pos_ref,
     arrived_ref,
     *refs,
 ):
-    key_refs, refs = refs[: spread - 1], refs[spread - 1 :]
+    seq_count, head_count = lax.axis_size("seq"), lax.axis_size("head")
+    key_refs, refs = refs[:seq_count], refs[seq_count:]
     (
         key_map_ref,
         phi_q,
@@ -324,7 +314,7 @@
         acc_k,
     ) = refs
     per_block = BLK // rows
-    part = rows // spread
+    seq_tokens = seq_blocks * BLK
     sequences = token_count // (seq_blocks * BLK)
     for number in range(token_count // BLK):
         stored[pos_ref[number]] = number
@@ -338,9 +328,8 @@
                 pair_weights[seq, (at + 1) * BLK : (at + 2) * BLK, at * BLK : (at + 1) * BLK] = (
                     jnp.zeros((BLK, BLK), BF16)
                 )
-    mine = lax.axis_index("seq")
+    mine, plane = lax.axis_index("seq"), lax.axis_index("head")
     parts = map_parts(key_map_ref[lax.div(mine, share)])
-    mine = lax.rem(mine, spread)
     lane = lax.broadcasted_iota(jnp.int32, (BLK, BLK), 1)
     sublane = lax.broadcasted_iota(jnp.int32, (BLK, BLK), 0)
     unit = jnp.where(lane == sublane, 1.0, 0.0).astype(BF16)
@@ -356,27 +345,18 @@
     def place(seq, at):
         return stored[seq * seq_blocks + at]
 
-    def load_queries(seq, at):
-        first = place(seq, at) * per_block
-        tokens = arrived_ref[pl.ds(first, per_block), :rows, :]
-        query_rows[seq, block(at), :] = tokens.reshape(BLK, HEAD_SIZE)
+    def flat(seq, here):
+        return slice(seq * seq_tokens + here.start, seq * seq_tokens + here.stop)
+
+    def sorted_rows(chunk):
+        first = pos_ref[lax.div(chunk, per_block)] * BLK + lax.rem(chunk, per_block) * rows
+        return pl.ds(pl.multiple_of(first, rows), rows)
+
+    def load_features(seq, at):
         phi_qb[seq, :, block(at)] = phi_q[place(seq, at)].astype(BF16)
 
-    def load_keys(seq, at):
-        first = place(seq, at) * per_block
-        for chunk in range(per_block):
-            for other in range(spread):
-                start = pl.multiple_of(
-                    at * BLK + chunk * rows + (mine ^ other) * part, part
-                )
-                if other:
-                    piece = key_refs[other - 1][first + chunk]
-                else:
-                    piece = arrived_ref[first + chunk, rows:, :]
-                key_rows[seq, pl.ds(start, part), :] = piece
-
     def key_logits(seq, at):
-        return logits_t(parts, key_rows[seq, block(at), :])
+        return logits_t(parts, key_rows[flat(seq, block(at)), :])
 
     def key_features(seq, at, logits):
         feature = features_t(logits)
@@ -389,7 +369,7 @@
     def pair_scores(seq, tile):
         here = span(tile)
         slot = tile % 2
-        teacher = nt(key_rows[seq, : here.stop, :], query_rows[seq, here, :])
+        teacher = nt(key_rows[flat(seq, slice(0, here.stop)), :], query_rows[flat(seq, here), :])
         student = nn(phi_kb_rows[seq, : here.stop, :], phi_qb[seq, :, here])
         stats = []
         for half in range(width):
@@ -449,7 +429,7 @@
 
     def query_change(seq, tile, upstream):
         phis = [phi_q[place(seq, tile * width + half)] for half in range(width)]
-        acc_q[...] += map_change(phis, upstream, query_rows[seq, span(tile), :])
+        acc_q[...] += map_change(phis, upstream, query_rows[flat(seq, span(tile)), :])
 
     def key_upstream(seq, tile):
         later = slice(tile * width * BLK, seq_blocks * BLK)
@@ -457,7 +437,7 @@
 
     def key_change(seq, tile, upstream):
         phis = [phi_k[seq, :, block(tile * width + half)] for half in range(width)]
-        acc_k[...] += map_change(phis, upstream, key_rows[seq, span(tile), :])
+        acc_k[...] += map_change(phis, upstream, key_rows[flat(seq, span(tile)), :])
 
     def feature_steps(seq):
         ahead = [key_logits(seq, at) for at in range(min(3, seq_blocks))]
@@ -498,10 +478,15 @@
             key_change(seq, tile, upstream)
             yield
 
+    for other in range(seq_count):
+        for number in range(head_count):
+            chunk = (mine ^ other) * head_count + (plane ^ number)
+            key_rows[sorted_rows(chunk), :] = key_refs[other][number]
+    for chunk in range(token_count // rows):
+        query_rows[sorted_rows(chunk), :] = arrived_ref[chunk]
     for seq in range(sequences):
         for at in range(seq_blocks):
-            load_keys(seq, at)
-            load_queries(seq, at)
+            load_features(seq, at)
     stages = (feature_steps, pair_steps, key_steps)
     for turn in range(sequences + len(stages) - 1):
         active = [
@@ -517,14 +502,37 @@
     out_ref[HEAD_SIZE:, :] = bf16_parts(acc_k[...].T, 2)
 
 
+def collect_kernel(everyone_ref, queries_out_ref, keys_out_ref, buffer, sems):
+    seq_count = queries_out_ref.shape[0]
+    key_heads = keys_out_ref.shape[0]
+    share = seq_count // key_heads
+    copies = []
+
+    def leave(number, value, out_ref):
+        buffer[number] = value
+        copies.append(pltpu.make_async_copy(buffer.at[number], out_ref, sems.at[number]))
+        copies[-1].start()
+
+    for number in range(seq_count):
+        leave(number, everyone_ref[number, :HEAD_SIZE, :].astype(F32), queries_out_ref.at[number])
+    for number in range(key_heads):
+        total = None
+        for seq in range(number * share, (number + 1) * share):
+            for half in (1, 2):
+                rows = slice(half * HEAD_SIZE, (half + 1) * HEAD_SIZE)
+                value = everyone_ref[seq, rows, :].astype(F32)
+                total = value if total is None else total + value
+        leave(seq_count + number, total, keys_out_ref.at[number])
+    for copy in copies:
+        copy.wait()
+
+
 def per_device_head(queries, keys, block_pos, query_map, key_map):
     seq_count = lax.axis_size("seq")
     head_count = lax.axis_size("head")
     key_heads = key_map.shape[0]
     share = seq_count // key_heads
     rows = queries.shape[0]
-    spread = math.gcd(share, 2)
-    part = rows // spread
     devices = seq_count * head_count
     token_count = rows * devices
     blocks = token_count // BLK
@@ -532,22 +540,43 @@
     sequences = token_count // seq_tokens
     vmem = pl.BlockSpec(memory_space=pltpu.VMEM)
     smem = pl.BlockSpec(memory_space=pltpu.SMEM)
-    sent_shape = (devices, rows + part, HEAD_SIZE)
+
+    def swap(piece, axis, bits):
+        size = lax.axis_size(axis)
+        return lax.ppermute(piece, axis, [(i, i ^ bits) for i in range(size)])
+
+    small = pltpu.CompilerParams(vmem_limit_bytes=4 << 20)
+    by_plane = pl.pallas_call(
+        key_send_kernel,
+        out_shape=[jax.ShapeDtypeStruct((key_heads, rows, HEAD_SIZE), BF16)] * head_count,
+        in_specs=[vmem],
+        out_specs=[vmem] * head_count,
+        compiler_params=small,
+    )(keys)
+    by_plane = list(by_plane)
+    for other in range(1, head_count):
+        by_plane[other] = swap(by_plane[other], "head", other)
     sent = pl.pallas_call(
-        functools.partial(send_kernel, seq_count, head_count, key_heads, spread),
-        out_shape=jax.ShapeDtypeStruct(sent_shape, BF16),
-        in_specs=[pl.BlockSpec(memory_space=pl.ANY)] * 2,
-        out_specs=pl.BlockSpec(memory_space=pl.ANY),
-        scratch_shapes=[
-            pltpu.VMEM(sent_shape, BF16),
-            pltpu.SemaphoreType.DMA((3, devices)),
-        ],
-        compiler_params=pltpu.CompilerParams(vmem_limit_bytes=60 << 20),
-    )(queries, keys)
+        functools.partial(query_send_kernel, seq_count, head_count),
+        out_shape=jax.ShapeDtypeStruct((devices, rows, HEAD_SIZE), BF16),
+        in_specs=[vmem],
+        out_specs=vmem,
+        compiler_params=small,
+    )(queries)
     arrived = lax.all_to_all(sent, ("seq", "head"), split_axis=0, concat_axis=0, tiled=True)
-    def swap(piece, bit):
-        return lax.ppermute(piece, "seq", [(i, i ^ bit) for i in range(seq_count)])
-
+    by_key_head = pl.pallas_call(
+        functools.partial(key_turn_kernel, share),
+        out_shape=[jax.ShapeDtypeStruct((head_count, rows, HEAD_SIZE), BF16)] * key_heads,
+        in_specs=[vmem] * head_count,
+        out_specs=[vmem] * key_heads,
+        compiler_params=small,
+    )(*by_plane)
+    pieces = [None] * seq_count
+    for other in range(0, seq_count, 2):
+        piece = by_key_head[other // share]
+        pieces[other] = swap(piece, "seq", other) if other else piece
+    for other in range(0, seq_count, 2):
+        pieces[other + 1] = swap(pieces[other], "seq", 1)
     phi = pl.pallas_call(
         functools.partial(query_kernel, rows),
         out_shape=jax.ShapeDtypeStruct((blocks, 2 * HEAD_SIZE, BLK), F32),
@@ -560,18 +589,15 @@
             transcendentals=token_count * HEAD_SIZE * 2,
         ),
     )(arrived, query_map)
-    pieces = [arrived[:, rows:, :]]
-    for other in range(1, spread):
-        pieces.append(swap(pieces[0], other))
     grads = pl.pallas_call(
-        functools.partial(pair_kernel, token_count, seq_count, rows, share, spread),
+        functools.partial(pair_kernel, token_count, seq_count, rows, share),
         out_shape=jax.ShapeDtypeStruct((3 * HEAD_SIZE, HEAD_SIZE), BF16),
-        in_specs=[smem] + [vmem] * (spread + 2),
+        in_specs=[smem] + [vmem] * (seq_count + 3),
         out_specs=vmem,
         scratch_shapes=[
             pltpu.SMEM((blocks,), jnp.int32),
-            pltpu.VMEM((sequences, seq_tokens, HEAD_SIZE), BF16),
-            pltpu.VMEM((sequences, seq_tokens, HEAD_SIZE), BF16),
+            pltpu.VMEM((token_count, HEAD_SIZE), BF16),
+            pltpu.VMEM((token_count, HEAD_SIZE), BF16),
             pltpu.VMEM((sequences, 2 * HEAD_SIZE, seq_tokens), BF16),
             pltpu.VMEM((sequences, 2 * HEAD_SIZE, seq_tokens), F32),
             pltpu.VMEM((sequences, 2 * HEAD_SIZE, seq_tokens), BF16),
@@ -583,26 +609,37 @@
             pltpu.VMEM((HEAD_SIZE, HEAD_SIZE), F32),
         ],
         compiler_params=pltpu.CompilerParams(vmem_limit_bytes=32 << 20),
-    )(block_pos, arrived, *pieces[1:], key_map, phi)
+    )(block_pos, arrived, *pieces, key_map, phi)
     everyone = lax.all_gather(grads, "seq", axis=0, tiled=False)
-    everyone = everyone.reshape(seq_count, 3, HEAD_SIZE, HEAD_SIZE).astype(F32)
-    key_sums = (everyone[:, 1] + everyone[:, 2]).reshape(
-        key_heads, share, HEAD_SIZE, HEAD_SIZE
-    )
-    return everyone[:, 0], jnp.sum(key_sums, axis=1)
-
-
-def per_device(queries, keys, block_pos, query_map, key_map):
-    seq_count = lax.axis_size("seq")
-    share = seq_count // key_map.shape[0]
-    one_head_each = (
-        query_map.shape[0] == seq_count
-        and seq_count == share * key_map.shape[0]
-        and BLK % queries.shape[0] == 0
-        and queries.shape[0] % 32 == 0
-    )
-    chosen = per_device_head if one_head_each else per_device_general
-    return chosen(queries, keys, block_pos, query_map, key_map)
+    return pl.pallas_call(
+        collect_kernel,
+        out_shape=(
+            jax.ShapeDtypeStruct((seq_count, HEAD_SIZE, HEAD_SIZE), F32),
+            jax.ShapeDtypeStruct((key_heads, HEAD_SIZE, HEAD_SIZE), F32),
+        ),
+        in_specs=[vmem],
+        out_specs=(pl.BlockSpec(memory_space=pl.ANY),) * 2,
+        scratch_shapes=[
+            pltpu.VMEM((seq_count + key_heads, HEAD_SIZE, HEAD_SIZE), F32),
+            pltpu.SemaphoreType.DMA((seq_count + key_heads,)),
+        ],
+        compiler_params=small,
+    )(everyone)
+
+
+def one_head_each(mesh, queries, keys, block_pos, query_map, key_map):
+    del keys, block_pos
+    seq_count, head_count = mesh.shape["seq"], mesh.shape["head"]
+    rows = queries.shape[0] // (seq_count * head_count)
+    key_heads = key_map.shape[0] // head_count
+    return (
+        query_map.shape[0] == seq_count * head_count
+        and seq_count % (2 * key_heads) == 0
+        and seq_count & (seq_count - 1) == 0
+        and head_count & (head_count - 1) == 0
+        and BLK % rows == 0
+        and rows % 16 == 0
+    )
 
 
 def solution(mesh):
@@ -614,6 +651,15 @@
         P("head", None, None),
     )
     out_specs = (P("head", None, None), P("head", None, None))
-    return jax.shard_map(
-        per_device, mesh=mesh, in_specs=in_specs, out_specs=out_specs, check_vma=False
-    )
+
+    def sharded(function):
+        return jax.shard_map(
+            function, mesh=mesh, in_specs=in_specs, out_specs=out_specs, check_vma=False
+        )
+
+    def step(*args):
+        if one_head_each(mesh, *args):
+            return sharded(per_device_head)(*args)
+        return sharded(per_device_general)(*args)
+
+    return step

time: 53.9 us -> 55.9 us (1.037)
  blocking collectives: 37.2 us -> 10.4 us
  waiting for transfers between devices: 0.26 us -> 16.9 us
  starting transfers between devices: 1.63 us -> 15.3 us
  other arithmetic: 1.74 us -> 0 us
  local copies, waits for them, and re-layouts: 0.03 us -> 1.05 us
  Pallas kernels: 12.1 us -> 11.2 us
    all_to_all x1 -> x0, blocking collectives: 26.8 us -> none  [per_device_head(): lax.all_to_all(sent, ('seq', 'head'), split_axis=0, concat_axis=0, tiled=...]
    ppermute x1 -> x10, waiting for transfers between devices: 0.26 us -> 16.9 us  [swap(): return lax.ppermute(piece, axis, [(i, i ^ bits) for i in range(size)])]
    all_to_all x0 -> x1, starting transfers between devices: none -> 7.33 us  [per_device_head(): lax.all_to_all(sent, ('seq', 'head'), split_axis=0, concat_axis=0, tiled=...]
    ppermute x1 -> x10, starting transfers between devices: 1.63 us -> 8.02 us  [swap(): return lax.ppermute(piece, axis, [(i, i ^ bits) for i in range(size)])]
    unnamed x6 -> x10, local copies, waits for them, and re-layouts: 0.02 us -> 1.05 us
    add x1 -> x0, other arithmetic: 0.89 us -> none  [per_device_head(): everyone[:, 1] + everyone[:, 2]]
    pallas_call x1 -> x4, Pallas kernels: 2.7 us -> 1.85 us  [the longest x1 0.91 us: per_device_head(): pl.pallas_call(collect_kernel, out_shape=(jax.ShapeDtypeStruct((seq_count...]
    reduce_sum x1 -> x0, other arithmetic: 0.68 us -> none  [per_device_head(): return (everyone[:, 0], jnp.sum(key_sums, axis=1))]
  transfers between devices with their start and end apart: 1 -> 11, of which waited for: 1 -> 6; matrix products, arithmetic and copies ran while one was open for 0% -> 0% of each run, Pallas kernels for 2% -> 2%
where the time goes in v5:
time: 55.9 us; the launch traced here: 55.6 us
  waiting for transfers between devices  16.9 us (30%)
  starting transfers between devices  15.3 us (27%)
  Pallas kernels  11.2 us (20%)
  blocking collectives  10.4 us (19%)
  local copies, waits for them, and re-layouts  1.05 us (2%)
  between operations  0.72 us (1%)
    ppermute x10, waiting for transfers between devices, swap(): return lax.ppermute(piece, axis, [(i, i ^ bits) for i in range(size)])  16.9 us
    all_gather x1, blocking collectives, per_device_head(): everyone = lax.all_gather(grads, 'seq', axis=0, tiled=False)  10.4 us
    pallas_call x1, Pallas kernels, per_device_head(): pl.pallas_call(functools.partial(pair_kernel, token_count, seq_count, row...  8.48 us
    ppermute x10, starting transfers between devices, swap(): return lax.ppermute(piece, axis, [(i, i ^ bits) for i in range(size)])  8.02 us
    all_to_all x1, starting transfers between devices, per_device_head(): lax.all_to_all(sent, ('seq', 'head'), split_axis=0, concat_axis=0, tiled=...  7.33 us
  transfers between devices with their start and end apart: 11, of which 6 were waited for; matrix products, arithmetic and copies ran while one was open for 0% of the time, Pallas kernels for 2%

profile of v5, /device:TPU:0, one launch (start us, length us, event | category | flops | bytes accessed | tf_op | source)
XLA Modules:
  0.0 55.6 jit_solution(15353485727039871632)
XLA Ops:
  0.6 1.0 %copy-done = bf16[64,4096]{1,0:T(8,128)(2,1)S(1)} copy-done((bf16[64,4096]{1,0:T(8,128)(2,1)S(1)}, bf16[64,4096]{1,0:T(8,128)(2,1)}, u32[]{:S(2)}) %copy-start) | copy-done | bytes 524312
  1.7 0.9 %shard_map.68 = bf16[32,64,128]{2,1,0:T(8,128)(2,1)} custom-call(bf16[64,4096]{1,0:T(8,128)(2,1)S(1)} %copy-done), custom_call_target="tpu_custom_call" | custom-call | tf_op jit(solution)/shard_map/pallas_call | solution.py:559
  2.6 7.3 %all-to-all-start = ((bf16[32,64,128]{2,1,0:T(8,128)(2,1)}), bf16[32,64,128]{2,1,0:T(8,128)(2,1)S(1)}, u32[]{:S(2)}, u32[]{:S(2)}) async-start(bf16[32,64,128]{2,1,0:T(8,128)(2,1)} %shard_map.68), calls=%async_computation | async-start | bytes 1048576 | tf_op jit(solution)/shard_map/all_to_all | solution.py:566
  10.0 1.8 %collective-permute-start = (bf16[2,64,128]{2,1,0:T(8,128)(2,1)S(1)}, bf16[2,64,128]{2,1,0:T(8,128)(2,1)S(1)}, u32[]{:S(2)}, u32[]{:S(2)}) collective-permute-start(bf16[2,64,128]{2,1,0:T(8,128)(2,1)S(1)} %get-tuple-element.9), channel_id=1, source_target_pairs={{0,1},{1,0},{2,3},{3,2},{4,5},{5,4},{6,7},{7,6},{8,9},{9,8},{10,11... | collective-permute-start | bytes 98312 | tf_op jit(solution)/shard_map/ppermute | solution.py:546
  11.8 2.4 %collective-permute-start.1 = (bf16[2,64,128]{2,1,0:T(8,128)(2,1)S(1)}, bf16[2,64,128]{2,1,0:T(8,128)(2,1)S(1)}, u32[]{:S(2)}, u32[]{:S(2)}) collective-permute-start(bf16[2,64,128]{2,1,0:T(8,128)(2,1)S(1)} %get-tuple-element.10), channel_id=1, source_target_pairs={{0,2},{1,3},{2,0},{3,1},{4,6},{5,7},{6,4},{7,5},{8,10},{9,11},{10,... | collective-permute-start | bytes 98312 | tf_op jit(solution)/shard_map/ppermute | solution.py:546
  14.2 0.2 collective-permute-start.2
  14.4 5.7 %collective-permute-done.refs_1_ = bf16[2,64,128]{2,1,0:T(8,128)(2,1)S(1)} collective-permute-done((bf16[2,64,128]{2,1,0:T(8,128)(2,1)S(1)}, bf16[2,64,128]{2,1,0:T(8,128)(2,1)S(1)}, u32[]{:S(2)}, u32[]{:S(2)}) %collective-permute-start) | collective-permute-done | bytes 32800 | tf_op jit(solution)/shard_map/ppermute | solution.py:546
  20.1 7.3 %collective-permute-done.1.refs_2_ = bf16[2,64,128]{2,1,0:T(8,128)(2,1)S(1)} collective-permute-done((bf16[2,64,128]{2,1,0:T(8,128)(2,1)S(1)}, bf16[2,64,128]{2,1,0:T(8,128)(2,1)S(1)}, u32[]{:S(2)}, u32[]{:S(2)}) %collective-permute-start.1) | collective-permute-done | bytes 32800 | tf_op jit(solution)/shard_map/ppermute | solution.py:546
  27.3 0.0 collective-permute-done.2.refs_3_
  27.3 2.5 %collective-permute-start.8 = (bf16[4,64,128]{2,1,0:T(8,128)(2,1)S(1)}, bf16[4,64,128]{2,1,0:T(8,128)(2,1)S(1)}, u32[]{:S(2)}, u32[]{:S(2)}) collective-permute-start(bf16[4,64,128]{2,1,0:T(8,128)(2,1)S(1)} %get-tuple-element.13), channel_id=1, source_target_pairs={{0,24},{4,28},{8,16},{12,20},{16,8},{20,12},{24,0},{28,4},{1,25},{... | collective-permute-start | bytes 196616 | tf_op jit(solution)/shard_map/ppermute | solution.py:546
  29.8 0.5 collective-permute-start.6
  30.3 0.6 %collective-permute-start.4 = (bf16[4,64,128]{2,1,0:T(8,128)(2,1)S(1)}, bf16[4,64,128]{2,1,0:T(8,128)(2,1)S(1)}, u32[]{:S(2)}, u32[]{:S(2)}) collective-permute-start(bf16[4,64,128]{2,1,0:T(8,128)(2,1)S(1)} %get-tuple-element.12.refs_0_), channel_id=1, source_target_pairs={{0,8},{4,12},{8,0},{12,4},{16,24},{20,28},{24,16},{28,20},{1,9},{5... | collective-permute-start | bytes 196616 | tf_op jit(solution)/shard_map/ppermute | solution.py:546
  30.9 2.0 %collective-permute-done.8.refs_6_ = bf16[4,64,128]{2,1,0:T(8,128)(2,1)S(1)} collective-permute-done((bf16[4,64,128]{2,1,0:T(8,128)(2,1)S(1)}, bf16[4,64,128]{2,1,0:T(8,128)(2,1)S(1)}, u32[]{:S(2)}, u32[]{:S(2)}) %collective-permute-start.8) | collective-permute-done | bytes 65568 | tf_op jit(solution)/shard_map/ppermute | solution.py:546
  32.9 0.0 collective-permute-start.9
  32.9 1.1 %collective-permute-done.6.refs_4_ = bf16[4,64,128]{2,1,0:T(8,128)(2,1)S(1)} collective-permute-done((bf16[4,64,128]{2,1,0:T(8,128)(2,1)S(1)}, bf16[4,64,128]{2,1,0:T(8,128)(2,1)S(1)}, u32[]{:S(2)}, u32[]{:S(2)}) %collective-permute-start.6) | collective-permute-done | bytes 65568 | tf_op jit(solution)/shard_map/ppermute | solution.py:546
  34.1 0.0 collective-permute-start.7
  34.1 0.5 collective-permute-done.4.refs_2_
  34.6 0.0 collective-permute-start.5
  34.6 0.0 all-to-all-done.arrived_ref
  34.6 0.9 %shard_map.71.refs_9_ = f32[16,256,128]{2,1,0:T(8,128)S(1)} custom-call(bf16[32,64,128]{2,1,0:T(8,128)(2,1)S(1)} %all-to-all-done.arrived_ref, f32[8,128,128]{2,1,0:T(8,128)S(1)} %copy-done.1), custom_call_target="tpu_custom_call" | custom-call | flops 201326592 | bytes 5242880 | tf_op jit(solution)/shard_map/pallas_call | solution.py:580
  35.5 0.3 collective-permute-done.5.refs_3_
  35.9 8.5 %shard_map.72 = bf16[384,128]{1,0:T(8,128)(2,1)S(1)} custom-call(s32[16]{0:T(128)S(1)} %copy-done.4, bf16[32,64,128]{2,1,0:T(8,128)(2,1)S(1)} %all-to-all-done.arrived_ref, bf16[4,64,128]{2,1,0:T(8,128)(2,1)S(1)} %get-tuple-element.12.refs_0_, bf16[4,64,128]{2,1,0:T(8,128)(2,1)S(1)} %collective-permute-done.3.refs_1_, ...), custom_call_target="tpu_custom_call" | custom-call | tf_op jit(solution)/shard_map/pallas_call | solution.py:592
  44.4 10.4 %all-gather = bf16[3072,128]{1,0:T(8,128)(2,1)S(1)} all-gather(bf16[384,128]{1,0:T(8,128)(2,1)S(1)} %shard_map.72), channel_id=2, replica_groups=mesh['seq'=8,'head'=4] {'seq'}, dimensions={0}, use_global_device_ids=true | all-gather | bytes 884736 | tf_op jit(solution)/shard_map/all_gather | solution.py:613
  54.7 0.9 %shard_map.73 = (f32[8,128,128]{2,1,0:T(8,128)}, f32[2,128,128]{2,1,0:T(8,128)}) custom-call(bf16[8,384,128]{2,1,0:T(8,128)(2,1)S(1)} %bitcast.1), custom_call_target="tpu_custom_call" | custom-call | tf_op jit(solution)/shard_map/pallas_call | solution.py:614
  (15 shorter events, 0.1 us)
Async XLA Ops:
  0.6 1.0 %copy-start = (bf16[64,4096]{1,0:T(8,128)(2,1)S(1)}, bf16[64,4096]{1,0:T(8,128)(2,1)}, u32[]{:S(2)}) copy-start(bf16[64,4096]{1,0:T(8,128)(2,1)} %queries_ref.1) | copy-start | bytes 1572868
  1.7 8.2 %copy-start.3 = (bf16[64,1024]{1,0:T(8,128)(2,1)S(1)}, bf16[64,1024]{1,0:T(8,128)(2,1)}, u32[]{:S(2)}) copy-start(bf16[64,1024]{1,0:T(8,128)(2,1)} %keys_ref.1) | copy-start | bytes 393220
  1.7 32.9 %copy-start.1 = (f32[8,128,128]{2,1,0:T(8,128)S(1)}, f32[8,128,128]{2,1,0:T(8,128)}, u32[]{:S(2)}) copy-start(f32[8,128,128]{2,1,0:T(8,128)} %query_map_ref.1) | copy-start | bytes 1572868
  2.6 33.3 %copy-start.2 = (f32[2,128,128]{2,1,0:T(8,128)S(1)}, f32[2,128,128]{2,1,0:T(8,128)}, u32[]{:S(2)}) copy-start(f32[2,128,128]{2,1,0:T(8,128)} %refs_8_.1) | copy-start | bytes 393220
  2.6 33.3 %copy-start.4 = (s32[16]{0:T(128)S(1)}, s32[16]{0:T(128)}, u32[]{:S(2)}) copy-start(s32[16]{0:T(128)} %pos_ref.1) | copy-start | bytes 196
  2.6 32.0 %all-to-all-start = ((bf16[32,64,128]{2,1,0:T(8,128)(2,1)}), bf16[32,64,128]{2,1,0:T(8,128)(2,1)S(1)}, u32[]{:S(2)}, u32[]{:S(2)}) async-start(bf16[32,64,128]{2,1,0:T(8,128)(2,1)} %shard_map.68), calls=%async_computation | async-start | bytes 1048576 | tf_op jit(solution)/shard_map/all_to_all | solution.py:566
  10.0 10.1 %collective-permute-start = (bf16[2,64,128]{2,1,0:T(8,128)(2,1)S(1)}, bf16[2,64,128]{2,1,0:T(8,128)(2,1)S(1)}, u32[]{:S(2)}, u32[]{:S(2)}) collective-permute-start(bf16[2,64,128]{2,1,0:T(8,128)(2,1)S(1)} %get-tuple-element.9), channel_id=1, source_target_pairs={{0,1},{1,0},{2,3},{3,2},{4,5},{5,4},{6,7},{7,6},{8,9},{9,8},{10,11... | collective-permute-start | bytes 98312 | tf_op jit(solution)/shard_map/ppermute | solution.py:546
  11.8 15.5 %collective-permute-start.1 = (bf16[2,64,128]{2,1,0:T(8,128)(2,1)S(1)}, bf16[2,64,128]{2,1,0:T(8,128)(2,1)S(1)}, u32[]{:S(2)}, u32[]{:S(2)}) collective-permute-start(bf16[2,64,128]{2,1,0:T(8,128)(2,1)S(1)} %get-tuple-element.10), channel_id=1, source_target_pairs={{0,2},{1,3},{2,0},{3,1},{4,6},{5,7},{6,4},{7,5},{8,10},{9,11},{10,... | collective-permute-start | bytes 98312 | tf_op jit(solution)/shard_map/ppermute | solution.py:546
  14.2 13.1 %collective-permute-start.2 = (bf16[2,64,128]{2,1,0:T(8,128)(2,1)S(1)}, bf16[2,64,128]{2,1,0:T(8,128)(2,1)S(1)}, u32[]{:S(2)}, u32[]{:S(2)}) collective-permute-start(bf16[2,64,128]{2,1,0:T(8,128)(2,1)S(1)} %get-tuple-element.11), channel_id=1, source_target_pairs={{0,3},{1,2},{2,1},{3,0},{4,7},{5,6},{6,5},{7,4},{8,11},{9,10},{10,... | collective-permute-start | bytes 98312 | tf_op jit(solution)/shard_map/ppermute | solution.py:546
  27.3 5.6 %collective-permute-start.8 = (bf16[4,64,128]{2,1,0:T(8,128)(2,1)S(1)}, bf16[4,64,128]{2,1,0:T(8,128)(2,1)S(1)}, u32[]{:S(2)}, u32[]{:S(2)}) collective-permute-start(bf16[4,64,128]{2,1,0:T(8,128)(2,1)S(1)} %get-tuple-element.13), channel_id=1, source_target_pairs={{0,24},{4,28},{8,16},{12,20},{16,8},{20,12},{24,0},{28,4},{1,25},{... | collective-permute-start | bytes 196616 | tf_op jit(solution)/shard_map/ppermute | solution.py:546
  29.8 4.3 %collective-permute-start.6 = (bf16[4,64,128]{2,1,0:T(8,128)(2,1)S(1)}, bf16[4,64,128]{2,1,0:T(8,128)(2,1)S(1)}, u32[]{:S(2)}, u32[]{:S(2)}) collective-permute-start(bf16[4,64,128]{2,1,0:T(8,128)(2,1)S(1)} %get-tuple-element.13), channel_id=1, source_target_pairs={{0,16},{4,20},{8,24},{12,28},{16,0},{20,4},{24,8},{28,12},{1,17},{... | collective-permute-start | bytes 196616 | tf_op jit(solution)/shard_map/ppermute | solution.py:546
  30.3 4.3 %collective-permute-start.4 = (bf16[4,64,128]{2,1,0:T(8,128)(2,1)S(1)}, bf16[4,64,128]{2,1,0:T(8,128)(2,1)S(1)}, u32[]{:S(2)}, u32[]{:S(2)}) collective-permute-start(bf16[4,64,128]{2,1,0:T(8,128)(2,1)S(1)} %get-tuple-element.12.refs_0_), channel_id=1, source_target_pairs={{0,8},{4,12},{8,0},{12,4},{16,24},{20,28},{24,16},{28,20},{1,9},{5... | collective-permute-start | bytes 196616 | tf_op jit(solution)/shard_map/ppermute | solution.py:546
  30.9 4.6 %collective-permute-start.3 = (bf16[4,64,128]{2,1,0:T(8,128)(2,1)S(1)}, bf16[4,64,128]{2,1,0:T(8,128)(2,1)S(1)}, u32[]{:S(2)}, u32[]{:S(2)}) collective-permute-start(bf16[4,64,128]{2,1,0:T(8,128)(2,1)S(1)} %get-tuple-element.12.refs_0_), channel_id=1, source_target_pairs={{0,4},{4,0},{8,12},{12,8},{16,20},{20,16},{24,28},{28,24},{1,5},{5... | collective-permute-start | bytes 196616 | tf_op jit(solution)/shard_map/ppermute | solution.py:546
  32.9 2.6 %collective-permute-start.9 = (bf16[4,64,128]{2,1,0:T(8,128)(2,1)S(1)}, bf16[4,64,128]{2,1,0:T(8,128)(2,1)S(1)}, u32[]{:S(2)}, u32[]{:S(2)}) collective-permute-start(bf16[4,64,128]{2,1,0:T(8,128)(2,1)S(1)} %collective-permute-done.8.refs_6_), channel_id=1, source_target_pairs={{0,4},{4,0},{8,12},{12,8},{16,20},{20,16},{24,28},{28,24},{1,5},{5... | collective-permute-start | bytes 196616 | tf_op jit(solution)/shard_map/ppermute | solution.py:546
  34.1 1.5 %collective-permute-start.7 = (bf16[4,64,128]{2,1,0:T(8,128)(2,1)S(1)}, bf16[4,64,128]{2,1,0:T(8,128)(2,1)S(1)}, u32[]{:S(2)}, u32[]{:S(2)}) collective-permute-start(bf16[4,64,128]{2,1,0:T(8,128)(2,1)S(1)} %collective-permute-done.6.refs_4_), channel_id=1, source_target_pairs={{0,4},{4,0},{8,12},{12,8},{16,20},{20,16},{24,28},{28,24},{1,5},{5... | collective-permute-start | bytes 196616 | tf_op jit(solution)/shard_map/ppermute | solution.py:546
  34.6 1.3 %collective-permute-start.5 = (bf16[4,64,128]{2,1,0:T(8,128)(2,1)S(1)}, bf16[4,64,128]{2,1,0:T(8,128)(2,1)S(1)}, u32[]{:S(2)}, u32[]{:S(2)}) collective-permute-start(bf16[4,64,128]{2,1,0:T(8,128)(2,1)S(1)} %collective-permute-done.4.refs_2_), channel_id=1, source_target_pairs={{0,4},{4,0},{8,12},{12,8},{16,20},{20,16},{24,28},{28,24},{1,5},{5... | collective-permute-start | bytes 196616 | tf_op jit(solution)/shard_map/ppermute | solution.py:546

commit v6 on v5

--- a/solution.py
+++ b/solution.py
@@ -268,56 +268,64 @@
             out_ref[number] = in_ref[mine ^ other]
 
 
-def query_kernel(rows, arrived_ref, query_map_ref, phi_ref):
+def sorted_rows(pos_ref, chunk, rows):
     per_block = BLK // rows
-    parts = map_parts(query_map_ref[lax.axis_index("seq")])
-
-    def block_logits(number):
-        tokens = arrived_ref[number * per_block : (number + 1) * per_block]
-        return logits_t(parts, tokens.reshape(BLK, HEAD_SIZE))
-
-    blocks = phi_ref.shape[0]
-    ahead = block_logits(0)
+    first = pos_ref[lax.div(chunk, per_block)] * BLK + lax.rem(chunk, per_block) * rows
+    return pl.ds(pl.multiple_of(first, rows), rows)
+
+
+def block(at):
+    return slice(at * BLK, (at + 1) * BLK)
+
+
+def key_kernel(share, pos_ref, key_map_ref, query_map_ref, *refs):
+    seq_count, head_count = lax.axis_size("seq"), lax.axis_size("head")
+    piece_refs, refs = refs[:seq_count], refs[seq_count:]
+    key_rows, phi, query_weights_ref, key_weights_ref = refs
+    rows = piece_refs[0].shape[1]
+    seq_blocks = phi.shape[2] // BLK
+    blocks = phi.shape[0] * seq_blocks
+    mine, plane = lax.axis_index("seq"), lax.axis_index("head")
+    query_weights_ref[...] = query_map_ref[mine]
+    for other in range(seq_count):
+        for number in range(head_count):
+            chunk = (mine ^ other) * head_count + (plane ^ number)
+            key_rows[sorted_rows(pos_ref, chunk, rows), :] = piece_refs[other][number]
+    key_weights_ref[...] = key_map_ref[lax.div(mine, share)]
+    parts = map_parts(key_weights_ref[...])
+    ahead = []
     for number in range(blocks):
-        logits = ahead
-        if number + 1 < blocks:
-            ahead = block_logits(number + 1)
-        phi_ref[number] = features_t(logits)
+        while number + len(ahead) < min(number + 3, blocks):
+            ahead.append(logits_t(parts, key_rows[block(number + len(ahead)), :]))
+        seq, at = divmod(number, seq_blocks)
+        phi[seq, :, block(at)] = features_t(ahead.pop(0))
 
 
 def pair_kernel(
     token_count,
     seq_blocks,
-    rows,
-    share,
     pos_ref,
     arrived_ref,
-    *refs,
+    query_weights_ref,
+    key_weights_ref,
+    key_rows,
+    phi_k_early,
+    out_ref,
+    query_rows,
+    phi_q,
+    phi_qb,
+    phi_k_late,
+    phi_kb,
+    phi_kb_rows,
+    pair_weights,
+    scores,
+    linears,
+    acc_q,
+    acc_k,
 ):
-    seq_count, head_count = lax.axis_size("seq"), lax.axis_size("head")
-    key_refs, refs = refs[:seq_count], refs[seq_count:]
-    (
-        key_map_ref,
-        phi_q,
-        out_ref,
-        stored,
-        key_rows,
-        query_rows,
-        phi_qb,
-        phi_k,
-        phi_kb,
-        phi_kb_rows,
-        pair_weights,
-        scores,
-        linears,
-        acc_q,
-        acc_k,
-    ) = refs
-    per_block = BLK // rows
+    rows = arrived_ref.shape[1]
     seq_tokens = seq_blocks * BLK
-    sequences = token_count // (seq_blocks * BLK)
-    for number in range(token_count // BLK):
-        stored[pos_ref[number]] = number
+    sequences = token_count // seq_tokens
     acc_q[...] = jnp.zeros_like(acc_q)
     acc_k[...] = jnp.zeros_like(acc_k)
     width = 2 if seq_blocks % 2 == 0 else 1
@@ -325,46 +333,48 @@
     for seq in range(sequences):
         for at in range(0, seq_blocks, width):
             if width > 1:
-                pair_weights[seq, (at + 1) * BLK : (at + 2) * BLK, at * BLK : (at + 1) * BLK] = (
-                    jnp.zeros((BLK, BLK), BF16)
-                )
-    mine, plane = lax.axis_index("seq"), lax.axis_index("head")
-    parts = map_parts(key_map_ref[lax.div(mine, share)])
+                pair_weights[seq, block(at + 1), block(at)] = jnp.zeros((BLK, BLK), BF16)
+    parts = map_parts(query_weights_ref[...])
+    key_parts = map_parts(key_weights_ref[...])
+    early = phi_k_early.shape[0]
     lane = lax.broadcasted_iota(jnp.int32, (BLK, BLK), 1)
     sublane = lax.broadcasted_iota(jnp.int32, (BLK, BLK), 0)
     unit = jnp.where(lane == sublane, 1.0, 0.0).astype(BF16)
     visible = sublane <= lane
     exponent_scale = HEAD_SIZE ** (-0.5) * math.log2(math.e)
 
-    def block(at):
-        return slice(at * BLK, (at + 1) * BLK)
-
     def span(tile):
         return slice(tile * width * BLK, (tile + 1) * width * BLK)
 
-    def place(seq, at):
-        return stored[seq * seq_blocks + at]
-
     def flat(seq, here):
         return slice(seq * seq_tokens + here.start, seq * seq_tokens + here.stop)
 
-    def sorted_rows(chunk):
-        first = pos_ref[lax.div(chunk, per_block)] * BLK + lax.rem(chunk, per_block) * rows
-        return pl.ds(pl.multiple_of(first, rows), rows)
-
-    def load_features(seq, at):
-        phi_qb[seq, :, block(at)] = phi_q[place(seq, at)].astype(BF16)
+    def query_logits(seq, at):
+        return logits_t(parts, query_rows[flat(seq, block(at)), :])
+
+    def query_features(seq, at, logits):
+        feature = features_t(logits)
+        phi_q[seq, :, block(at)] = feature
+        phi_qb[seq, :, block(at)] = feature.astype(BF16)
+
+    def phi_k(seq, at):
+        if seq < early:
+            return phi_k_early[seq, :, block(at)]
+        return phi_k_late[seq - early, :, block(at)]
 
     def key_logits(seq, at):
-        return logits_t(parts, key_rows[flat(seq, block(at)), :])
+        if seq < early:
+            return None
+        return logits_t(key_parts, key_rows[flat(seq, block(at)), :])
 
     def key_features(seq, at, logits):
-        feature = features_t(logits)
-        phi_k[seq, :, block(at)] = feature
-        phi_kb[seq, :, block(at)] = feature.astype(BF16)
+        if seq >= early:
+            phi_k_late[seq - early, :, block(at)] = features_t(logits)
 
     def turn_features(seq, at):
-        phi_kb_rows[seq, block(at), :] = nt(unit, phi_kb[seq, :, block(at)]).astype(BF16)
+        rounded = phi_k(seq, at).astype(BF16)
+        phi_kb[seq, :, block(at)] = rounded
+        phi_kb_rows[seq, block(at), :] = nt(unit, rounded).astype(BF16)
 
     def pair_scores(seq, tile):
         here = span(tile)
@@ -428,7 +438,7 @@
         return nn(phi_kb[seq, :, : here.stop], pair_weights[seq, : here.stop, here])
 
     def query_change(seq, tile, upstream):
-        phis = [phi_q[place(seq, tile * width + half)] for half in range(width)]
+        phis = [phi_q[seq, :, block(tile * width + half)] for half in range(width)]
         acc_q[...] += map_change(phis, upstream, query_rows[flat(seq, span(tile)), :])
 
     def key_upstream(seq, tile):
@@ -436,7 +446,7 @@
         return nt(phi_qb[seq, :, later], pair_weights[seq, span(tile), later])
 
     def key_change(seq, tile, upstream):
-        phis = [phi_k[seq, :, block(tile * width + half)] for half in range(width)]
+        phis = [phi_k(seq, tile * width + half) for half in range(width)]
         acc_k[...] += map_change(phis, upstream, key_rows[flat(seq, span(tile)), :])
 
     def feature_steps(seq):
@@ -450,6 +460,20 @@
             yield
         for at in range(max(seq_blocks - 2, 0), seq_blocks):
             turn_features(seq, at)
+
+    def feature_steps(seq):
+        ahead = []
+        for at in range(seq_blocks):
+            while at + len(ahead) < min(at + 3, seq_blocks):
+                later = at + len(ahead)
+                ahead.append((key_logits(seq, later), query_logits(seq, later)))
+            from_keys, from_queries = ahead.pop(0)
+            key_features(seq, at, from_keys)
+            query_features(seq, at, from_queries)
+            if at:
+                turn_features(seq, at - 1)
+            yield
+        turn_features(seq, seq_blocks - 1)
 
     def pair_steps(seq):
         ahead = pair_scores(seq, 0)
@@ -478,15 +502,8 @@
             key_change(seq, tile, upstream)
             yield
 
-    for other in range(seq_count):
-        for number in range(head_count):
-            chunk = (mine ^ other) * head_count + (plane ^ number)
-            key_rows[sorted_rows(chunk), :] = key_refs[other][number]
     for chunk in range(token_count // rows):
-        query_rows[sorted_rows(chunk), :] = arrived_ref[chunk]
-    for seq in range(sequences):
-        for at in range(seq_blocks):
-            load_features(seq, at)
+        query_rows[sorted_rows(pos_ref, chunk, rows), :] = arrived_ref[chunk]
     stages = (feature_steps, pair_steps, key_steps)
     for turn in range(sequences + len(stages) - 1):
         active = [
@@ -535,7 +552,6 @@
     rows = queries.shape[0]
     devices = seq_count * head_count
     token_count = rows * devices
-    blocks = token_count // BLK
     seq_tokens = seq_count * BLK
     sequences = token_count // seq_tokens
     vmem = pl.BlockSpec(memory_space=pltpu.VMEM)
@@ -577,29 +593,35 @@
         pieces[other] = swap(piece, "seq", other) if other else piece
     for other in range(0, seq_count, 2):
         pieces[other + 1] = swap(pieces[other], "seq", 1)
-    phi = pl.pallas_call(
-        functools.partial(query_kernel, rows),
-        out_shape=jax.ShapeDtypeStruct((blocks, 2 * HEAD_SIZE, BLK), F32),
-        in_specs=[vmem, vmem],
-        out_specs=vmem,
-        compiler_params=pltpu.CompilerParams(vmem_limit_bytes=16 << 20),
+    early = max(sequences // 2, 1)
+    weights_shape = jax.ShapeDtypeStruct((HEAD_SIZE, HEAD_SIZE), F32)
+    key_rows, phi_k, query_weights, key_weights = pl.pallas_call(
+        functools.partial(key_kernel, share),
+        out_shape=(
+            jax.ShapeDtypeStruct((token_count, HEAD_SIZE), BF16),
+            jax.ShapeDtypeStruct((early, 2 * HEAD_SIZE, seq_tokens), F32),
+            weights_shape,
+            weights_shape,
+        ),
+        in_specs=[smem] + [vmem] * (seq_count + 2),
+        out_specs=(vmem,) * 4,
+        compiler_params=pltpu.CompilerParams(vmem_limit_bytes=8 << 20),
         cost_estimate=pl.CostEstimate(
             flops=token_count * HEAD_SIZE * HEAD_SIZE * 6,
-            bytes_accessed=token_count * HEAD_SIZE * 20,
+            bytes_accessed=token_count * HEAD_SIZE * 12,
             transcendentals=token_count * HEAD_SIZE * 2,
         ),
-    )(arrived, query_map)
+    )(block_pos, key_map, query_map, *pieces)
     grads = pl.pallas_call(
-        functools.partial(pair_kernel, token_count, seq_count, rows, share),
+        functools.partial(pair_kernel, token_count, seq_count),
         out_shape=jax.ShapeDtypeStruct((3 * HEAD_SIZE, HEAD_SIZE), BF16),
-        in_specs=[smem] + [vmem] * (seq_count + 3),
+        in_specs=[smem] + [vmem] * 5,
         out_specs=vmem,
         scratch_shapes=[
-            pltpu.SMEM((blocks,), jnp.int32),
             pltpu.VMEM((token_count, HEAD_SIZE), BF16),
-            pltpu.VMEM((token_count, HEAD_SIZE), BF16),
+            pltpu.VMEM((sequences, 2 * HEAD_SIZE, seq_tokens), F32),
             pltpu.VMEM((sequences, 2 * HEAD_SIZE, seq_tokens), BF16),
-            pltpu.VMEM((sequences, 2 * HEAD_SIZE, seq_tokens), F32),
+            pltpu.VMEM((max(sequences - early, 1), 2 * HEAD_SIZE, seq_tokens), F32),
             pltpu.VMEM((sequences, 2 * HEAD_SIZE, seq_tokens), BF16),
             pltpu.VMEM((sequences, seq_tokens, 2 * HEAD_SIZE), BF16),
             pltpu.VMEM((sequences, seq_tokens, seq_tokens), BF16),
@@ -609,7 +631,7 @@
             pltpu.VMEM((HEAD_SIZE, HEAD_SIZE), F32),
         ],
         compiler_params=pltpu.CompilerParams(vmem_limit_bytes=32 << 20),
-    )(block_pos, arrived, *pieces, key_map, phi)
+    )(block_pos, arrived, query_weights, key_weights, key_rows, phi_k)
     everyone = lax.all_gather(grads, "seq", axis=0, tiled=False)
     return pl.pallas_call(
         collect_kernel,

time: 55.9 us -> 57 us (1.020)
  waiting for transfers between devices: 16.9 us -> 17.8 us
    ppermute x10, waiting for transfers between devices: 16.9 us -> 17.8 us  [swap(): return lax.ppermute(piece, axis, [(i, i ^ bits) for i in range(size)])]
  transfers between devices with their start and end apart: 11 -> 11, of which waited for: 6 -> 7; matrix products, arithmetic and copies ran while one was open for 0% -> 0% of each run, Pallas kernels for 2% -> 2%
where the time goes in v6:
time: 57 us; the launch traced here: 56.8 us
  waiting for transfers between devices  17.8 us (31%)
  starting transfers between devices  15.3 us (27%)
  Pallas kernels  11.4 us (20%)
  blocking collectives  10.4 us (18%)
  local copies, waits for them, and re-layouts  1.05 us (2%)
  between operations  0.72 us (1%)
    ppermute x10, waiting for transfers between devices, swap(): return lax.ppermute(piece, axis, [(i, i ^ bits) for i in range(size)])  17.8 us
    all_gather x1, blocking collectives, per_device_head(): everyone = lax.all_gather(grads, 'seq', axis=0, tiled=False)  10.4 us
    pallas_call x1, Pallas kernels, per_device_head(): pl.pallas_call(functools.partial(pair_kernel, token_count, seq_count), ou...  8.3 us
    ppermute x10, starting transfers between devices, swap(): return lax.ppermute(piece, axis, [(i, i ^ bits) for i in range(size)])  8.02 us
    all_to_all x1, starting transfers between devices, per_device_head(): lax.all_to_all(sent, ('seq', 'head'), split_axis=0, concat_axis=0, tiled=...  7.33 us
    pallas_call x1, Pallas kernels, per_device_head(): pl.pallas_call(functools.partial(key_kernel, share), out_shape=(jax.Shape...  1.28 us
  transfers between devices with their start and end apart: 11, of which 7 were waited for; matrix products, arithmetic and copies ran while one was open for 0% of the time, Pallas kernels for 2%

profile of v6, /device:TPU:0, one launch (start us, length us, event | category | flops | bytes accessed | tf_op | source)
XLA Modules:
  0.0 56.8 jit_solution(14880200937151585593)
XLA Ops:
  0.6 1.0 %copy-done = bf16[64,4096]{1,0:T(8,128)(2,1)S(1)} copy-done((bf16[64,4096]{1,0:T(8,128)(2,1)S(1)}, bf16[64,4096]{1,0:T(8,128)(2,1)}, u32[]{:S(2)}) %copy-start) | copy-done | bytes 524312
  1.7 0.9 %shard_map.68 = bf16[32,64,128]{2,1,0:T(8,128)(2,1)} custom-call(bf16[64,4096]{1,0:T(8,128)(2,1)S(1)} %copy-done), custom_call_target="tpu_custom_call" | custom-call | tf_op jit(solution)/shard_map/pallas_call | solution.py:575
  2.6 7.3 %all-to-all-start = ((bf16[32,64,128]{2,1,0:T(8,128)(2,1)}), bf16[32,64,128]{2,1,0:T(8,128)(2,1)S(1)}, u32[]{:S(2)}, u32[]{:S(2)}) async-start(bf16[32,64,128]{2,1,0:T(8,128)(2,1)} %shard_map.68), calls=%async_computation | async-start | bytes 1048576 | tf_op jit(solution)/shard_map/all_to_all | solution.py:582
  9.9 0.0 copy-start.2
  10.0 1.8 %collective-permute-start = (bf16[2,64,128]{2,1,0:T(8,128)(2,1)S(1)}, bf16[2,64,128]{2,1,0:T(8,128)(2,1)S(1)}, u32[]{:S(2)}, u32[]{:S(2)}) collective-permute-start(bf16[2,64,128]{2,1,0:T(8,128)(2,1)S(1)} %get-tuple-element.13), channel_id=1, source_target_pairs={{0,1},{1,0},{2,3},{3,2},{4,5},{5,4},{6,7},{7,6},{8,9},{9,8},{10,11... | collective-permute-start | bytes 98312 | tf_op jit(solution)/shard_map/ppermute | solution.py:562
  11.8 2.4 %collective-permute-start.1 = (bf16[2,64,128]{2,1,0:T(8,128)(2,1)S(1)}, bf16[2,64,128]{2,1,0:T(8,128)(2,1)S(1)}, u32[]{:S(2)}, u32[]{:S(2)}) collective-permute-start(bf16[2,64,128]{2,1,0:T(8,128)(2,1)S(1)} %get-tuple-element.14), channel_id=1, source_target_pairs={{0,2},{1,3},{2,0},{3,1},{4,6},{5,7},{6,4},{7,5},{8,10},{9,11},{10,... | collective-permute-start | bytes 98312 | tf_op jit(solution)/shard_map/ppermute | solution.py:562
  14.2 0.2 collective-permute-start.2
  14.4 5.6 %collective-permute-done.refs_1_ = bf16[2,64,128]{2,1,0:T(8,128)(2,1)S(1)} collective-permute-done((bf16[2,64,128]{2,1,0:T(8,128)(2,1)S(1)}, bf16[2,64,128]{2,1,0:T(8,128)(2,1)S(1)}, u32[]{:S(2)}, u32[]{:S(2)}) %collective-permute-start) | collective-permute-done | bytes 32800 | tf_op jit(solution)/shard_map/ppermute | solution.py:562
  20.1 7.3 %collective-permute-done.1.refs_2_ = bf16[2,64,128]{2,1,0:T(8,128)(2,1)S(1)} collective-permute-done((bf16[2,64,128]{2,1,0:T(8,128)(2,1)S(1)}, bf16[2,64,128]{2,1,0:T(8,128)(2,1)S(1)}, u32[]{:S(2)}, u32[]{:S(2)}) %collective-permute-start.1) | collective-permute-done | bytes 32800 | tf_op jit(solution)/shard_map/ppermute | solution.py:562
  27.3 0.0 copy-start.4
  27.3 2.5 %collective-permute-start.8 = (bf16[4,64,128]{2,1,0:T(8,128)(2,1)S(1)}, bf16[4,64,128]{2,1,0:T(8,128)(2,1)S(1)}, u32[]{:S(2)}, u32[]{:S(2)}) collective-permute-start(bf16[4,64,128]{2,1,0:T(8,128)(2,1)S(1)} %get-tuple-element.17), channel_id=1, source_target_pairs={{0,24},{4,28},{8,16},{12,20},{16,8},{20,12},{24,0},{28,4},{1,25},{... | collective-permute-start | bytes 196616 | tf_op jit(solution)/shard_map/ppermute | solution.py:562
  29.8 0.5 collective-permute-start.6
  30.3 0.6 collective-permute-start.4
  30.9 2.0 %collective-permute-done.8.refs_6_ = bf16[4,64,128]{2,1,0:T(8,128)(2,1)S(1)} collective-permute-done((bf16[4,64,128]{2,1,0:T(8,128)(2,1)S(1)}, bf16[4,64,128]{2,1,0:T(8,128)(2,1)S(1)}, u32[]{:S(2)}, u32[]{:S(2)}) %collective-permute-start.8) | collective-permute-done | bytes 65568 | tf_op jit(solution)/shard_map/ppermute | solution.py:562
  32.9 0.0 collective-permute-start.9
  33.0 1.1 %collective-permute-done.6.refs_4_ = bf16[4,64,128]{2,1,0:T(8,128)(2,1)S(1)} collective-permute-done((bf16[4,64,128]{2,1,0:T(8,128)(2,1)S(1)}, bf16[4,64,128]{2,1,0:T(8,128)(2,1)S(1)}, u32[]{:S(2)}, u32[]{:S(2)}) %collective-permute-start.6) | collective-permute-done | bytes 65568 | tf_op jit(solution)/shard_map/ppermute | solution.py:562
  34.1 0.0 collective-permute-start.7
  34.1 0.5 collective-permute-done.4.refs_2_
  34.6 0.7 %collective-permute-done.7.refs_5_ = bf16[4,64,128]{2,1,0:T(8,128)(2,1)S(1)} collective-permute-done((bf16[4,64,128]{2,1,0:T(8,128)(2,1)S(1)}, bf16[4,64,128]{2,1,0:T(8,128)(2,1)S(1)}, u32[]{:S(2)}, u32[]{:S(2)}) %collective-permute-start.7) | collective-permute-done | bytes 65568 | tf_op jit(solution)/shard_map/ppermute | solution.py:562
  35.3 0.5 collective-permute-done.5.refs_3_
  35.9 1.3 %shard_map.71 = (bf16[2048,128]{1,0:T(8,128)(2,1)S(1)}, f32[1,256,1024]{2,1,0:T(8,128)S(1)}, f32[128,128]{1,0:T(8,128)S(1)}, f32[128,128]{1,0:T(8,128)S(1)}) custom-call(s32[16]{0:T(128)S(1)} %copy-done.4, f32[2,128,128]{2,1,0:T(8,128)S(1)} %copy-done.2, f32[8,128,128]{2,1,0:T(8,128)S(1)} %copy-done.1, bf16[4,64,128]{2,1,0:T(8,128)(2,1)S(1)} %get-tuple-element.16.refs_0_, ...), custom_call_target="tpu_custom_call" | custom-call | flops 201326592 | bytes 3145728 | tf_op jit(solution)/shard_map/pallas_call | solution.py:598
  37.2 8.3 %shard_map.72 = bf16[384,128]{1,0:T(8,128)(2,1)S(1)} custom-call(s32[16]{0:T(128)S(1)} %copy-done.4, bf16[32,64,128]{2,1,0:T(8,128)(2,1)S(1)} %all-to-all-done.arrived_ref, f32[128,128]{1,0:T(8,128)S(1)} %get-tuple-element.18.query_weights_ref, f32[128,128]{1,0:T(8,128)S(1)} %get-tuple-element.19.key_weights_ref, ...), custom_call_target="tpu_custom_call" | custom-call | tf_op jit(solution)/shard_map/pallas_call | solution.py:615
  45.5 10.4 %all-gather = bf16[3072,128]{1,0:T(8,128)(2,1)S(1)} all-gather(bf16[384,128]{1,0:T(8,128)(2,1)S(1)} %shard_map.72), channel_id=2, replica_groups=mesh['seq'=8,'head'=4] {'seq'}, dimensions={0}, use_global_device_ids=true | all-gather | bytes 884736 | tf_op jit(solution)/shard_map/all_gather | solution.py:635
  55.9 0.9 %shard_map.73 = (f32[8,128,128]{2,1,0:T(8,128)}, f32[2,128,128]{2,1,0:T(8,128)}) custom-call(bf16[8,384,128]{2,1,0:T(8,128)(2,1)S(1)} %bitcast.1), custom_call_target="tpu_custom_call" | custom-call | tf_op jit(solution)/shard_map/pallas_call | solution.py:636
  (15 shorter events, 0.1 us)
Async XLA Ops:
  0.6 1.0 %copy-start = (bf16[64,4096]{1,0:T(8,128)(2,1)S(1)}, bf16[64,4096]{1,0:T(8,128)(2,1)}, u32[]{:S(2)}) copy-start(bf16[64,4096]{1,0:T(8,128)(2,1)} %queries_ref.1) | copy-start | bytes 1572868
  2.6 7.3 %copy-start.3 = (bf16[64,1024]{1,0:T(8,128)(2,1)S(1)}, bf16[64,1024]{1,0:T(8,128)(2,1)}, u32[]{:S(2)}) copy-start(bf16[64,1024]{1,0:T(8,128)(2,1)} %keys_ref.1) | copy-start | bytes 393220
  2.6 33.3 %copy-start.1 = (f32[8,128,128]{2,1,0:T(8,128)S(1)}, f32[8,128,128]{2,1,0:T(8,128)}, u32[]{:S(2)}) copy-start(f32[8,128,128]{2,1,0:T(8,128)} %query_map_ref.1) | copy-start | bytes 1572868
  2.6 34.6 %all-to-all-start = ((bf16[32,64,128]{2,1,0:T(8,128)(2,1)}), bf16[32,64,128]{2,1,0:T(8,128)(2,1)S(1)}, u32[]{:S(2)}, u32[]{:S(2)}) async-start(bf16[32,64,128]{2,1,0:T(8,128)(2,1)} %shard_map.68), calls=%async_computation | async-start | bytes 1048576 | tf_op jit(solution)/shard_map/all_to_all | solution.py:582
  9.9 26.0 %copy-start.2 = (f32[2,128,128]{2,1,0:T(8,128)S(1)}, f32[2,128,128]{2,1,0:T(8,128)}, u32[]{:S(2)}) copy-start(f32[2,128,128]{2,1,0:T(8,128)} %key_map_ref.1) | copy-start | bytes 393220
  10.0 10.1 %collective-permute-start = (bf16[2,64,128]{2,1,0:T(8,128)(2,1)S(1)}, bf16[2,64,128]{2,1,0:T(8,128)(2,1)S(1)}, u32[]{:S(2)}, u32[]{:S(2)}) collective-permute-start(bf16[2,64,128]{2,1,0:T(8,128)(2,1)S(1)} %get-tuple-element.13), channel_id=1, source_target_pairs={{0,1},{1,0},{2,3},{3,2},{4,5},{5,4},{6,7},{7,6},{8,9},{9,8},{10,11... | collective-permute-start | bytes 98312 | tf_op jit(solution)/shard_map/ppermute | solution.py:562
  11.8 15.5 %collective-permute-start.1 = (bf16[2,64,128]{2,1,0:T(8,128)(2,1)S(1)}, bf16[2,64,128]{2,1,0:T(8,128)(2,1)S(1)}, u32[]{:S(2)}, u32[]{:S(2)}) collective-permute-start(bf16[2,64,128]{2,1,0:T(8,128)(2,1)S(1)} %get-tuple-element.14), channel_id=1, source_target_pairs={{0,2},{1,3},{2,0},{3,1},{4,6},{5,7},{6,4},{7,5},{8,10},{9,11},{10,... | collective-permute-start | bytes 98312 | tf_op jit(solution)/shard_map/ppermute | solution.py:562
  14.2 13.1 %collective-permute-start.2 = (bf16[2,64,128]{2,1,0:T(8,128)(2,1)S(1)}, bf16[2,64,128]{2,1,0:T(8,128)(2,1)S(1)}, u32[]{:S(2)}, u32[]{:S(2)}) collective-permute-start(bf16[2,64,128]{2,1,0:T(8,128)(2,1)S(1)} %get-tuple-element.15), channel_id=1, source_target_pairs={{0,3},{1,2},{2,1},{3,0},{4,7},{5,6},{6,5},{7,4},{8,11},{9,10},{10,... | collective-permute-start | bytes 98312 | tf_op jit(solution)/shard_map/ppermute | solution.py:562
  27.3 8.5 %copy-start.4 = (s32[16]{0:T(128)S(1)}, s32[16]{0:T(128)}, u32[]{:S(2)}) copy-start(s32[16]{0:T(128)} %pos_ref.3) | copy-start | bytes 196
  27.3 5.6 %collective-permute-start.8 = (bf16[4,64,128]{2,1,0:T(8,128)(2,1)S(1)}, bf16[4,64,128]{2,1,0:T(8,128)(2,1)S(1)}, u32[]{:S(2)}, u32[]{:S(2)}) collective-permute-start(bf16[4,64,128]{2,1,0:T(8,128)(2,1)S(1)} %get-tuple-element.17), channel_id=1, source_target_pairs={{0,24},{4,28},{8,16},{12,20},{16,8},{20,12},{24,0},{28,4},{1,25},{... | collective-permute-start | bytes 196616 | tf_op jit(solution)/shard_map/ppermute | solution.py:562
  29.8 4.3 %collective-permute-start.6 = (bf16[4,64,128]{2,1,0:T(8,128)(2,1)S(1)}, bf16[4,64,128]{2,1,0:T(8,128)(2,1)S(1)}, u32[]{:S(2)}, u32[]{:S(2)}) collective-permute-start(bf16[4,64,128]{2,1,0:T(8,128)(2,1)S(1)} %get-tuple-element.17), channel_id=1, source_target_pairs={{0,16},{4,20},{8,24},{12,28},{16,0},{20,4},{24,8},{28,12},{1,17},{... | collective-permute-start | bytes 196616 | tf_op jit(solution)/shard_map/ppermute | solution.py:562
  30.3 4.3 %collective-permute-start.4 = (bf16[4,64,128]{2,1,0:T(8,128)(2,1)S(1)}, bf16[4,64,128]{2,1,0:T(8,128)(2,1)S(1)}, u32[]{:S(2)}, u32[]{:S(2)}) collective-permute-start(bf16[4,64,128]{2,1,0:T(8,128)(2,1)S(1)} %get-tuple-element.16.refs_0_), channel_id=1, source_target_pairs={{0,8},{4,12},{8,0},{12,4},{16,24},{20,28},{24,16},{28,20},{1,9},{5... | collective-permute-start | bytes 196616 | tf_op jit(solution)/shard_map/ppermute | solution.py:562
  30.9 3.7 %collective-permute-start.3 = (bf16[4,64,128]{2,1,0:T(8,128)(2,1)S(1)}, bf16[4,64,128]{2,1,0:T(8,128)(2,1)S(1)}, u32[]{:S(2)}, u32[]{:S(2)}) collective-permute-start(bf16[4,64,128]{2,1,0:T(8,128)(2,1)S(1)} %get-tuple-element.16.refs_0_), channel_id=1, source_target_pairs={{0,4},{4,0},{8,12},{12,8},{16,20},{20,16},{24,28},{28,24},{1,5},{5... | collective-permute-start | bytes 196616 | tf_op jit(solution)/shard_map/ppermute | solution.py:562
  32.9 1.7 %collective-permute-start.9 = (bf16[4,64,128]{2,1,0:T(8,128)(2,1)S(1)}, bf16[4,64,128]{2,1,0:T(8,128)(2,1)S(1)}, u32[]{:S(2)}, u32[]{:S(2)}) collective-permute-start(bf16[4,64,128]{2,1,0:T(8,128)(2,1)S(1)} %collective-permute-done.8.refs_6_), channel_id=1, source_target_pairs={{0,4},{4,0},{8,12},{12,8},{16,20},{20,16},{24,28},{28,24},{1,5},{5... | collective-permute-start | bytes 196616 | tf_op jit(solution)/shard_map/ppermute | solution.py:562
  34.1 1.3 %collective-permute-start.7 = (bf16[4,64,128]{2,1,0:T(8,128)(2,1)S(1)}, bf16[4,64,128]{2,1,0:T(8,128)(2,1)S(1)}, u32[]{:S(2)}, u32[]{:S(2)}) collective-permute-start(bf16[4,64,128]{2,1,0:T(8,128)(2,1)S(1)} %collective-permute-done.6.refs_4_), channel_id=1, source_target_pairs={{0,4},{4,0},{8,12},{12,8},{16,20},{20,16},{24,28},{28,24},{1,5},{5... | collective-permute-start | bytes 196616 | tf_op jit(solution)/shard_map/ppermute | solution.py:562
  34.6 1.3 %collective-permute-start.5 = (bf16[4,64,128]{2,1,0:T(8,128)(2,1)S(1)}, bf16[4,64,128]{2,1,0:T(8,128)(2,1)S(1)}, u32[]{:S(2)}, u32[]{:S(2)}) collective-permute-start(bf16[4,64,128]{2,1,0:T(8,128)(2,1)S(1)} %collective-permute-done.4.refs_2_), channel_id=1, source_target_pairs={{0,4},{4,0},{8,12},{12,8},{16,20},{20,16},{24,28},{28,24},{1,5},{5... | collective-permute-start | bytes 196616 | tf_op jit(solution)/shard_map/ppermute | solution.py:562

commit v7 on v6

--- a/solution.py
+++ b/solution.py
@@ -242,21 +242,43 @@
     return nt(parts, jnp.concatenate([tokens] * 3, axis=1))
 
 
-def key_send_kernel(keys_ref, *out_refs):
-    head = lax.axis_index("head")
-    key_heads = out_refs[0].shape[0]
-    for other, out_ref in enumerate(out_refs):
+def send_kernel(seq_count, queries_ref, keys_ref, *refs):
+    queries_out_ref, *keys_out_refs, query_buffer, key_buffer, sems, query_sems, key_sems = refs
+    head_count = len(keys_out_refs)
+    key_heads = keys_out_refs[0].shape[0]
+    keys_in = pltpu.make_async_copy(keys_ref, key_buffer, sems.at[0])
+    queries_in = pltpu.make_async_copy(queries_ref, query_buffer, sems.at[1])
+    keys_in.start()
+    queries_in.start()
+    leaving = []
+    keys_in.wait()
+    for other, out_ref in enumerate(keys_out_refs):
         for number in range(key_heads):
-            column = ((head ^ other) * key_heads + number) * HEAD_SIZE
+            column = ((lax.axis_index("head") ^ other) * key_heads + number) * HEAD_SIZE
             column = pl.multiple_of(column, HEAD_SIZE)
-            out_ref[number] = keys_ref[:, pl.ds(column, HEAD_SIZE)]
-
-
-def query_send_kernel(seq_count, head_count, queries_ref, out_ref):
+            leaving.append(
+                pltpu.make_async_copy(
+                    key_buffer.at[:, pl.ds(column, HEAD_SIZE)],
+                    out_ref.at[number],
+                    key_sems.at[other, number],
+                )
+            )
+            leaving[-1].start()
+    queries_in.wait()
     for head in range(head_count):
         for seq in range(seq_count):
             column = (head * seq_count + seq) * HEAD_SIZE
-            out_ref[seq * head_count + head] = queries_ref[:, column : column + HEAD_SIZE]
+            target = seq * head_count + head
+            leaving.append(
+                pltpu.make_async_copy(
+                    query_buffer.at[:, column : column + HEAD_SIZE],
+                    queries_out_ref.at[target],
+                    query_sems.at[target],
+                )
+            )
+            leaving[-1].start()
+    for copy in leaving:
+        copy.wait()
 
 
 def key_turn_kernel(share, *refs):
@@ -476,35 +498,28 @@
         turn_features(seq, seq_blocks - 1)
 
     def pair_steps(seq):
-        ahead = pair_scores(seq, 0)
+        order = list(reversed(range(tiles)))
+        ahead = pair_scores(seq, order[0])
         behind = None
-        for tile in range(tiles):
+        for number, tile in enumerate(order):
             stats = ahead
-            if tile + 1 < tiles:
-                ahead = pair_scores(seq, tile + 1)
+            if number + 1 < tiles:
+                ahead = pair_scores(seq, order[number + 1])
             for half in range(width):
                 pair_gradients(seq, tile, half, stats[half])
                 yield
-            upstream = query_upstream(seq, tile)
-            if tile:
-                query_change(seq, tile - 1, behind)
-            behind = upstream
+            upstreams = query_upstream(seq, tile), key_upstream(seq, tile)
+            if behind:
+                query_change(seq, order[number - 1], behind[0])
+                key_change(seq, order[number - 1], behind[1])
+            behind = upstreams
         yield
-        query_change(seq, tiles - 1, behind)
-
-    def key_steps(seq):
-        ahead = key_upstream(seq, 0)
-        yield
-        for tile in range(tiles):
-            upstream = ahead
-            if tile + 1 < tiles:
-                ahead = key_upstream(seq, tile + 1)
-            key_change(seq, tile, upstream)
-            yield
+        query_change(seq, order[-1], behind[0])
+        key_change(seq, order[-1], behind[1])
 
     for chunk in range(token_count // rows):
         query_rows[sorted_rows(pos_ref, chunk, rows), :] = arrived_ref[chunk]
-    stages = (feature_steps, pair_steps, key_steps)
+    stages = (feature_steps, pair_steps)
     for turn in range(sequences + len(stages) - 1):
         active = [
             stage(turn - number)
@@ -562,23 +577,24 @@
         return lax.ppermute(piece, axis, [(i, i ^ bits) for i in range(size)])
 
     small = pltpu.CompilerParams(vmem_limit_bytes=4 << 20)
-    by_plane = pl.pallas_call(
-        key_send_kernel,
-        out_shape=[jax.ShapeDtypeStruct((key_heads, rows, HEAD_SIZE), BF16)] * head_count,
-        in_specs=[vmem],
-        out_specs=[vmem] * head_count,
-        compiler_params=small,
-    )(keys)
-    by_plane = list(by_plane)
+    anywhere = pl.BlockSpec(memory_space=pl.ANY)
+    sent, *by_plane = pl.pallas_call(
+        functools.partial(send_kernel, seq_count),
+        out_shape=[jax.ShapeDtypeStruct((devices, rows, HEAD_SIZE), BF16)]
+        + [jax.ShapeDtypeStruct((key_heads, rows, HEAD_SIZE), BF16)] * head_count,
+        in_specs=[anywhere] * 2,
+        out_specs=[anywhere] * (head_count + 1),
+        scratch_shapes=[
+            pltpu.VMEM(queries.shape, BF16),
+            pltpu.VMEM(keys.shape, BF16),
+            pltpu.SemaphoreType.DMA((2,)),
+            pltpu.SemaphoreType.DMA((devices,)),
+            pltpu.SemaphoreType.DMA((head_count, key_heads)),
+        ],
+        compiler_params=pltpu.CompilerParams(vmem_limit_bytes=60 << 20),
+    )(queries, keys)
     for other in range(1, head_count):
         by_plane[other] = swap(by_plane[other], "head", other)
-    sent = pl.pallas_call(
-        functools.partial(query_send_kernel, seq_count, head_count),
-        out_shape=jax.ShapeDtypeStruct((devices, rows, HEAD_SIZE), BF16),
-        in_specs=[vmem],
-        out_specs=vmem,
-        compiler_params=small,
-    )(queries)
     arrived = lax.all_to_all(sent, ("seq", "head"), split_axis=0, concat_axis=0, tiled=True)
     by_key_head = pl.pallas_call(
         functools.partial(key_turn_kernel, share),

time: 57 us -> 57.1 us (level)
  local copies, waits for them, and re-layouts: 1.05 us -> 0.04 us
  Pallas kernels: 11.4 us -> 12.4 us
    pallas_call x2 -> x1, Pallas kernels: 0.93 us -> 2.26 us  [per_device_head(): pl.pallas_call(functools.partial(send_kernel, seq_count), out_shape=[jax....]
    unnamed x10 -> x14, local copies, waits for them, and re-layouts: 1.05 us -> 0.04 us
where the time goes in v7:
time: 57.1 us; the launch traced here: 56.8 us
  waiting for transfers between devices  17.9 us (31%)
  starting transfers between devices  15.3 us (27%)
  Pallas kernels  12.4 us (22%)
  blocking collectives  10.4 us (18%)
  between operations  0.76 us (1%)
    ppermute x10, waiting for transfers between devices, swap(): return lax.ppermute(piece, axis, [(i, i ^ bits) for i in range(size)])  17.9 us
    all_gather x1, blocking collectives, per_device_head(): everyone = lax.all_gather(grads, 'seq', axis=0, tiled=False)  10.4 us
    ppermute x10, starting transfers between devices, swap(): return lax.ppermute(piece, axis, [(i, i ^ bits) for i in range(size)])  8.02 us
    pallas_call x1, Pallas kernels, per_device_head(): pl.pallas_call(functools.partial(pair_kernel, token_count, seq_count), ou...  7.93 us
    all_to_all x1, starting transfers between devices, per_device_head(): lax.all_to_all(sent, ('seq', 'head'), split_axis=0, concat_axis=0, tiled=...  7.33 us
    pallas_call x1, Pallas kernels, per_device_head(): pl.pallas_call(functools.partial(send_kernel, seq_count), out_shape=[jax....  2.26 us
    pallas_call x1, Pallas kernels, per_device_head(): pl.pallas_call(functools.partial(key_kernel, share), out_shape=(jax.Shape...  1.28 us
  transfers between devices with their start and end apart: 11, of which 7 were waited for; matrix products, arithmetic and copies ran while one was open for 0% of the time, Pallas kernels for 2%

profile of v7, /device:TPU:0, one launch (start us, length us, event | category | flops | bytes accessed | tf_op | source)
XLA Modules:
  0.0 56.8 jit_solution(4676612471566329526)
XLA Ops:
  0.6 2.3 %shard_map.68 = (bf16[32,64,128]{2,1,0:T(8,128)(2,1)}, bf16[2,64,128]{2,1,0:T(8,128)(2,1)}, bf16[2,64,128]{2,1,0:T(8,128)(2,1)}, bf16[2,64,128]{2,1,0:T(8,128)(2,1)}, bf16[2,64,128]{2,1,0:T(8,128)(2,1)}) custom-call(bf16[64,4096]{1,0:T(8,128)(2,1)} %queries_ref.1, bf16[64,1024]{1,0:T(8,128)(2,1)} %keys_ref.1), custom_call_target="tpu_custom_call" | custom-call | tf_op jit(solution)/shard_map/pallas_call | solution.py:581
  2.9 0.0 copy-start.2
  2.9 0.0 copy-start
  2.9 7.3 %all-to-all-start = ((bf16[32,64,128]{2,1,0:T(8,128)(2,1)}), bf16[32,64,128]{2,1,0:T(8,128)(2,1)S(1)}, u32[]{:S(2)}, u32[]{:S(2)}) async-start(bf16[32,64,128]{2,1,0:T(8,128)(2,1)} %get-tuple-element.13), calls=%async_computation | async-start | bytes 1048576 | tf_op jit(solution)/shard_map/all_to_all | solution.py:598
  10.3 0.0 copy-start.1
  10.3 1.8 %collective-permute-start = (bf16[2,64,128]{2,1,0:T(8,128)(2,1)S(1)}, bf16[2,64,128]{2,1,0:T(8,128)(2,1)S(1)}, u32[]{:S(2)}, u32[]{:S(2)}) collective-permute-start(bf16[2,64,128]{2,1,0:T(8,128)(2,1)S(1)} %copy-done.6), channel_id=1, source_target_pairs={{0,1},{1,0},{2,3},{3,2},{4,5},{5,4},{6,7},{7,6},{8,9},{9,8},{10,11... | collective-permute-start | bytes 98312 | tf_op jit(solution)/shard_map/ppermute | solution.py:577
  12.1 2.4 %collective-permute-start.1 = (bf16[2,64,128]{2,1,0:T(8,128)(2,1)S(1)}, bf16[2,64,128]{2,1,0:T(8,128)(2,1)S(1)}, u32[]{:S(2)}, u32[]{:S(2)}) collective-permute-start(bf16[2,64,128]{2,1,0:T(8,128)(2,1)S(1)} %copy-done.5), channel_id=1, source_target_pairs={{0,2},{1,3},{2,0},{3,1},{4,6},{5,7},{6,4},{7,5},{8,10},{9,11},{10,... | collective-permute-start | bytes 98312 | tf_op jit(solution)/shard_map/ppermute | solution.py:577
  14.6 0.2 collective-permute-start.2
  14.8 5.7 %collective-permute-done.refs_1_ = bf16[2,64,128]{2,1,0:T(8,128)(2,1)S(1)} collective-permute-done((bf16[2,64,128]{2,1,0:T(8,128)(2,1)S(1)}, bf16[2,64,128]{2,1,0:T(8,128)(2,1)S(1)}, u32[]{:S(2)}, u32[]{:S(2)}) %collective-permute-start) | collective-permute-done | bytes 32800 | tf_op jit(solution)/shard_map/ppermute | solution.py:577
  20.5 7.3 %collective-permute-done.1.refs_2_ = bf16[2,64,128]{2,1,0:T(8,128)(2,1)S(1)} collective-permute-done((bf16[2,64,128]{2,1,0:T(8,128)(2,1)S(1)}, bf16[2,64,128]{2,1,0:T(8,128)(2,1)S(1)}, u32[]{:S(2)}, u32[]{:S(2)}) %collective-permute-start.1) | collective-permute-done | bytes 32800 | tf_op jit(solution)/shard_map/ppermute | solution.py:577
  27.7 0.0 collective-permute-done.2.refs_3_
  27.7 0.0 copy-start.3
  27.7 2.5 %collective-permute-start.8 = (bf16[4,64,128]{2,1,0:T(8,128)(2,1)S(1)}, bf16[4,64,128]{2,1,0:T(8,128)(2,1)S(1)}, u32[]{:S(2)}, u32[]{:S(2)}) collective-permute-start(bf16[4,64,128]{2,1,0:T(8,128)(2,1)S(1)} %get-tuple-element.19), channel_id=1, source_target_pairs={{0,24},{4,28},{8,16},{12,20},{16,8},{20,12},{24,0},{28,4},{1,25},{... | collective-permute-start | bytes 196616 | tf_op jit(solution)/shard_map/ppermute | solution.py:577
  30.2 0.5 collective-permute-start.6
  30.7 0.6 collective-permute-start.4
  31.3 2.0 %collective-permute-done.8.refs_6_ = bf16[4,64,128]{2,1,0:T(8,128)(2,1)S(1)} collective-permute-done((bf16[4,64,128]{2,1,0:T(8,128)(2,1)S(1)}, bf16[4,64,128]{2,1,0:T(8,128)(2,1)S(1)}, u32[]{:S(2)}, u32[]{:S(2)}) %collective-permute-start.8) | collective-permute-done | bytes 65568 | tf_op jit(solution)/shard_map/ppermute | solution.py:577
  33.3 1.1 %collective-permute-done.6.refs_4_ = bf16[4,64,128]{2,1,0:T(8,128)(2,1)S(1)} collective-permute-done((bf16[4,64,128]{2,1,0:T(8,128)(2,1)S(1)}, bf16[4,64,128]{2,1,0:T(8,128)(2,1)S(1)}, u32[]{:S(2)}, u32[]{:S(2)}) %collective-permute-start.6) | collective-permute-done | bytes 65568 | tf_op jit(solution)/shard_map/ppermute | solution.py:577
  34.5 0.5 collective-permute-done.4.refs_2_
  35.0 0.7 %collective-permute-done.7.refs_5_ = bf16[4,64,128]{2,1,0:T(8,128)(2,1)S(1)} collective-permute-done((bf16[4,64,128]{2,1,0:T(8,128)(2,1)S(1)}, bf16[4,64,128]{2,1,0:T(8,128)(2,1)S(1)}, u32[]{:S(2)}, u32[]{:S(2)}) %collective-permute-start.7) | collective-permute-done | bytes 65568 | tf_op jit(solution)/shard_map/ppermute | solution.py:577
  35.7 0.5 collective-permute-done.5.refs_3_
  36.3 1.3 %shard_map.70 = (bf16[2048,128]{1,0:T(8,128)(2,1)S(1)}, f32[1,256,1024]{2,1,0:T(8,128)S(1)}, f32[128,128]{1,0:T(8,128)S(1)}, f32[128,128]{1,0:T(8,128)S(1)}) custom-call(s32[16]{0:T(128)S(1)} %copy-done.3, f32[2,128,128]{2,1,0:T(8,128)S(1)} %copy-done.1, f32[8,128,128]{2,1,0:T(8,128)S(1)} %copy-done, bf16[4,64,128]{2,1,0:T(8,128)(2,1)S(1)} %get-tuple-element.18.refs_0_, ...), custom_call_target="tpu_custom_call" | custom-call | flops 201326592 | bytes 3145728 | tf_op jit(solution)/shard_map/pallas_call | solution.py:614
  37.6 7.9 %shard_map.71 = bf16[384,128]{1,0:T(8,128)(2,1)S(1)} custom-call(s32[16]{0:T(128)S(1)} %copy-done.3, bf16[32,64,128]{2,1,0:T(8,128)(2,1)S(1)} %all-to-all-done.arrived_ref, f32[128,128]{1,0:T(8,128)S(1)} %get-tuple-element.20.query_weights_ref, f32[128,128]{1,0:T(8,128)S(1)} %get-tuple-element.21.key_weights_ref, ...), custom_call_target="tpu_custom_call" | custom-call | tf_op jit(solution)/shard_map/pallas_call | solution.py:631
  45.5 10.4 %all-gather = bf16[3072,128]{1,0:T(8,128)(2,1)S(1)} all-gather(bf16[384,128]{1,0:T(8,128)(2,1)S(1)} %shard_map.71), channel_id=2, replica_groups=mesh['seq'=8,'head'=4] {'seq'}, dimensions={0}, use_global_device_ids=true | all-gather | bytes 884736 | tf_op jit(solution)/shard_map/all_gather | solution.py:651
  55.9 0.9 %shard_map.72 = (f32[8,128,128]{2,1,0:T(8,128)}, f32[2,128,128]{2,1,0:T(8,128)}) custom-call(bf16[8,384,128]{2,1,0:T(8,128)(2,1)S(1)} %bitcast.1), custom_call_target="tpu_custom_call" | custom-call | tf_op jit(solution)/shard_map/pallas_call | solution.py:652
  (18 shorter events, 0.0 us)
Async XLA Ops:
  2.9 7.4 %copy-start.6 = (bf16[2,64,128]{2,1,0:T(8,128)(2,1)S(1)}, bf16[2,64,128]{2,1,0:T(8,128)(2,1)}, u32[]{:S(2)}) copy-start(bf16[2,64,128]{2,1,0:T(8,128)(2,1)} %get-tuple-element.15) | copy-start | bytes 98308
  2.9 9.2 %copy-start.5 = (bf16[2,64,128]{2,1,0:T(8,128)(2,1)S(1)}, bf16[2,64,128]{2,1,0:T(8,128)(2,1)}, u32[]{:S(2)}) copy-start(bf16[2,64,128]{2,1,0:T(8,128)(2,1)} %get-tuple-element.16) | copy-start | bytes 98308
  2.9 11.7 %copy-start.4 = (bf16[2,64,128]{2,1,0:T(8,128)(2,1)S(1)}, bf16[2,64,128]{2,1,0:T(8,128)(2,1)}, u32[]{:S(2)}) copy-start(bf16[2,64,128]{2,1,0:T(8,128)(2,1)} %get-tuple-element.17) | copy-start | bytes 98308
  2.9 24.8 %copy-start.2 = (bf16[2,64,128]{2,1,0:T(8,128)(2,1)S(1)}, bf16[2,64,128]{2,1,0:T(8,128)(2,1)}, u32[]{:S(2)}) copy-start(bf16[2,64,128]{2,1,0:T(8,128)(2,1)} %get-tuple-element.14.refs_0_) | copy-start | bytes 98308
  2.9 33.3 %copy-start = (f32[8,128,128]{2,1,0:T(8,128)S(1)}, f32[8,128,128]{2,1,0:T(8,128)}, u32[]{:S(2)}) copy-start(f32[8,128,128]{2,1,0:T(8,128)} %query_map_ref.1) | copy-start | bytes 1572868
  2.9 34.6 %all-to-all-start = ((bf16[32,64,128]{2,1,0:T(8,128)(2,1)}), bf16[32,64,128]{2,1,0:T(8,128)(2,1)S(1)}, u32[]{:S(2)}, u32[]{:S(2)}) async-start(bf16[32,64,128]{2,1,0:T(8,128)(2,1)} %get-tuple-element.13), calls=%async_computation | async-start | bytes 1048576 | tf_op jit(solution)/shard_map/all_to_all | solution.py:598
  10.3 26.0 %copy-start.1 = (f32[2,128,128]{2,1,0:T(8,128)S(1)}, f32[2,128,128]{2,1,0:T(8,128)}, u32[]{:S(2)}) copy-start(f32[2,128,128]{2,1,0:T(8,128)} %key_map_ref.1) | copy-start | bytes 393220
  10.3 10.2 %collective-permute-start = (bf16[2,64,128]{2,1,0:T(8,128)(2,1)S(1)}, bf16[2,64,128]{2,1,0:T(8,128)(2,1)S(1)}, u32[]{:S(2)}, u32[]{:S(2)}) collective-permute-start(bf16[2,64,128]{2,1,0:T(8,128)(2,1)S(1)} %copy-done.6), channel_id=1, source_target_pairs={{0,1},{1,0},{2,3},{3,2},{4,5},{5,4},{6,7},{7,6},{8,9},{9,8},{10,11... | collective-permute-start | bytes 98312 | tf_op jit(solution)/shard_map/ppermute | solution.py:577
  12.1 15.6 %collective-permute-start.1 = (bf16[2,64,128]{2,1,0:T(8,128)(2,1)S(1)}, bf16[2,64,128]{2,1,0:T(8,128)(2,1)S(1)}, u32[]{:S(2)}, u32[]{:S(2)}) collective-permute-start(bf16[2,64,128]{2,1,0:T(8,128)(2,1)S(1)} %copy-done.5), channel_id=1, source_target_pairs={{0,2},{1,3},{2,0},{3,1},{4,6},{5,7},{6,4},{7,5},{8,10},{9,11},{10,... | collective-permute-start | bytes 98312 | tf_op jit(solution)/shard_map/ppermute | solution.py:577
  14.6 13.2 %collective-permute-start.2 = (bf16[2,64,128]{2,1,0:T(8,128)(2,1)S(1)}, bf16[2,64,128]{2,1,0:T(8,128)(2,1)S(1)}, u32[]{:S(2)}, u32[]{:S(2)}) collective-permute-start(bf16[2,64,128]{2,1,0:T(8,128)(2,1)S(1)} %copy-done.4), channel_id=1, source_target_pairs={{0,3},{1,2},{2,1},{3,0},{4,7},{5,6},{6,5},{7,4},{8,11},{9,10},{10,... | collective-permute-start | bytes 98312 | tf_op jit(solution)/shard_map/ppermute | solution.py:577
  27.7 8.5 %copy-start.3 = (s32[16]{0:T(128)S(1)}, s32[16]{0:T(128)}, u32[]{:S(2)}) copy-start(s32[16]{0:T(128)} %pos_ref.3) | copy-start | bytes 196
  27.7 5.6 %collective-permute-start.8 = (bf16[4,64,128]{2,1,0:T(8,128)(2,1)S(1)}, bf16[4,64,128]{2,1,0:T(8,128)(2,1)S(1)}, u32[]{:S(2)}, u32[]{:S(2)}) collective-permute-start(bf16[4,64,128]{2,1,0:T(8,128)(2,1)S(1)} %get-tuple-element.19), channel_id=1, source_target_pairs={{0,24},{4,28},{8,16},{12,20},{16,8},{20,12},{24,0},{28,4},{1,25},{... | collective-permute-start | bytes 196616 | tf_op jit(solution)/shard_map/ppermute | solution.py:577
  30.2 4.3 %collective-permute-start.6 = (bf16[4,64,128]{2,1,0:T(8,128)(2,1)S(1)}, bf16[4,64,128]{2,1,0:T(8,128)(2,1)S(1)}, u32[]{:S(2)}, u32[]{:S(2)}) collective-permute-start(bf16[4,64,128]{2,1,0:T(8,128)(2,1)S(1)} %get-tuple-element.19), channel_id=1, source_target_pairs={{0,16},{4,20},{8,24},{12,28},{16,0},{20,4},{24,8},{28,12},{1,17},{... | collective-permute-start | bytes 196616 | tf_op jit(solution)/shard_map/ppermute | solution.py:577
  30.7 4.3 %collective-permute-start.4 = (bf16[4,64,128]{2,1,0:T(8,128)(2,1)S(1)}, bf16[4,64,128]{2,1,0:T(8,128)(2,1)S(1)}, u32[]{:S(2)}, u32[]{:S(2)}) collective-permute-start(bf16[4,64,128]{2,1,0:T(8,128)(2,1)S(1)} %get-tuple-element.18.refs_0_), channel_id=1, source_target_pairs={{0,8},{4,12},{8,0},{12,4},{16,24},{20,28},{24,16},{28,20},{1,9},{5... | collective-permute-start | bytes 196616 | tf_op jit(solution)/shard_map/ppermute | solution.py:577
  31.3 3.7 %collective-permute-start.3 = (bf16[4,64,128]{2,1,0:T(8,128)(2,1)S(1)}, bf16[4,64,128]{2,1,0:T(8,128)(2,1)S(1)}, u32[]{:S(2)}, u32[]{:S(2)}) collective-permute-start(bf16[4,64,128]{2,1,0:T(8,128)(2,1)S(1)} %get-tuple-element.18.refs_0_), channel_id=1, source_target_pairs={{0,4},{4,0},{8,12},{12,8},{16,20},{20,16},{24,28},{28,24},{1,5},{5... | collective-permute-start | bytes 196616 | tf_op jit(solution)/shard_map/ppermute | solution.py:577
  33.3 1.7 %collective-permute-start.9 = (bf16[4,64,128]{2,1,0:T(8,128)(2,1)S(1)}, bf16[4,64,128]{2,1,0:T(8,128)(2,1)S(1)}, u32[]{:S(2)}, u32[]{:S(2)}) collective-permute-start(bf16[4,64,128]{2,1,0:T(8,128)(2,1)S(1)} %collective-permute-done.8.refs_6_), channel_id=1, source_target_pairs={{0,4},{4,0},{8,12},{12,8},{16,20},{20,16},{24,28},{28,24},{1,5},{5... | collective-permute-start | bytes 196616 | tf_op jit(solution)/shard_map/ppermute | solution.py:577
  34.5 1.3 %collective-permute-start.7 = (bf16[4,64,128]{2,1,0:T(8,128)(2,1)S(1)}, bf16[4,64,128]{2,1,0:T(8,128)(2,1)S(1)}, u32[]{:S(2)}, u32[]{:S(2)}) collective-permute-start(bf16[4,64,128]{2,1,0:T(8,128)(2,1)S(1)} %collective-permute-done.6.refs_4_), channel_id=1, source_target_pairs={{0,4},{4,0},{8,12},{12,8},{16,20},{20,16},{24,28},{28,24},{1,5},{5... | collective-permute-start | bytes 196616 | tf_op jit(solution)/shard_map/ppermute | solution.py:577
  35.0 1.3 %collective-permute-start.5 = (bf16[4,64,128]{2,1,0:T(8,128)(2,1)S(1)}, bf16[4,64,128]{2,1,0:T(8,128)(2,1)S(1)}, u32[]{:S(2)}, u32[]{:S(2)}) collective-permute-start(bf16[4,64,128]{2,1,0:T(8,128)(2,1)S(1)} %collective-permute-done.4.refs_2_), channel_id=1, source_target_pairs={{0,4},{4,0},{8,12},{12,8},{16,20},{20,16},{24,28},{28,24},{1,5},{5... | collective-permute-start | bytes 196616 | tf_op jit(solution)/shard_map/ppermute | solution.py:577

commit v8 on v7

--- a/solution.py
+++ b/solution.py
@@ -201,8 +201,8 @@
 
 
 def features_t(logits):
-    up = jnp.exp(logits - jnp.max(logits, axis=0, keepdims=True))
-    down = jnp.exp(jnp.min(logits, axis=0, keepdims=True) - logits)
+    up = jnp.exp2(logits - jnp.max(logits, axis=0, keepdims=True))
+    down = jnp.exp2(jnp.min(logits, axis=0, keepdims=True) - logits)
     up = up * (1.0 / jnp.sum(up, axis=0, keepdims=True))
     down = down * (1.0 / jnp.sum(down, axis=0, keepdims=True))
     return jnp.concatenate([up, down], axis=0)
@@ -230,7 +230,7 @@
 
 
 def map_parts(weights):
-    rest = weights.T
+    rest = weights.T * math.log2(math.e)
     parts = []
     for _ in range(3):
         parts.append(rest.astype(BF16))
@@ -355,15 +355,20 @@
     for seq in range(sequences):
         for at in range(0, seq_blocks, width):
             if width > 1:
-                pair_weights[seq, block(at + 1), block(at)] = jnp.zeros((BLK, BLK), BF16)
+                pair_weights[seq, at, block(at + 1), :] = jnp.zeros((BLK, BLK), BF16)
     parts = map_parts(query_weights_ref[...])
     key_parts = map_parts(key_weights_ref[...])
     early = phi_k_early.shape[0]
     lane = lax.broadcasted_iota(jnp.int32, (BLK, BLK), 1)
     sublane = lax.broadcasted_iota(jnp.int32, (BLK, BLK), 0)
-    unit = jnp.where(lane == sublane, 1.0, 0.0).astype(BF16)
     visible = sublane <= lane
     exponent_scale = HEAD_SIZE ** (-0.5) * math.log2(math.e)
+
+    def side_by_side(pieces):
+        return jnp.concatenate(list(pieces), axis=1)
+
+    def blocks_of(here):
+        return range(here.start // BLK, here.stop // BLK)
 
     def span(tile):
         return slice(tile * width * BLK, (tile + 1) * width * BLK)
@@ -377,7 +382,7 @@
     def query_features(seq, at, logits):
         feature = features_t(logits)
         phi_q[seq, :, block(at)] = feature
-        phi_qb[seq, :, block(at)] = feature.astype(BF16)
+        phi_qb[seq, at] = feature.astype(BF16)
 
     def phi_k(seq, at):
         if seq < early:
@@ -394,15 +399,20 @@
             phi_k_late[seq - early, :, block(at)] = features_t(logits)
 
     def turn_features(seq, at):
-        rounded = phi_k(seq, at).astype(BF16)
-        phi_kb[seq, :, block(at)] = rounded
-        phi_kb_rows[seq, block(at), :] = nt(unit, rounded).astype(BF16)
+        feature = phi_k(seq, at)
+        phi_kb[seq, at] = feature.astype(BF16)
+        for half in range(2):
+            turned = feature[half * HEAD_SIZE : (half + 1) * HEAD_SIZE].T
+            phi_kb_rows[seq, half, block(at), :] = turned.astype(BF16)
 
     def pair_scores(seq, tile):
         here = span(tile)
         slot = tile % 2
         teacher = nt(key_rows[flat(seq, slice(0, here.stop)), :], query_rows[flat(seq, here), :])
-        student = nn(phi_kb_rows[seq, : here.stop, :], phi_qb[seq, :, here])
+        student = nn(
+            side_by_side(phi_kb_rows[seq, half, : here.stop, :] for half in range(2)),
+            side_by_side(phi_qb[seq, at] for at in blocks_of(here)),
+        )
         stats = []
         for half in range(width):
             at = tile * width + half
@@ -445,7 +455,7 @@
             weights = base - exponent * rate / linears[seq, slot, block(number), block(half)]
             if number == at:
                 weights = jnp.where(visible, weights, 0.0)
-            pair_weights[seq, block(number), block(at)] = weights.astype(BF16)
+            pair_weights[seq, at, block(number), :] = weights.astype(BF16)
 
     def map_change(phis, upstream, tokens):
         changes = [
@@ -457,15 +467,21 @@
 
     def query_upstream(seq, tile):
         here = span(tile)
-        return nn(phi_kb[seq, :, : here.stop], pair_weights[seq, : here.stop, here])
+        return nn(
+            side_by_side(phi_kb[seq, at] for at in range(here.stop // BLK)),
+            side_by_side(pair_weights[seq, at, : here.stop, :] for at in blocks_of(here)),
+        )
 
     def query_change(seq, tile, upstream):
         phis = [phi_q[seq, :, block(tile * width + half)] for half in range(width)]
         acc_q[...] += map_change(phis, upstream, query_rows[flat(seq, span(tile)), :])
 
     def key_upstream(seq, tile):
-        later = slice(tile * width * BLK, seq_blocks * BLK)
-        return nt(phi_qb[seq, :, later], pair_weights[seq, span(tile), later])
+        later = range(tile * width, seq_blocks)
+        return nt(
+            side_by_side(phi_qb[seq, at] for at in later),
+            side_by_side(pair_weights[seq, at, span(tile), :] for at in later),
+        )
 
     def key_change(seq, tile, upstream):
         phis = [phi_k(seq, tile * width + half) for half in range(width)]
@@ -636,11 +652,11 @@
         scratch_shapes=[
             pltpu.VMEM((token_count, HEAD_SIZE), BF16),
             pltpu.VMEM((sequences, 2 * HEAD_SIZE, seq_tokens), F32),
-            pltpu.VMEM((sequences, 2 * HEAD_SIZE, seq_tokens), BF16),
+            pltpu.VMEM((sequences, seq_count, 2 * HEAD_SIZE, BLK), BF16),
             pltpu.VMEM((max(sequences - early, 1), 2 * HEAD_SIZE, seq_tokens), F32),
-            pltpu.VMEM((sequences, 2 * HEAD_SIZE, seq_tokens), BF16),
-            pltpu.VMEM((sequences, seq_tokens, 2 * HEAD_SIZE), BF16),
-            pltpu.VMEM((sequences, seq_tokens, seq_tokens), BF16),
+            pltpu.VMEM((sequences, seq_count, 2 * HEAD_SIZE, BLK), BF16),
+            pltpu.VMEM((sequences, 2, seq_tokens, HEAD_SIZE), BF16),
+            pltpu.VMEM((sequences, seq_count, seq_tokens, BLK), BF16),
             pltpu.VMEM((sequences, 2, seq_tokens, 2 * BLK), F32),
             pltpu.VMEM((sequences, 2, seq_tokens, 2 * BLK), F32),
             pltpu.VMEM((HEAD_SIZE, HEAD_SIZE), F32),

time: 57.1 us -> 56.1 us (0.982)
  Pallas kernels: 12.4 us -> 11.4 us
    pallas_call x1, Pallas kernels: 7.93 us -> 6.93 us  [per_device_head(): pl.pallas_call(functools.partial(pair_kernel, token_count, seq_count), ou...]
where the time goes in v8:
time: 56.1 us; the launch traced here: 55.8 us
  waiting for transfers between devices  17.9 us (32%)
  starting transfers between devices  15.3 us (27%)
  Pallas kernels  11.4 us (20%)
  blocking collectives  10.4 us (19%)
  between operations  0.76 us (1%)
    ppermute x10, waiting for transfers between devices, swap(): return lax.ppermute(piece, axis, [(i, i ^ bits) for i in range(size)])  17.9 us
    all_gather x1, blocking collectives, per_device_head(): everyone = lax.all_gather(grads, 'seq', axis=0, tiled=False)  10.4 us
    ppermute x10, starting transfers between devices, swap(): return lax.ppermute(piece, axis, [(i, i ^ bits) for i in range(size)])  8.02 us
    all_to_all x1, starting transfers between devices, per_device_head(): lax.all_to_all(sent, ('seq', 'head'), split_axis=0, concat_axis=0, tiled=...  7.33 us
    pallas_call x1, Pallas kernels, per_device_head(): pl.pallas_call(functools.partial(pair_kernel, token_count, seq_count), ou...  6.93 us
    pallas_call x1, Pallas kernels, per_device_head(): pl.pallas_call(functools.partial(send_kernel, seq_count), out_shape=[jax....  2.26 us
    pallas_call x1, Pallas kernels, per_device_head(): pl.pallas_call(functools.partial(key_kernel, share), out_shape=(jax.Shape...  1.28 us
  transfers between devices with their start and end apart: 11, of which 7 were waited for; matrix products, arithmetic and copies ran while one was open for 0% of the time, Pallas kernels for 2%

profile of v8, /device:TPU:0, one launch (start us, length us, event | category | flops | bytes accessed | tf_op | source)
XLA Modules:
  0.0 55.8 jit_solution(11733886175002380818)
XLA Ops:
  0.6 2.3 %shard_map.68 = (bf16[32,64,128]{2,1,0:T(8,128)(2,1)}, bf16[2,64,128]{2,1,0:T(8,128)(2,1)}, bf16[2,64,128]{2,1,0:T(8,128)(2,1)}, bf16[2,64,128]{2,1,0:T(8,128)(2,1)}, bf16[2,64,128]{2,1,0:T(8,128)(2,1)}) custom-call(bf16[64,4096]{1,0:T(8,128)(2,1)} %queries_ref.1, bf16[64,1024]{1,0:T(8,128)(2,1)} %keys_ref.1), custom_call_target="tpu_custom_call" | custom-call | tf_op jit(solution)/shard_map/pallas_call | solution.py:597
  2.9 0.0 copy-start.2
  2.9 0.0 copy-start
  2.9 7.3 %all-to-all-start = ((bf16[32,64,128]{2,1,0:T(8,128)(2,1)}), bf16[32,64,128]{2,1,0:T(8,128)(2,1)S(1)}, u32[]{:S(2)}, u32[]{:S(2)}) async-start(bf16[32,64,128]{2,1,0:T(8,128)(2,1)} %get-tuple-element.13), calls=%async_computation | async-start | bytes 1048576 | tf_op jit(solution)/shard_map/all_to_all | solution.py:614
  10.3 0.0 copy-start.1
  10.3 1.8 %collective-permute-start = (bf16[2,64,128]{2,1,0:T(8,128)(2,1)S(1)}, bf16[2,64,128]{2,1,0:T(8,128)(2,1)S(1)}, u32[]{:S(2)}, u32[]{:S(2)}) collective-permute-start(bf16[2,64,128]{2,1,0:T(8,128)(2,1)S(1)} %copy-done.6), channel_id=1, source_target_pairs={{0,1},{1,0},{2,3},{3,2},{4,5},{5,4},{6,7},{7,6},{8,9},{9,8},{10,11... | collective-permute-start | bytes 98312 | tf_op jit(solution)/shard_map/ppermute | solution.py:593
  12.1 2.4 %collective-permute-start.1 = (bf16[2,64,128]{2,1,0:T(8,128)(2,1)S(1)}, bf16[2,64,128]{2,1,0:T(8,128)(2,1)S(1)}, u32[]{:S(2)}, u32[]{:S(2)}) collective-permute-start(bf16[2,64,128]{2,1,0:T(8,128)(2,1)S(1)} %copy-done.5), channel_id=1, source_target_pairs={{0,2},{1,3},{2,0},{3,1},{4,6},{5,7},{6,4},{7,5},{8,10},{9,11},{10,... | collective-permute-start | bytes 98312 | tf_op jit(solution)/shard_map/ppermute | solution.py:593
  14.6 0.2 collective-permute-start.2
  14.8 5.7 %collective-permute-done.refs_1_ = bf16[2,64,128]{2,1,0:T(8,128)(2,1)S(1)} collective-permute-done((bf16[2,64,128]{2,1,0:T(8,128)(2,1)S(1)}, bf16[2,64,128]{2,1,0:T(8,128)(2,1)S(1)}, u32[]{:S(2)}, u32[]{:S(2)}) %collective-permute-start) | collective-permute-done | bytes 32800 | tf_op jit(solution)/shard_map/ppermute | solution.py:593
  20.5 7.3 %collective-permute-done.1.refs_2_ = bf16[2,64,128]{2,1,0:T(8,128)(2,1)S(1)} collective-permute-done((bf16[2,64,128]{2,1,0:T(8,128)(2,1)S(1)}, bf16[2,64,128]{2,1,0:T(8,128)(2,1)S(1)}, u32[]{:S(2)}, u32[]{:S(2)}) %collective-permute-start.1) | collective-permute-done | bytes 32800 | tf_op jit(solution)/shard_map/ppermute | solution.py:593
  27.7 0.0 collective-permute-done.2.refs_3_
  27.7 0.0 copy-start.3
  27.7 2.5 %collective-permute-start.8 = (bf16[4,64,128]{2,1,0:T(8,128)(2,1)S(1)}, bf16[4,64,128]{2,1,0:T(8,128)(2,1)S(1)}, u32[]{:S(2)}, u32[]{:S(2)}) collective-permute-start(bf16[4,64,128]{2,1,0:T(8,128)(2,1)S(1)} %get-tuple-element.19), channel_id=1, source_target_pairs={{0,24},{4,28},{8,16},{12,20},{16,8},{20,12},{24,0},{28,4},{1,25},{... | collective-permute-start | bytes 196616 | tf_op jit(solution)/shard_map/ppermute | solution.py:593
  30.2 0.5 collective-permute-start.6
  30.7 0.6 %collective-permute-start.4 = (bf16[4,64,128]{2,1,0:T(8,128)(2,1)S(1)}, bf16[4,64,128]{2,1,0:T(8,128)(2,1)S(1)}, u32[]{:S(2)}, u32[]{:S(2)}) collective-permute-start(bf16[4,64,128]{2,1,0:T(8,128)(2,1)S(1)} %get-tuple-element.18.refs_0_), channel_id=1, source_target_pairs={{0,8},{4,12},{8,0},{12,4},{16,24},{20,28},{24,16},{28,20},{1,9},{5... | collective-permute-start | bytes 196616 | tf_op jit(solution)/shard_map/ppermute | solution.py:593
  31.3 2.0 %collective-permute-done.8.refs_6_ = bf16[4,64,128]{2,1,0:T(8,128)(2,1)S(1)} collective-permute-done((bf16[4,64,128]{2,1,0:T(8,128)(2,1)S(1)}, bf16[4,64,128]{2,1,0:T(8,128)(2,1)S(1)}, u32[]{:S(2)}, u32[]{:S(2)}) %collective-permute-start.8) | collective-permute-done | bytes 65568 | tf_op jit(solution)/shard_map/ppermute | solution.py:593
  33.3 1.1 %collective-permute-done.6.refs_4_ = bf16[4,64,128]{2,1,0:T(8,128)(2,1)S(1)} collective-permute-done((bf16[4,64,128]{2,1,0:T(8,128)(2,1)S(1)}, bf16[4,64,128]{2,1,0:T(8,128)(2,1)S(1)}, u32[]{:S(2)}, u32[]{:S(2)}) %collective-permute-start.6) | collective-permute-done | bytes 65568 | tf_op jit(solution)/shard_map/ppermute | solution.py:593
  34.5 0.5 collective-permute-done.4.refs_2_
  35.0 0.7 %collective-permute-done.7.refs_5_ = bf16[4,64,128]{2,1,0:T(8,128)(2,1)S(1)} collective-permute-done((bf16[4,64,128]{2,1,0:T(8,128)(2,1)S(1)}, bf16[4,64,128]{2,1,0:T(8,128)(2,1)S(1)}, u32[]{:S(2)}, u32[]{:S(2)}) %collective-permute-start.7) | collective-permute-done | bytes 65568 | tf_op jit(solution)/shard_map/ppermute | solution.py:593
  35.7 0.5 collective-permute-done.5.refs_3_
  36.3 1.3 %shard_map.70 = (bf16[2048,128]{1,0:T(8,128)(2,1)S(1)}, f32[1,256,1024]{2,1,0:T(8,128)S(1)}, f32[128,128]{1,0:T(8,128)S(1)}, f32[128,128]{1,0:T(8,128)S(1)}) custom-call(s32[16]{0:T(128)S(1)} %copy-done.3, f32[2,128,128]{2,1,0:T(8,128)S(1)} %copy-done.1, f32[8,128,128]{2,1,0:T(8,128)S(1)} %copy-done, bf16[4,64,128]{2,1,0:T(8,128)(2,1)S(1)} %get-tuple-element.18.refs_0_, ...), custom_call_target="tpu_custom_call" | custom-call | flops 201326592 | bytes 3145728 | tf_op jit(solution)/shard_map/pallas_call | solution.py:630
  37.6 6.9 %shard_map.71 = bf16[384,128]{1,0:T(8,128)(2,1)S(1)} custom-call(s32[16]{0:T(128)S(1)} %copy-done.3, bf16[32,64,128]{2,1,0:T(8,128)(2,1)S(1)} %all-to-all-done.arrived_ref, f32[128,128]{1,0:T(8,128)S(1)} %get-tuple-element.20.query_weights_ref, f32[128,128]{1,0:T(8,128)S(1)} %get-tuple-element.21.key_weights_ref, ...), custom_call_target="tpu_custom_call" | custom-call | tf_op jit(solution)/shard_map/pallas_call | solution.py:647
  44.5 10.4 %all-gather = bf16[3072,128]{1,0:T(8,128)(2,1)S(1)} all-gather(bf16[384,128]{1,0:T(8,128)(2,1)S(1)} %shard_map.71), channel_id=2, replica_groups=mesh['seq'=8,'head'=4] {'seq'}, dimensions={0}, use_global_device_ids=true | all-gather | bytes 884736 | tf_op jit(solution)/shard_map/all_gather | solution.py:667
  54.9 0.9 %shard_map.72 = (f32[8,128,128]{2,1,0:T(8,128)}, f32[2,128,128]{2,1,0:T(8,128)}) custom-call(bf16[8,384,128]{2,1,0:T(8,128)(2,1)S(1)} %bitcast.1), custom_call_target="tpu_custom_call" | custom-call | tf_op jit(solution)/shard_map/pallas_call | solution.py:668
  (18 shorter events, 0.0 us)
Async XLA Ops:
  2.9 7.4 %copy-start.6 = (bf16[2,64,128]{2,1,0:T(8,128)(2,1)S(1)}, bf16[2,64,128]{2,1,0:T(8,128)(2,1)}, u32[]{:S(2)}) copy-start(bf16[2,64,128]{2,1,0:T(8,128)(2,1)} %get-tuple-element.15) | copy-start | bytes 98308
  2.9 9.2 %copy-start.5 = (bf16[2,64,128]{2,1,0:T(8,128)(2,1)S(1)}, bf16[2,64,128]{2,1,0:T(8,128)(2,1)}, u32[]{:S(2)}) copy-start(bf16[2,64,128]{2,1,0:T(8,128)(2,1)} %get-tuple-element.16) | copy-start | bytes 98308
  2.9 11.7 %copy-start.4 = (bf16[2,64,128]{2,1,0:T(8,128)(2,1)S(1)}, bf16[2,64,128]{2,1,0:T(8,128)(2,1)}, u32[]{:S(2)}) copy-start(bf16[2,64,128]{2,1,0:T(8,128)(2,1)} %get-tuple-element.17) | copy-start | bytes 98308
  2.9 24.8 %copy-start.2 = (bf16[2,64,128]{2,1,0:T(8,128)(2,1)S(1)}, bf16[2,64,128]{2,1,0:T(8,128)(2,1)}, u32[]{:S(2)}) copy-start(bf16[2,64,128]{2,1,0:T(8,128)(2,1)} %get-tuple-element.14.refs_0_) | copy-start | bytes 98308
  2.9 33.3 %copy-start = (f32[8,128,128]{2,1,0:T(8,128)S(1)}, f32[8,128,128]{2,1,0:T(8,128)}, u32[]{:S(2)}) copy-start(f32[8,128,128]{2,1,0:T(8,128)} %query_map_ref.1) | copy-start | bytes 1572868
  2.9 34.6 %all-to-all-start = ((bf16[32,64,128]{2,1,0:T(8,128)(2,1)}), bf16[32,64,128]{2,1,0:T(8,128)(2,1)S(1)}, u32[]{:S(2)}, u32[]{:S(2)}) async-start(bf16[32,64,128]{2,1,0:T(8,128)(2,1)} %get-tuple-element.13), calls=%async_computation | async-start | bytes 1048576 | tf_op jit(solution)/shard_map/all_to_all | solution.py:614
  10.3 26.0 %copy-start.1 = (f32[2,128,128]{2,1,0:T(8,128)S(1)}, f32[2,128,128]{2,1,0:T(8,128)}, u32[]{:S(2)}) copy-start(f32[2,128,128]{2,1,0:T(8,128)} %key_map_ref.1) | copy-start | bytes 393220
  10.3 10.2 %collective-permute-start = (bf16[2,64,128]{2,1,0:T(8,128)(2,1)S(1)}, bf16[2,64,128]{2,1,0:T(8,128)(2,1)S(1)}, u32[]{:S(2)}, u32[]{:S(2)}) collective-permute-start(bf16[2,64,128]{2,1,0:T(8,128)(2,1)S(1)} %copy-done.6), channel_id=1, source_target_pairs={{0,1},{1,0},{2,3},{3,2},{4,5},{5,4},{6,7},{7,6},{8,9},{9,8},{10,11... | collective-permute-start | bytes 98312 | tf_op jit(solution)/shard_map/ppermute | solution.py:593
  12.1 15.6 %collective-permute-start.1 = (bf16[2,64,128]{2,1,0:T(8,128)(2,1)S(1)}, bf16[2,64,128]{2,1,0:T(8,128)(2,1)S(1)}, u32[]{:S(2)}, u32[]{:S(2)}) collective-permute-start(bf16[2,64,128]{2,1,0:T(8,128)(2,1)S(1)} %copy-done.5), channel_id=1, source_target_pairs={{0,2},{1,3},{2,0},{3,1},{4,6},{5,7},{6,4},{7,5},{8,10},{9,11},{10,... | collective-permute-start | bytes 98312 | tf_op jit(solution)/shard_map/ppermute | solution.py:593
  14.6 13.2 %collective-permute-start.2 = (bf16[2,64,128]{2,1,0:T(8,128)(2,1)S(1)}, bf16[2,64,128]{2,1,0:T(8,128)(2,1)S(1)}, u32[]{:S(2)}, u32[]{:S(2)}) collective-permute-start(bf16[2,64,128]{2,1,0:T(8,128)(2,1)S(1)} %copy-done.4), channel_id=1, source_target_pairs={{0,3},{1,2},{2,1},{3,0},{4,7},{5,6},{6,5},{7,4},{8,11},{9,10},{10,... | collective-permute-start | bytes 98312 | tf_op jit(solution)/shard_map/ppermute | solution.py:593
  27.7 8.5 %copy-start.3 = (s32[16]{0:T(128)S(1)}, s32[16]{0:T(128)}, u32[]{:S(2)}) copy-start(s32[16]{0:T(128)} %pos_ref.3) | copy-start | bytes 196
  27.7 5.6 %collective-permute-start.8 = (bf16[4,64,128]{2,1,0:T(8,128)(2,1)S(1)}, bf16[4,64,128]{2,1,0:T(8,128)(2,1)S(1)}, u32[]{:S(2)}, u32[]{:S(2)}) collective-permute-start(bf16[4,64,128]{2,1,0:T(8,128)(2,1)S(1)} %get-tuple-element.19), channel_id=1, source_target_pairs={{0,24},{4,28},{8,16},{12,20},{16,8},{20,12},{24,0},{28,4},{1,25},{... | collective-permute-start | bytes 196616 | tf_op jit(solution)/shard_map/ppermute | solution.py:593
  30.2 4.3 %collective-permute-start.6 = (bf16[4,64,128]{2,1,0:T(8,128)(2,1)S(1)}, bf16[4,64,128]{2,1,0:T(8,128)(2,1)S(1)}, u32[]{:S(2)}, u32[]{:S(2)}) collective-permute-start(bf16[4,64,128]{2,1,0:T(8,128)(2,1)S(1)} %get-tuple-element.19), channel_id=1, source_target_pairs={{0,16},{4,20},{8,24},{12,28},{16,0},{20,4},{24,8},{28,12},{1,17},{... | collective-permute-start | bytes 196616 | tf_op jit(solution)/shard_map/ppermute | solution.py:593
  30.7 4.3 %collective-permute-start.4 = (bf16[4,64,128]{2,1,0:T(8,128)(2,1)S(1)}, bf16[4,64,128]{2,1,0:T(8,128)(2,1)S(1)}, u32[]{:S(2)}, u32[]{:S(2)}) collective-permute-start(bf16[4,64,128]{2,1,0:T(8,128)(2,1)S(1)} %get-tuple-element.18.refs_0_), channel_id=1, source_target_pairs={{0,8},{4,12},{8,0},{12,4},{16,24},{20,28},{24,16},{28,20},{1,9},{5... | collective-permute-start | bytes 196616 | tf_op jit(solution)/shard_map/ppermute | solution.py:593
  31.3 3.7 %collective-permute-start.3 = (bf16[4,64,128]{2,1,0:T(8,128)(2,1)S(1)}, bf16[4,64,128]{2,1,0:T(8,128)(2,1)S(1)}, u32[]{:S(2)}, u32[]{:S(2)}) collective-permute-start(bf16[4,64,128]{2,1,0:T(8,128)(2,1)S(1)} %get-tuple-element.18.refs_0_), channel_id=1, source_target_pairs={{0,4},{4,0},{8,12},{12,8},{16,20},{20,16},{24,28},{28,24},{1,5},{5... | collective-permute-start | bytes 196616 | tf_op jit(solution)/shard_map/ppermute | solution.py:593
  33.3 1.7 %collective-permute-start.9 = (bf16[4,64,128]{2,1,0:T(8,128)(2,1)S(1)}, bf16[4,64,128]{2,1,0:T(8,128)(2,1)S(1)}, u32[]{:S(2)}, u32[]{:S(2)}) collective-permute-start(bf16[4,64,128]{2,1,0:T(8,128)(2,1)S(1)} %collective-permute-done.8.refs_6_), channel_id=1, source_target_pairs={{0,4},{4,0},{8,12},{12,8},{16,20},{20,16},{24,28},{28,24},{1,5},{5... | collective-permute-start | bytes 196616 | tf_op jit(solution)/shard_map/ppermute | solution.py:593
  34.5 1.3 %collective-permute-start.7 = (bf16[4,64,128]{2,1,0:T(8,128)(2,1)S(1)}, bf16[4,64,128]{2,1,0:T(8,128)(2,1)S(1)}, u32[]{:S(2)}, u32[]{:S(2)}) collective-permute-start(bf16[4,64,128]{2,1,0:T(8,128)(2,1)S(1)} %collective-permute-done.6.refs_4_), channel_id=1, source_target_pairs={{0,4},{4,0},{8,12},{12,8},{16,20},{20,16},{24,28},{28,24},{1,5},{5... | collective-permute-start | bytes 196616 | tf_op jit(solution)/shard_map/ppermute | solution.py:593
  35.0 1.3 %collective-permute-start.5 = (bf16[4,64,128]{2,1,0:T(8,128)(2,1)S(1)}, bf16[4,64,128]{2,1,0:T(8,128)(2,1)S(1)}, u32[]{:S(2)}, u32[]{:S(2)}) collective-permute-start(bf16[4,64,128]{2,1,0:T(8,128)(2,1)S(1)} %collective-permute-done.4.refs_2_), channel_id=1, source_target_pairs={{0,4},{4,0},{8,12},{12,8},{16,20},{20,16},{24,28},{28,24},{1,5},{5... | collective-permute-start | bytes 196616 | tf_op jit(solution)/shard_map/ppermute | solution.py:593

commit v9 on v8

--- a/solution.py
+++ b/solution.py
@@ -382,7 +382,7 @@
     def query_features(seq, at, logits):
         feature = features_t(logits)
         phi_q[seq, :, block(at)] = feature
-        phi_qb[seq, at] = feature.astype(BF16)
+        phi_qb[seq, at] = feature.astype(BF16) * token_count
 
     def phi_k(seq, at):
         if seq < early:
@@ -448,8 +448,8 @@
             total = tile_sum(exponent)
             denominator = total if number == 0 else denominator + total
         denominator = jnp.sum(denominator, axis=0, keepdims=True)
-        base = 1.0 / (linear_sum * token_count)
-        rate = 1.0 / (denominator * token_count)
+        base = 1.0 / linear_sum
+        rate = 1.0 / denominator
         for number in range(at + 1):
             exponent = scores[seq, slot, block(number), block(half)]
             weights = base - exponent * rate / linears[seq, slot, block(number), block(half)]
@@ -543,11 +543,11 @@
             if 0 <= turn - number < sequences
         ]
         while active:
-            for step in list(active):
+            for step in active[::-1]:
                 if next(step, step) is step:
                     active.remove(step)
     out_ref[:HEAD_SIZE, :] = acc_q[...].T.astype(BF16)
-    out_ref[HEAD_SIZE:, :] = bf16_parts(acc_k[...].T, 2)
+    out_ref[HEAD_SIZE:, :] = bf16_parts(acc_k[...].T * (1.0 / token_count), 2)
 
 
 def collect_kernel(everyone_ref, queries_out_ref, keys_out_ref, buffer, sems):

time: 56.1 us -> 56.1 us (level)
  no operation moved by 1% of the time
where the time goes in v9:
time: 56.1 us; the launch traced here: 55.8 us
  waiting for transfers between devices  17.9 us (32%)
  starting transfers between devices  15.3 us (27%)
  Pallas kernels  11.4 us (20%)
  blocking collectives  10.4 us (19%)
  between operations  0.75 us (1%)
    ppermute x10, waiting for transfers between devices, swap(): return lax.ppermute(piece, axis, [(i, i ^ bits) for i in range(size)])  17.9 us
    all_gather x1, blocking collectives, per_device_head(): everyone = lax.all_gather(grads, 'seq', axis=0, tiled=False)  10.4 us
    ppermute x10, starting transfers between devices, swap(): return lax.ppermute(piece, axis, [(i, i ^ bits) for i in range(size)])  8.02 us
    all_to_all x1, starting transfers between devices, per_device_head(): lax.all_to_all(sent, ('seq', 'head'), split_axis=0, concat_axis=0, tiled=...  7.33 us
    pallas_call x1, Pallas kernels, per_device_head(): pl.pallas_call(functools.partial(pair_kernel, token_count, seq_count), ou...  6.93 us
    pallas_call x1, Pallas kernels, per_device_head(): pl.pallas_call(functools.partial(send_kernel, seq_count), out_shape=[jax....  2.26 us
    pallas_call x1, Pallas kernels, per_device_head(): pl.pallas_call(functools.partial(key_kernel, share), out_shape=(jax.Shape...  1.28 us
  transfers between devices with their start and end apart: 11, of which 7 were waited for; matrix products, arithmetic and copies ran while one was open for 0% of the time, Pallas kernels for 2%

profile of v9, /device:TPU:0, one launch (start us, length us, event | category | flops | bytes accessed | tf_op | source)
XLA Modules:
  0.0 55.8 jit_solution(10394678247933534867)
XLA Ops:
  0.6 2.3 %shard_map.68 = (bf16[32,64,128]{2,1,0:T(8,128)(2,1)}, bf16[2,64,128]{2,1,0:T(8,128)(2,1)}, bf16[2,64,128]{2,1,0:T(8,128)(2,1)}, bf16[2,64,128]{2,1,0:T(8,128)(2,1)}, bf16[2,64,128]{2,1,0:T(8,128)(2,1)}) custom-call(bf16[64,4096]{1,0:T(8,128)(2,1)} %queries_ref.1, bf16[64,1024]{1,0:T(8,128)(2,1)} %keys_ref.1), custom_call_target="tpu_custom_call" | custom-call | tf_op jit(solution)/shard_map/pallas_call | solution.py:597
  2.9 0.0 copy-start.2
  2.9 0.0 copy-start
  2.9 7.3 %all-to-all-start = ((bf16[32,64,128]{2,1,0:T(8,128)(2,1)}), bf16[32,64,128]{2,1,0:T(8,128)(2,1)S(1)}, u32[]{:S(2)}, u32[]{:S(2)}) async-start(bf16[32,64,128]{2,1,0:T(8,128)(2,1)} %get-tuple-element.13), calls=%async_computation | async-start | bytes 1048576 | tf_op jit(solution)/shard_map/all_to_all | solution.py:614
  10.3 0.0 copy-start.1
  10.3 1.8 %collective-permute-start = (bf16[2,64,128]{2,1,0:T(8,128)(2,1)S(1)}, bf16[2,64,128]{2,1,0:T(8,128)(2,1)S(1)}, u32[]{:S(2)}, u32[]{:S(2)}) collective-permute-start(bf16[2,64,128]{2,1,0:T(8,128)(2,1)S(1)} %copy-done.6), channel_id=1, source_target_pairs={{0,1},{1,0},{2,3},{3,2},{4,5},{5,4},{6,7},{7,6},{8,9},{9,8},{10,11... | collective-permute-start | bytes 98312 | tf_op jit(solution)/shard_map/ppermute | solution.py:593
  12.1 2.4 %collective-permute-start.1 = (bf16[2,64,128]{2,1,0:T(8,128)(2,1)S(1)}, bf16[2,64,128]{2,1,0:T(8,128)(2,1)S(1)}, u32[]{:S(2)}, u32[]{:S(2)}) collective-permute-start(bf16[2,64,128]{2,1,0:T(8,128)(2,1)S(1)} %copy-done.5), channel_id=1, source_target_pairs={{0,2},{1,3},{2,0},{3,1},{4,6},{5,7},{6,4},{7,5},{8,10},{9,11},{10,... | collective-permute-start | bytes 98312 | tf_op jit(solution)/shard_map/ppermute | solution.py:593
  14.6 0.2 collective-permute-start.2
  14.8 5.7 %collective-permute-done.refs_1_ = bf16[2,64,128]{2,1,0:T(8,128)(2,1)S(1)} collective-permute-done((bf16[2,64,128]{2,1,0:T(8,128)(2,1)S(1)}, bf16[2,64,128]{2,1,0:T(8,128)(2,1)S(1)}, u32[]{:S(2)}, u32[]{:S(2)}) %collective-permute-start) | collective-permute-done | bytes 32800 | tf_op jit(solution)/shard_map/ppermute | solution.py:593
  20.5 7.3 %collective-permute-done.1.refs_2_ = bf16[2,64,128]{2,1,0:T(8,128)(2,1)S(1)} collective-permute-done((bf16[2,64,128]{2,1,0:T(8,128)(2,1)S(1)}, bf16[2,64,128]{2,1,0:T(8,128)(2,1)S(1)}, u32[]{:S(2)}, u32[]{:S(2)}) %collective-permute-start.1) | collective-permute-done | bytes 32800 | tf_op jit(solution)/shard_map/ppermute | solution.py:593
  27.7 0.0 collective-permute-done.2.refs_3_
  27.7 0.0 copy-start.3
  27.7 2.5 %collective-permute-start.8 = (bf16[4,64,128]{2,1,0:T(8,128)(2,1)S(1)}, bf16[4,64,128]{2,1,0:T(8,128)(2,1)S(1)}, u32[]{:S(2)}, u32[]{:S(2)}) collective-permute-start(bf16[4,64,128]{2,1,0:T(8,128)(2,1)S(1)} %get-tuple-element.19), channel_id=1, source_target_pairs={{0,24},{4,28},{8,16},{12,20},{16,8},{20,12},{24,0},{28,4},{1,25},{... | collective-permute-start | bytes 196616 | tf_op jit(solution)/shard_map/ppermute | solution.py:593
  30.2 0.5 collective-permute-start.6
  30.7 0.6 %collective-permute-start.4 = (bf16[4,64,128]{2,1,0:T(8,128)(2,1)S(1)}, bf16[4,64,128]{2,1,0:T(8,128)(2,1)S(1)}, u32[]{:S(2)}, u32[]{:S(2)}) collective-permute-start(bf16[4,64,128]{2,1,0:T(8,128)(2,1)S(1)} %get-tuple-element.18.refs_0_), channel_id=1, source_target_pairs={{0,8},{4,12},{8,0},{12,4},{16,24},{20,28},{24,16},{28,20},{1,9},{5... | collective-permute-start | bytes 196616 | tf_op jit(solution)/shard_map/ppermute | solution.py:593
  31.3 2.0 %collective-permute-done.8.refs_6_ = bf16[4,64,128]{2,1,0:T(8,128)(2,1)S(1)} collective-permute-done((bf16[4,64,128]{2,1,0:T(8,128)(2,1)S(1)}, bf16[4,64,128]{2,1,0:T(8,128)(2,1)S(1)}, u32[]{:S(2)}, u32[]{:S(2)}) %collective-permute-start.8) | collective-permute-done | bytes 65568 | tf_op jit(solution)/shard_map/ppermute | solution.py:593
  33.3 1.1 %collective-permute-done.6.refs_4_ = bf16[4,64,128]{2,1,0:T(8,128)(2,1)S(1)} collective-permute-done((bf16[4,64,128]{2,1,0:T(8,128)(2,1)S(1)}, bf16[4,64,128]{2,1,0:T(8,128)(2,1)S(1)}, u32[]{:S(2)}, u32[]{:S(2)}) %collective-permute-start.6) | collective-permute-done | bytes 65568 | tf_op jit(solution)/shard_map/ppermute | solution.py:593
  34.5 0.5 collective-permute-done.4.refs_2_
  35.0 0.7 %collective-permute-done.7.refs_5_ = bf16[4,64,128]{2,1,0:T(8,128)(2,1)S(1)} collective-permute-done((bf16[4,64,128]{2,1,0:T(8,128)(2,1)S(1)}, bf16[4,64,128]{2,1,0:T(8,128)(2,1)S(1)}, u32[]{:S(2)}, u32[]{:S(2)}) %collective-permute-start.7) | collective-permute-done | bytes 65568 | tf_op jit(solution)/shard_map/ppermute | solution.py:593
  35.7 0.5 collective-permute-done.5.refs_3_
  36.3 1.3 %shard_map.70 = (bf16[2048,128]{1,0:T(8,128)(2,1)S(1)}, f32[1,256,1024]{2,1,0:T(8,128)S(1)}, f32[128,128]{1,0:T(8,128)S(1)}, f32[128,128]{1,0:T(8,128)S(1)}) custom-call(s32[16]{0:T(128)S(1)} %copy-done.3, f32[2,128,128]{2,1,0:T(8,128)S(1)} %copy-done.1, f32[8,128,128]{2,1,0:T(8,128)S(1)} %copy-done, bf16[4,64,128]{2,1,0:T(8,128)(2,1)S(1)} %get-tuple-element.18.refs_0_, ...), custom_call_target="tpu_custom_call" | custom-call | flops 201326592 | bytes 3145728 | tf_op jit(solution)/shard_map/pallas_call | solution.py:630
  37.6 6.9 %shard_map.71 = bf16[384,128]{1,0:T(8,128)(2,1)S(1)} custom-call(s32[16]{0:T(128)S(1)} %copy-done.3, bf16[32,64,128]{2,1,0:T(8,128)(2,1)S(1)} %all-to-all-done.arrived_ref, f32[128,128]{1,0:T(8,128)S(1)} %get-tuple-element.20.query_weights_ref, f32[128,128]{1,0:T(8,128)S(1)} %get-tuple-element.21.key_weights_ref, ...), custom_call_target="tpu_custom_call" | custom-call | tf_op jit(solution)/shard_map/pallas_call | solution.py:647
  44.5 10.4 %all-gather = bf16[3072,128]{1,0:T(8,128)(2,1)S(1)} all-gather(bf16[384,128]{1,0:T(8,128)(2,1)S(1)} %shard_map.71), channel_id=2, replica_groups=mesh['seq'=8,'head'=4] {'seq'}, dimensions={0}, use_global_device_ids=true | all-gather | bytes 884736 | tf_op jit(solution)/shard_map/all_gather | solution.py:667
  54.9 0.9 %shard_map.72 = (f32[8,128,128]{2,1,0:T(8,128)}, f32[2,128,128]{2,1,0:T(8,128)}) custom-call(bf16[8,384,128]{2,1,0:T(8,128)(2,1)S(1)} %bitcast.1), custom_call_target="tpu_custom_call" | custom-call | tf_op jit(solution)/shard_map/pallas_call | solution.py:668
  (18 shorter events, 0.0 us)
Async XLA Ops:
  2.9 7.4 %copy-start.6 = (bf16[2,64,128]{2,1,0:T(8,128)(2,1)S(1)}, bf16[2,64,128]{2,1,0:T(8,128)(2,1)}, u32[]{:S(2)}) copy-start(bf16[2,64,128]{2,1,0:T(8,128)(2,1)} %get-tuple-element.15) | copy-start | bytes 98308
  2.9 9.2 %copy-start.5 = (bf16[2,64,128]{2,1,0:T(8,128)(2,1)S(1)}, bf16[2,64,128]{2,1,0:T(8,128)(2,1)}, u32[]{:S(2)}) copy-start(bf16[2,64,128]{2,1,0:T(8,128)(2,1)} %get-tuple-element.16) | copy-start | bytes 98308
  2.9 11.7 %copy-start.4 = (bf16[2,64,128]{2,1,0:T(8,128)(2,1)S(1)}, bf16[2,64,128]{2,1,0:T(8,128)(2,1)}, u32[]{:S(2)}) copy-start(bf16[2,64,128]{2,1,0:T(8,128)(2,1)} %get-tuple-element.17) | copy-start | bytes 98308
  2.9 24.8 %copy-start.2 = (bf16[2,64,128]{2,1,0:T(8,128)(2,1)S(1)}, bf16[2,64,128]{2,1,0:T(8,128)(2,1)}, u32[]{:S(2)}) copy-start(bf16[2,64,128]{2,1,0:T(8,128)(2,1)} %get-tuple-element.14.refs_0_) | copy-start | bytes 98308
  2.9 33.3 %copy-start = (f32[8,128,128]{2,1,0:T(8,128)S(1)}, f32[8,128,128]{2,1,0:T(8,128)}, u32[]{:S(2)}) copy-start(f32[8,128,128]{2,1,0:T(8,128)} %query_map_ref.1) | copy-start | bytes 1572868
  2.9 34.6 %all-to-all-start = ((bf16[32,64,128]{2,1,0:T(8,128)(2,1)}), bf16[32,64,128]{2,1,0:T(8,128)(2,1)S(1)}, u32[]{:S(2)}, u32[]{:S(2)}) async-start(bf16[32,64,128]{2,1,0:T(8,128)(2,1)} %get-tuple-element.13), calls=%async_computation | async-start | bytes 1048576 | tf_op jit(solution)/shard_map/all_to_all | solution.py:614
  10.3 26.0 %copy-start.1 = (f32[2,128,128]{2,1,0:T(8,128)S(1)}, f32[2,128,128]{2,1,0:T(8,128)}, u32[]{:S(2)}) copy-start(f32[2,128,128]{2,1,0:T(8,128)} %key_map_ref.1) | copy-start | bytes 393220
  10.3 10.2 %collective-permute-start = (bf16[2,64,128]{2,1,0:T(8,128)(2,1)S(1)}, bf16[2,64,128]{2,1,0:T(8,128)(2,1)S(1)}, u32[]{:S(2)}, u32[]{:S(2)}) collective-permute-start(bf16[2,64,128]{2,1,0:T(8,128)(2,1)S(1)} %copy-done.6), channel_id=1, source_target_pairs={{0,1},{1,0},{2,3},{3,2},{4,5},{5,4},{6,7},{7,6},{8,9},{9,8},{10,11... | collective-permute-start | bytes 98312 | tf_op jit(solution)/shard_map/ppermute | solution.py:593
  12.1 15.6 %collective-permute-start.1 = (bf16[2,64,128]{2,1,0:T(8,128)(2,1)S(1)}, bf16[2,64,128]{2,1,0:T(8,128)(2,1)S(1)}, u32[]{:S(2)}, u32[]{:S(2)}) collective-permute-start(bf16[2,64,128]{2,1,0:T(8,128)(2,1)S(1)} %copy-done.5), channel_id=1, source_target_pairs={{0,2},{1,3},{2,0},{3,1},{4,6},{5,7},{6,4},{7,5},{8,10},{9,11},{10,... | collective-permute-start | bytes 98312 | tf_op jit(solution)/shard_map/ppermute | solution.py:593
  14.6 13.2 %collective-permute-start.2 = (bf16[2,64,128]{2,1,0:T(8,128)(2,1)S(1)}, bf16[2,64,128]{2,1,0:T(8,128)(2,1)S(1)}, u32[]{:S(2)}, u32[]{:S(2)}) collective-permute-start(bf16[2,64,128]{2,1,0:T(8,128)(2,1)S(1)} %copy-done.4), channel_id=1, source_target_pairs={{0,3},{1,2},{2,1},{3,0},{4,7},{5,6},{6,5},{7,4},{8,11},{9,10},{10,... | collective-permute-start | bytes 98312 | tf_op jit(solution)/shard_map/ppermute | solution.py:593
  27.7 8.5 %copy-start.3 = (s32[16]{0:T(128)S(1)}, s32[16]{0:T(128)}, u32[]{:S(2)}) copy-start(s32[16]{0:T(128)} %pos_ref.3) | copy-start | bytes 196
  27.7 5.6 %collective-permute-start.8 = (bf16[4,64,128]{2,1,0:T(8,128)(2,1)S(1)}, bf16[4,64,128]{2,1,0:T(8,128)(2,1)S(1)}, u32[]{:S(2)}, u32[]{:S(2)}) collective-permute-start(bf16[4,64,128]{2,1,0:T(8,128)(2,1)S(1)} %get-tuple-element.19), channel_id=1, source_target_pairs={{0,24},{4,28},{8,16},{12,20},{16,8},{20,12},{24,0},{28,4},{1,25},{... | collective-permute-start | bytes 196616 | tf_op jit(solution)/shard_map/ppermute | solution.py:593
  30.2 4.3 %collective-permute-start.6 = (bf16[4,64,128]{2,1,0:T(8,128)(2,1)S(1)}, bf16[4,64,128]{2,1,0:T(8,128)(2,1)S(1)}, u32[]{:S(2)}, u32[]{:S(2)}) collective-permute-start(bf16[4,64,128]{2,1,0:T(8,128)(2,1)S(1)} %get-tuple-element.19), channel_id=1, source_target_pairs={{0,16},{4,20},{8,24},{12,28},{16,0},{20,4},{24,8},{28,12},{1,17},{... | collective-permute-start | bytes 196616 | tf_op jit(solution)/shard_map/ppermute | solution.py:593
  30.7 4.3 %collective-permute-start.4 = (bf16[4,64,128]{2,1,0:T(8,128)(2,1)S(1)}, bf16[4,64,128]{2,1,0:T(8,128)(2,1)S(1)}, u32[]{:S(2)}, u32[]{:S(2)}) collective-permute-start(bf16[4,64,128]{2,1,0:T(8,128)(2,1)S(1)} %get-tuple-element.18.refs_0_), channel_id=1, source_target_pairs={{0,8},{4,12},{8,0},{12,4},{16,24},{20,28},{24,16},{28,20},{1,9},{5... | collective-permute-start | bytes 196616 | tf_op jit(solution)/shard_map/ppermute | solution.py:593
  31.3 3.7 %collective-permute-start.3 = (bf16[4,64,128]{2,1,0:T(8,128)(2,1)S(1)}, bf16[4,64,128]{2,1,0:T(8,128)(2,1)S(1)}, u32[]{:S(2)}, u32[]{:S(2)}) collective-permute-start(bf16[4,64,128]{2,1,0:T(8,128)(2,1)S(1)} %get-tuple-element.18.refs_0_), channel_id=1, source_target_pairs={{0,4},{4,0},{8,12},{12,8},{16,20},{20,16},{24,28},{28,24},{1,5},{5... | collective-permute-start | bytes 196616 | tf_op jit(solution)/shard_map/ppermute | solution.py:593
  33.3 1.7 %collective-permute-start.9 = (bf16[4,64,128]{2,1,0:T(8,128)(2,1)S(1)}, bf16[4,64,128]{2,1,0:T(8,128)(2,1)S(1)}, u32[]{:S(2)}, u32[]{:S(2)}) collective-permute-start(bf16[4,64,128]{2,1,0:T(8,128)(2,1)S(1)} %collective-permute-done.8.refs_6_), channel_id=1, source_target_pairs={{0,4},{4,0},{8,12},{12,8},{16,20},{20,16},{24,28},{28,24},{1,5},{5... | collective-permute-start | bytes 196616 | tf_op jit(solution)/shard_map/ppermute | solution.py:593
  34.5 1.3 %collective-permute-start.7 = (bf16[4,64,128]{2,1,0:T(8,128)(2,1)S(1)}, bf16[4,64,128]{2,1,0:T(8,128)(2,1)S(1)}, u32[]{:S(2)}, u32[]{:S(2)}) collective-permute-start(bf16[4,64,128]{2,1,0:T(8,128)(2,1)S(1)} %collective-permute-done.6.refs_4_), channel_id=1, source_target_pairs={{0,4},{4,0},{8,12},{12,8},{16,20},{20,16},{24,28},{28,24},{1,5},{5... | collective-permute-start | bytes 196616 | tf_op jit(solution)/shard_map/ppermute | solution.py:593
  35.0 1.3 %collective-permute-start.5 = (bf16[4,64,128]{2,1,0:T(8,128)(2,1)S(1)}, bf16[4,64,128]{2,1,0:T(8,128)(2,1)S(1)}, u32[]{:S(2)}, u32[]{:S(2)}) collective-permute-start(bf16[4,64,128]{2,1,0:T(8,128)(2,1)S(1)} %collective-permute-done.4.refs_2_), channel_id=1, source_target_pairs={{0,4},{4,0},{8,12},{12,8},{16,20},{20,16},{24,28},{28,24},{1,5},{5... | collective-permute-start | bytes 196616 | tf_op jit(solution)/shard_map/ppermute | solution.py:593

commit v10 on v9

--- a/solution.py
+++ b/solution.py
@@ -303,7 +303,7 @@
 def key_kernel(share, pos_ref, key_map_ref, query_map_ref, *refs):
     seq_count, head_count = lax.axis_size("seq"), lax.axis_size("head")
     piece_refs, refs = refs[:seq_count], refs[seq_count:]
-    key_rows, phi, query_weights_ref, key_weights_ref = refs
+    key_rows, phi, phi_rows, query_weights_ref, key_weights_ref = refs
     rows = piece_refs[0].shape[1]
     seq_blocks = phi.shape[2] // BLK
     blocks = phi.shape[0] * seq_blocks
@@ -320,7 +320,11 @@
         while number + len(ahead) < min(number + 3, blocks):
             ahead.append(logits_t(parts, key_rows[block(number + len(ahead)), :]))
         seq, at = divmod(number, seq_blocks)
-        phi[seq, :, block(at)] = features_t(ahead.pop(0))
+        feature = features_t(ahead.pop(0))
+        phi[seq, :, block(at)] = feature
+        for half in range(2):
+            turned = feature[half * HEAD_SIZE : (half + 1) * HEAD_SIZE].T
+            phi_rows[seq, half, block(at), :] = turned.astype(BF16)
 
 
 def pair_kernel(
@@ -332,6 +336,7 @@
     key_weights_ref,
     key_rows,
     phi_k_early,
+    phi_kb_rows_early,
     out_ref,
     query_rows,
     phi_q,
@@ -401,16 +406,21 @@
     def turn_features(seq, at):
         feature = phi_k(seq, at)
         phi_kb[seq, at] = feature.astype(BF16)
-        for half in range(2):
+        for half in range(2 if seq >= early else 0):
             turned = feature[half * HEAD_SIZE : (half + 1) * HEAD_SIZE].T
-            phi_kb_rows[seq, half, block(at), :] = turned.astype(BF16)
+            phi_kb_rows[seq - early, half, block(at), :] = turned.astype(BF16)
+
+    def key_feature_rows(seq, half, stop):
+        if seq < early:
+            return phi_kb_rows_early[seq, half, :stop, :]
+        return phi_kb_rows[seq - early, half, :stop, :]
 
     def pair_scores(seq, tile):
         here = span(tile)
         slot = tile % 2
         teacher = nt(key_rows[flat(seq, slice(0, here.stop)), :], query_rows[flat(seq, here), :])
         student = nn(
-            side_by_side(phi_kb_rows[seq, half, : here.stop, :] for half in range(2)),
+            side_by_side(key_feature_rows(seq, half, here.stop) for half in range(2)),
             side_by_side(phi_qb[seq, at] for at in blocks_of(here)),
         )
         stats = []
@@ -627,16 +637,17 @@
         pieces[other + 1] = swap(pieces[other], "seq", 1)
     early = max(sequences // 2, 1)
     weights_shape = jax.ShapeDtypeStruct((HEAD_SIZE, HEAD_SIZE), F32)
-    key_rows, phi_k, query_weights, key_weights = pl.pallas_call(
+    key_rows, phi_k, phi_rows, query_weights, key_weights = pl.pallas_call(
         functools.partial(key_kernel, share),
         out_shape=(
             jax.ShapeDtypeStruct((token_count, HEAD_SIZE), BF16),
             jax.ShapeDtypeStruct((early, 2 * HEAD_SIZE, seq_tokens), F32),
+            jax.ShapeDtypeStruct((early, 2, seq_tokens, HEAD_SIZE), BF16),
             weights_shape,
             weights_shape,
         ),
         in_specs=[smem] + [vmem] * (seq_count + 2),
-        out_specs=(vmem,) * 4,
+        out_specs=(vmem,) * 5,
         compiler_params=pltpu.CompilerParams(vmem_limit_bytes=8 << 20),
         cost_estimate=pl.CostEstimate(
             flops=token_count * HEAD_SIZE * HEAD_SIZE * 6,
@@ -647,7 +658,7 @@
     grads = pl.pallas_call(
         functools.partial(pair_kernel, token_count, seq_count),
         out_shape=jax.ShapeDtypeStruct((3 * HEAD_SIZE, HEAD_SIZE), BF16),
-        in_specs=[smem] + [vmem] * 5,
+        in_specs=[smem] + [vmem] * 6,
         out_specs=vmem,
         scratch_shapes=[
             pltpu.VMEM((token_count, HEAD_SIZE), BF16),
@@ -655,7 +666,7 @@
             pltpu.VMEM((sequences, seq_count, 2 * HEAD_SIZE, BLK), BF16),
             pltpu.VMEM((max(sequences - early, 1), 2 * HEAD_SIZE, seq_tokens), F32),
             pltpu.VMEM((sequences, seq_count, 2 * HEAD_SIZE, BLK), BF16),
-            pltpu.VMEM((sequences, 2, seq_tokens, HEAD_SIZE), BF16),
+            pltpu.VMEM((max(sequences - early, 1), 2, seq_tokens, HEAD_SIZE), BF16),
             pltpu.VMEM((sequences, seq_count, seq_tokens, BLK), BF16),
             pltpu.VMEM((sequences, 2, seq_tokens, 2 * BLK), F32),
             pltpu.VMEM((sequences, 2, seq_tokens, 2 * BLK), F32),
@@ -663,7 +674,7 @@
             pltpu.VMEM((HEAD_SIZE, HEAD_SIZE), F32),
         ],
         compiler_params=pltpu.CompilerParams(vmem_limit_bytes=32 << 20),
-    )(block_pos, arrived, query_weights, key_weights, key_rows, phi_k)
+    )(block_pos, arrived, query_weights, key_weights, key_rows, phi_k, phi_rows)
     everyone = lax.all_gather(grads, "seq", axis=0, tiled=False)
     return pl.pallas_call(
         collect_kernel,

time: 56.1 us -> 55.9 us (level)
  transfers between devices with their start and end apart: 11 -> 11, of which waited for: 7 -> 7; matrix products, arithmetic and copies ran while one was open for 0% -> 0% of each run, Pallas kernels for 2% -> 3%
where the time goes in v10:
time: 55.9 us; the launch traced here: 55.7 us
  waiting for transfers between devices  17.9 us (32%)
  starting transfers between devices  15.3 us (27%)
  Pallas kernels  11.3 us (20%)
  blocking collectives  10.4 us (19%)
  between operations  0.75 us (1%)
    ppermute x10, waiting for transfers between devices, swap(): return lax.ppermute(piece, axis, [(i, i ^ bits) for i in range(size)])  17.9 us
    all_gather x1, blocking collectives, per_device_head(): everyone = lax.all_gather(grads, 'seq', axis=0, tiled=False)  10.4 us
    ppermute x10, starting transfers between devices, swap(): return lax.ppermute(piece, axis, [(i, i ^ bits) for i in range(size)])  8.02 us
    all_to_all x1, starting transfers between devices, per_device_head(): lax.all_to_all(sent, ('seq', 'head'), split_axis=0, concat_axis=0, tiled=...  7.33 us
    pallas_call x1, Pallas kernels, per_device_head(): pl.pallas_call(functools.partial(pair_kernel, token_count, seq_count), ou...  6.68 us
    pallas_call x1, Pallas kernels, per_device_head(): pl.pallas_call(functools.partial(send_kernel, seq_count), out_shape=[jax....  2.26 us
    pallas_call x1, Pallas kernels, per_device_head(): pl.pallas_call(functools.partial(key_kernel, share), out_shape=(jax.Shape...  1.41 us
  transfers between devices with their start and end apart: 11, of which 7 were waited for; matrix products, arithmetic and copies ran while one was open for 0% of the time, Pallas kernels for 3%

profile of v10, /device:TPU:0, one launch (start us, length us, event | category | flops | bytes accessed | tf_op | source)
XLA Modules:
  0.0 55.7 jit_solution(4570784225534509317)
XLA Ops:
  0.6 2.3 %shard_map.68 = (bf16[32,64,128]{2,1,0:T(8,128)(2,1)}, bf16[2,64,128]{2,1,0:T(8,128)(2,1)}, bf16[2,64,128]{2,1,0:T(8,128)(2,1)}, bf16[2,64,128]{2,1,0:T(8,128)(2,1)}, bf16[2,64,128]{2,1,0:T(8,128)(2,1)}) custom-call(bf16[64,4096]{1,0:T(8,128)(2,1)} %queries_ref.1, bf16[64,1024]{1,0:T(8,128)(2,1)} %keys_ref.1), custom_call_target="tpu_custom_call" | custom-call | tf_op jit(solution)/shard_map/pallas_call | solution.py:607
  2.9 0.0 copy-start.2
  2.9 0.0 copy-start
  2.9 7.3 %all-to-all-start = ((bf16[32,64,128]{2,1,0:T(8,128)(2,1)}), bf16[32,64,128]{2,1,0:T(8,128)(2,1)S(1)}, u32[]{:S(2)}, u32[]{:S(2)}) async-start(bf16[32,64,128]{2,1,0:T(8,128)(2,1)} %get-tuple-element.14), calls=%async_computation | async-start | bytes 1048576 | tf_op jit(solution)/shard_map/all_to_all | solution.py:624
  10.3 0.0 copy-start.1
  10.3 1.8 %collective-permute-start = (bf16[2,64,128]{2,1,0:T(8,128)(2,1)S(1)}, bf16[2,64,128]{2,1,0:T(8,128)(2,1)S(1)}, u32[]{:S(2)}, u32[]{:S(2)}) collective-permute-start(bf16[2,64,128]{2,1,0:T(8,128)(2,1)S(1)} %copy-done.6), channel_id=1, source_target_pairs={{0,1},{1,0},{2,3},{3,2},{4,5},{5,4},{6,7},{7,6},{8,9},{9,8},{10,11... | collective-permute-start | bytes 98312 | tf_op jit(solution)/shard_map/ppermute | solution.py:603
  12.1 2.4 %collective-permute-start.1 = (bf16[2,64,128]{2,1,0:T(8,128)(2,1)S(1)}, bf16[2,64,128]{2,1,0:T(8,128)(2,1)S(1)}, u32[]{:S(2)}, u32[]{:S(2)}) collective-permute-start(bf16[2,64,128]{2,1,0:T(8,128)(2,1)S(1)} %copy-done.5), channel_id=1, source_target_pairs={{0,2},{1,3},{2,0},{3,1},{4,6},{5,7},{6,4},{7,5},{8,10},{9,11},{10,... | collective-permute-start | bytes 98312 | tf_op jit(solution)/shard_map/ppermute | solution.py:603
  14.6 0.2 collective-permute-start.2
  14.8 5.7 %collective-permute-done.refs_1_ = bf16[2,64,128]{2,1,0:T(8,128)(2,1)S(1)} collective-permute-done((bf16[2,64,128]{2,1,0:T(8,128)(2,1)S(1)}, bf16[2,64,128]{2,1,0:T(8,128)(2,1)S(1)}, u32[]{:S(2)}, u32[]{:S(2)}) %collective-permute-start) | collective-permute-done | bytes 32800 | tf_op jit(solution)/shard_map/ppermute | solution.py:603
  20.5 7.3 %collective-permute-done.1.refs_2_ = bf16[2,64,128]{2,1,0:T(8,128)(2,1)S(1)} collective-permute-done((bf16[2,64,128]{2,1,0:T(8,128)(2,1)S(1)}, bf16[2,64,128]{2,1,0:T(8,128)(2,1)S(1)}, u32[]{:S(2)}, u32[]{:S(2)}) %collective-permute-start.1) | collective-permute-done | bytes 32800 | tf_op jit(solution)/shard_map/ppermute | solution.py:603
  27.7 0.0 collective-permute-done.2.refs_3_
  27.7 0.0 copy-start.3
  27.7 2.5 %collective-permute-start.8 = (bf16[4,64,128]{2,1,0:T(8,128)(2,1)S(1)}, bf16[4,64,128]{2,1,0:T(8,128)(2,1)S(1)}, u32[]{:S(2)}, u32[]{:S(2)}) collective-permute-start(bf16[4,64,128]{2,1,0:T(8,128)(2,1)S(1)} %get-tuple-element.20), channel_id=1, source_target_pairs={{0,24},{4,28},{8,16},{12,20},{16,8},{20,12},{24,0},{28,4},{1,25},{... | collective-permute-start | bytes 196616 | tf_op jit(solution)/shard_map/ppermute | solution.py:603
  30.2 0.5 collective-permute-start.6
  30.7 0.6 %collective-permute-start.4 = (bf16[4,64,128]{2,1,0:T(8,128)(2,1)S(1)}, bf16[4,64,128]{2,1,0:T(8,128)(2,1)S(1)}, u32[]{:S(2)}, u32[]{:S(2)}) collective-permute-start(bf16[4,64,128]{2,1,0:T(8,128)(2,1)S(1)} %get-tuple-element.19.refs_0_), channel_id=1, source_target_pairs={{0,8},{4,12},{8,0},{12,4},{16,24},{20,28},{24,16},{28,20},{1,9},{5... | collective-permute-start | bytes 196616 | tf_op jit(solution)/shard_map/ppermute | solution.py:603
  31.3 2.0 %collective-permute-done.8.refs_6_ = bf16[4,64,128]{2,1,0:T(8,128)(2,1)S(1)} collective-permute-done((bf16[4,64,128]{2,1,0:T(8,128)(2,1)S(1)}, bf16[4,64,128]{2,1,0:T(8,128)(2,1)S(1)}, u32[]{:S(2)}, u32[]{:S(2)}) %collective-permute-start.8) | collective-permute-done | bytes 65568 | tf_op jit(solution)/shard_map/ppermute | solution.py:603
  33.3 1.1 %collective-permute-done.6.refs_4_ = bf16[4,64,128]{2,1,0:T(8,128)(2,1)S(1)} collective-permute-done((bf16[4,64,128]{2,1,0:T(8,128)(2,1)S(1)}, bf16[4,64,128]{2,1,0:T(8,128)(2,1)S(1)}, u32[]{:S(2)}, u32[]{:S(2)}) %collective-permute-start.6) | collective-permute-done | bytes 65568 | tf_op jit(solution)/shard_map/ppermute | solution.py:603
  34.5 0.5 collective-permute-done.4.refs_2_
  35.0 0.7 %collective-permute-done.7.refs_5_ = bf16[4,64,128]{2,1,0:T(8,128)(2,1)S(1)} collective-permute-done((bf16[4,64,128]{2,1,0:T(8,128)(2,1)S(1)}, bf16[4,64,128]{2,1,0:T(8,128)(2,1)S(1)}, u32[]{:S(2)}, u32[]{:S(2)}) %collective-permute-start.7) | collective-permute-done | bytes 65568 | tf_op jit(solution)/shard_map/ppermute | solution.py:603
  35.7 0.5 collective-permute-done.5.refs_3_
  36.3 1.4 %shard_map.70 = (bf16[2048,128]{1,0:T(8,128)(2,1)S(1)}, f32[1,256,1024]{2,1,0:T(8,128)S(1)}, bf16[1,2,1024,128]{3,2,1,0:T(8,128)(2,1)S(1)}, f32[128,128]{1,0:T(8,128)S(1)}, f32[128,128]{1,0:T(8,128)S(1)}) custom-call(s32[16]{0:T(128)S(1)} %copy-done.3, f32[2,128,128]{2,1,0:T(8,128)S(1)} %copy-done.1, f32[8,128,128]{2,1,0:T(8,128)S(1)} %copy-done, ...), custom_call_target="tpu_custom_call" | custom-call | flops 201326592 | bytes 3145728 | tf_op jit(solution)/shard_map/pallas_call | solution.py:640
  37.7 6.7 %shard_map.71 = bf16[384,128]{1,0:T(8,128)(2,1)S(1)} custom-call(s32[16]{0:T(128)S(1)} %copy-done.3, bf16[32,64,128]{2,1,0:T(8,128)(2,1)S(1)} %all-to-all-done.arrived_ref, f32[128,128]{1,0:T(8,128)S(1)} %get-tuple-element.21.query_weights_ref, f32[128,128]{1,0:T(8,128)S(1)} %get-tuple-element.22.key_weights_ref, ...), custom_call_target="tpu_custom_call" | custom-call | tf_op jit(solution)/shard_map/pallas_call | solution.py:658
  44.4 10.4 %all-gather = bf16[3072,128]{1,0:T(8,128)(2,1)S(1)} all-gather(bf16[384,128]{1,0:T(8,128)(2,1)S(1)} %shard_map.71), channel_id=2, replica_groups=mesh['seq'=8,'head'=4] {'seq'}, dimensions={0}, use_global_device_ids=true | all-gather | bytes 884736 | tf_op jit(solution)/shard_map/all_gather | solution.py:678
  54.8 0.9 %shard_map.72 = (f32[8,128,128]{2,1,0:T(8,128)}, f32[2,128,128]{2,1,0:T(8,128)}) custom-call(bf16[8,384,128]{2,1,0:T(8,128)(2,1)S(1)} %bitcast.1), custom_call_target="tpu_custom_call" | custom-call | tf_op jit(solution)/shard_map/pallas_call | solution.py:679
  (18 shorter events, 0.0 us)
Async XLA Ops:
  2.9 7.4 %copy-start.6 = (bf16[2,64,128]{2,1,0:T(8,128)(2,1)S(1)}, bf16[2,64,128]{2,1,0:T(8,128)(2,1)}, u32[]{:S(2)}) copy-start(bf16[2,64,128]{2,1,0:T(8,128)(2,1)} %get-tuple-element.16) | copy-start | bytes 98308
  2.9 9.2 %copy-start.5 = (bf16[2,64,128]{2,1,0:T(8,128)(2,1)S(1)}, bf16[2,64,128]{2,1,0:T(8,128)(2,1)}, u32[]{:S(2)}) copy-start(bf16[2,64,128]{2,1,0:T(8,128)(2,1)} %get-tuple-element.17) | copy-start | bytes 98308
  2.9 11.7 %copy-start.4 = (bf16[2,64,128]{2,1,0:T(8,128)(2,1)S(1)}, bf16[2,64,128]{2,1,0:T(8,128)(2,1)}, u32[]{:S(2)}) copy-start(bf16[2,64,128]{2,1,0:T(8,128)(2,1)} %get-tuple-element.18) | copy-start | bytes 98308
  2.9 24.8 %copy-start.2 = (bf16[2,64,128]{2,1,0:T(8,128)(2,1)S(1)}, bf16[2,64,128]{2,1,0:T(8,128)(2,1)}, u32[]{:S(2)}) copy-start(bf16[2,64,128]{2,1,0:T(8,128)(2,1)} %get-tuple-element.15.refs_0_) | copy-start | bytes 98308
  2.9 33.3 %copy-start = (f32[8,128,128]{2,1,0:T(8,128)S(1)}, f32[8,128,128]{2,1,0:T(8,128)}, u32[]{:S(2)}) copy-start(f32[8,128,128]{2,1,0:T(8,128)} %query_map_ref.1) | copy-start | bytes 1572868
  2.9 34.7 %all-to-all-start = ((bf16[32,64,128]{2,1,0:T(8,128)(2,1)}), bf16[32,64,128]{2,1,0:T(8,128)(2,1)S(1)}, u32[]{:S(2)}, u32[]{:S(2)}) async-start(bf16[32,64,128]{2,1,0:T(8,128)(2,1)} %get-tuple-element.14), calls=%async_computation | async-start | bytes 1048576 | tf_op jit(solution)/shard_map/all_to_all | solution.py:624
  10.3 26.0 %copy-start.1 = (f32[2,128,128]{2,1,0:T(8,128)S(1)}, f32[2,128,128]{2,1,0:T(8,128)}, u32[]{:S(2)}) copy-start(f32[2,128,128]{2,1,0:T(8,128)} %key_map_ref.1) | copy-start | bytes 393220
  10.3 10.2 %collective-permute-start = (bf16[2,64,128]{2,1,0:T(8,128)(2,1)S(1)}, bf16[2,64,128]{2,1,0:T(8,128)(2,1)S(1)}, u32[]{:S(2)}, u32[]{:S(2)}) collective-permute-start(bf16[2,64,128]{2,1,0:T(8,128)(2,1)S(1)} %copy-done.6), channel_id=1, source_target_pairs={{0,1},{1,0},{2,3},{3,2},{4,5},{5,4},{6,7},{7,6},{8,9},{9,8},{10,11... | collective-permute-start | bytes 98312 | tf_op jit(solution)/shard_map/ppermute | solution.py:603
  12.1 15.6 %collective-permute-start.1 = (bf16[2,64,128]{2,1,0:T(8,128)(2,1)S(1)}, bf16[2,64,128]{2,1,0:T(8,128)(2,1)S(1)}, u32[]{:S(2)}, u32[]{:S(2)}) collective-permute-start(bf16[2,64,128]{2,1,0:T(8,128)(2,1)S(1)} %copy-done.5), channel_id=1, source_target_pairs={{0,2},{1,3},{2,0},{3,1},{4,6},{5,7},{6,4},{7,5},{8,10},{9,11},{10,... | collective-permute-start | bytes 98312 | tf_op jit(solution)/shard_map/ppermute | solution.py:603
  14.6 13.2 %collective-permute-start.2 = (bf16[2,64,128]{2,1,0:T(8,128)(2,1)S(1)}, bf16[2,64,128]{2,1,0:T(8,128)(2,1)S(1)}, u32[]{:S(2)}, u32[]{:S(2)}) collective-permute-start(bf16[2,64,128]{2,1,0:T(8,128)(2,1)S(1)} %copy-done.4), channel_id=1, source_target_pairs={{0,3},{1,2},{2,1},{3,0},{4,7},{5,6},{6,5},{7,4},{8,11},{9,10},{10,... | collective-permute-start | bytes 98312 | tf_op jit(solution)/shard_map/ppermute | solution.py:603
  27.7 8.5 %copy-start.3 = (s32[16]{0:T(128)S(1)}, s32[16]{0:T(128)}, u32[]{:S(2)}) copy-start(s32[16]{0:T(128)} %pos_ref.3) | copy-start | bytes 196
  27.7 5.6 %collective-permute-start.8 = (bf16[4,64,128]{2,1,0:T(8,128)(2,1)S(1)}, bf16[4,64,128]{2,1,0:T(8,128)(2,1)S(1)}, u32[]{:S(2)}, u32[]{:S(2)}) collective-permute-start(bf16[4,64,128]{2,1,0:T(8,128)(2,1)S(1)} %get-tuple-element.20), channel_id=1, source_target_pairs={{0,24},{4,28},{8,16},{12,20},{16,8},{20,12},{24,0},{28,4},{1,25},{... | collective-permute-start | bytes 196616 | tf_op jit(solution)/shard_map/ppermute | solution.py:603
  30.2 4.3 %collective-permute-start.6 = (bf16[4,64,128]{2,1,0:T(8,128)(2,1)S(1)}, bf16[4,64,128]{2,1,0:T(8,128)(2,1)S(1)}, u32[]{:S(2)}, u32[]{:S(2)}) collective-permute-start(bf16[4,64,128]{2,1,0:T(8,128)(2,1)S(1)} %get-tuple-element.20), channel_id=1, source_target_pairs={{0,16},{4,20},{8,24},{12,28},{16,0},{20,4},{24,8},{28,12},{1,17},{... | collective-permute-start | bytes 196616 | tf_op jit(solution)/shard_map/ppermute | solution.py:603
  30.7 4.3 %collective-permute-start.4 = (bf16[4,64,128]{2,1,0:T(8,128)(2,1)S(1)}, bf16[4,64,128]{2,1,0:T(8,128)(2,1)S(1)}, u32[]{:S(2)}, u32[]{:S(2)}) collective-permute-start(bf16[4,64,128]{2,1,0:T(8,128)(2,1)S(1)} %get-tuple-element.19.refs_0_), channel_id=1, source_target_pairs={{0,8},{4,12},{8,0},{12,4},{16,24},{20,28},{24,16},{28,20},{1,9},{5... | collective-permute-start | bytes 196616 | tf_op jit(solution)/shard_map/ppermute | solution.py:603
  31.3 3.7 %collective-permute-start.3 = (bf16[4,64,128]{2,1,0:T(8,128)(2,1)S(1)}, bf16[4,64,128]{2,1,0:T(8,128)(2,1)S(1)}, u32[]{:S(2)}, u32[]{:S(2)}) collective-permute-start(bf16[4,64,128]{2,1,0:T(8,128)(2,1)S(1)} %get-tuple-element.19.refs_0_), channel_id=1, source_target_pairs={{0,4},{4,0},{8,12},{12,8},{16,20},{20,16},{24,28},{28,24},{1,5},{5... | collective-permute-start | bytes 196616 | tf_op jit(solution)/shard_map/ppermute | solution.py:603
  33.3 1.7 %collective-permute-start.9 = (bf16[4,64,128]{2,1,0:T(8,128)(2,1)S(1)}, bf16[4,64,128]{2,1,0:T(8,128)(2,1)S(1)}, u32[]{:S(2)}, u32[]{:S(2)}) collective-permute-start(bf16[4,64,128]{2,1,0:T(8,128)(2,1)S(1)} %collective-permute-done.8.refs_6_), channel_id=1, source_target_pairs={{0,4},{4,0},{8,12},{12,8},{16,20},{20,16},{24,28},{28,24},{1,5},{5... | collective-permute-start | bytes 196616 | tf_op jit(solution)/shard_map/ppermute | solution.py:603
  34.5 1.3 %collective-permute-start.7 = (bf16[4,64,128]{2,1,0:T(8,128)(2,1)S(1)}, bf16[4,64,128]{2,1,0:T(8,128)(2,1)S(1)}, u32[]{:S(2)}, u32[]{:S(2)}) collective-permute-start(bf16[4,64,128]{2,1,0:T(8,128)(2,1)S(1)} %collective-permute-done.6.refs_4_), channel_id=1, source_target_pairs={{0,4},{4,0},{8,12},{12,8},{16,20},{20,16},{24,28},{28,24},{1,5},{5... | collective-permute-start | bytes 196616 | tf_op jit(solution)/shard_map/ppermute | solution.py:603
  35.0 1.3 %collective-permute-start.5 = (bf16[4,64,128]{2,1,0:T(8,128)(2,1)S(1)}, bf16[4,64,128]{2,1,0:T(8,128)(2,1)S(1)}, u32[]{:S(2)}, u32[]{:S(2)}) collective-permute-start(bf16[4,64,128]{2,1,0:T(8,128)(2,1)S(1)} %collective-permute-done.4.refs_2_), channel_id=1, source_target_pairs={{0,4},{4,0},{8,12},{12,8},{16,20},{20,16},{24,28},{28,24},{1,5},{5... | collective-permute-start | bytes 196616 | tf_op jit(solution)/shard_map/ppermute | solution.py:603

commit v11 on v10

--- a/solution.py
+++ b/solution.py
@@ -417,7 +417,7 @@
 
     def pair_scores(seq, tile):
         here = span(tile)
-        slot = tile % 2
+        slot = tile % 3
         teacher = nt(key_rows[flat(seq, slice(0, here.stop)), :], query_rows[flat(seq, here), :])
         student = nn(
             side_by_side(key_feature_rows(seq, half, here.stop) for half in range(2)),
@@ -448,7 +448,7 @@
 
     def pair_gradients(seq, tile, half, stats):
         highest, linear_sum = stats
-        slot = tile % 2
+        slot = tile % 3
         at = tile * width + half
         denominator = None
         for number in range(at + 1):
@@ -525,12 +525,12 @@
 
     def pair_steps(seq):
         order = list(reversed(range(tiles)))
-        ahead = pair_scores(seq, order[0])
+        ahead = [pair_scores(seq, order[0])]
         behind = None
         for number, tile in enumerate(order):
-            stats = ahead
-            if number + 1 < tiles:
-                ahead = pair_scores(seq, order[number + 1])
+            while number + len(ahead) < min(number + 3, tiles):
+                ahead.append(pair_scores(seq, order[number + len(ahead)]))
+            stats = ahead.pop(0)
             for half in range(width):
                 pair_gradients(seq, tile, half, stats[half])
                 yield
@@ -668,8 +668,8 @@
             pltpu.VMEM((sequences, seq_count, 2 * HEAD_SIZE, BLK), BF16),
             pltpu.VMEM((max(sequences - early, 1), 2, seq_tokens, HEAD_SIZE), BF16),
             pltpu.VMEM((sequences, seq_count, seq_tokens, BLK), BF16),
-            pltpu.VMEM((sequences, 2, seq_tokens, 2 * BLK), F32),
-            pltpu.VMEM((sequences, 2, seq_tokens, 2 * BLK), F32),
+            pltpu.VMEM((sequences, 3, seq_tokens, 2 * BLK), F32),
+            pltpu.VMEM((sequences, 3, seq_tokens, 2 * BLK), F32),
             pltpu.VMEM((HEAD_SIZE, HEAD_SIZE), F32),
             pltpu.VMEM((HEAD_SIZE, HEAD_SIZE), F32),
         ],

time: 55.9 us -> 56 us (level)
  no operation moved by 1% of the time
where the time goes in v11:
time: 56 us; the launch traced here: 55.7 us
  waiting for transfers between devices  17.9 us (32%)
  starting transfers between devices  15.3 us (27%)
  Pallas kernels  11.3 us (20%)
  blocking collectives  10.4 us (19%)
  between operations  0.75 us (1%)
    ppermute x10, waiting for transfers between devices, swap(): return lax.ppermute(piece, axis, [(i, i ^ bits) for i in range(size)])  17.9 us
    all_gather x1, blocking collectives, per_device_head(): everyone = lax.all_gather(grads, 'seq', axis=0, tiled=False)  10.4 us
    ppermute x10, starting transfers between devices, swap(): return lax.ppermute(piece, axis, [(i, i ^ bits) for i in range(size)])  8.02 us
    all_to_all x1, starting transfers between devices, per_device_head(): lax.all_to_all(sent, ('seq', 'head'), split_axis=0, concat_axis=0, tiled=...  7.33 us
    pallas_call x1, Pallas kernels, per_device_head(): pl.pallas_call(functools.partial(pair_kernel, token_count, seq_count), ou...  6.68 us
    pallas_call x1, Pallas kernels, per_device_head(): pl.pallas_call(functools.partial(send_kernel, seq_count), out_shape=[jax....  2.26 us
    pallas_call x1, Pallas kernels, per_device_head(): pl.pallas_call(functools.partial(key_kernel, share), out_shape=(jax.Shape...  1.41 us
  transfers between devices with their start and end apart: 11, of which 7 were waited for; matrix products, arithmetic and copies ran while one was open for 0% of the time, Pallas kernels for 3%

profile of v11, /device:TPU:0, one launch (start us, length us, event | category | flops | bytes accessed | tf_op | source)
XLA Modules:
  0.0 55.7 jit_solution(122175032352945549)
XLA Ops:
  0.6 2.3 %shard_map.68 = (bf16[32,64,128]{2,1,0:T(8,128)(2,1)}, bf16[2,64,128]{2,1,0:T(8,128)(2,1)}, bf16[2,64,128]{2,1,0:T(8,128)(2,1)}, bf16[2,64,128]{2,1,0:T(8,128)(2,1)}, bf16[2,64,128]{2,1,0:T(8,128)(2,1)}) custom-call(bf16[64,4096]{1,0:T(8,128)(2,1)} %queries_ref.1, bf16[64,1024]{1,0:T(8,128)(2,1)} %keys_ref.1), custom_call_target="tpu_custom_call" | custom-call | tf_op jit(solution)/shard_map/pallas_call | solution.py:607
  2.9 0.0 copy-start.2
  2.9 0.0 copy-start
  2.9 7.3 %all-to-all-start = ((bf16[32,64,128]{2,1,0:T(8,128)(2,1)}), bf16[32,64,128]{2,1,0:T(8,128)(2,1)S(1)}, u32[]{:S(2)}, u32[]{:S(2)}) async-start(bf16[32,64,128]{2,1,0:T(8,128)(2,1)} %get-tuple-element.14), calls=%async_computation | async-start | bytes 1048576 | tf_op jit(solution)/shard_map/all_to_all | solution.py:624
  10.3 0.0 copy-start.1
  10.3 1.8 %collective-permute-start = (bf16[2,64,128]{2,1,0:T(8,128)(2,1)S(1)}, bf16[2,64,128]{2,1,0:T(8,128)(2,1)S(1)}, u32[]{:S(2)}, u32[]{:S(2)}) collective-permute-start(bf16[2,64,128]{2,1,0:T(8,128)(2,1)S(1)} %copy-done.6), channel_id=1, source_target_pairs={{0,1},{1,0},{2,3},{3,2},{4,5},{5,4},{6,7},{7,6},{8,9},{9,8},{10,11... | collective-permute-start | bytes 98312 | tf_op jit(solution)/shard_map/ppermute | solution.py:603
  12.1 2.4 %collective-permute-start.1 = (bf16[2,64,128]{2,1,0:T(8,128)(2,1)S(1)}, bf16[2,64,128]{2,1,0:T(8,128)(2,1)S(1)}, u32[]{:S(2)}, u32[]{:S(2)}) collective-permute-start(bf16[2,64,128]{2,1,0:T(8,128)(2,1)S(1)} %copy-done.5), channel_id=1, source_target_pairs={{0,2},{1,3},{2,0},{3,1},{4,6},{5,7},{6,4},{7,5},{8,10},{9,11},{10,... | collective-permute-start | bytes 98312 | tf_op jit(solution)/shard_map/ppermute | solution.py:603
  14.6 0.2 collective-permute-start.2
  14.8 5.7 %collective-permute-done.refs_1_ = bf16[2,64,128]{2,1,0:T(8,128)(2,1)S(1)} collective-permute-done((bf16[2,64,128]{2,1,0:T(8,128)(2,1)S(1)}, bf16[2,64,128]{2,1,0:T(8,128)(2,1)S(1)}, u32[]{:S(2)}, u32[]{:S(2)}) %collective-permute-start) | collective-permute-done | bytes 32800 | tf_op jit(solution)/shard_map/ppermute | solution.py:603
  20.5 7.3 %collective-permute-done.1.refs_2_ = bf16[2,64,128]{2,1,0:T(8,128)(2,1)S(1)} collective-permute-done((bf16[2,64,128]{2,1,0:T(8,128)(2,1)S(1)}, bf16[2,64,128]{2,1,0:T(8,128)(2,1)S(1)}, u32[]{:S(2)}, u32[]{:S(2)}) %collective-permute-start.1) | collective-permute-done | bytes 32800 | tf_op jit(solution)/shard_map/ppermute | solution.py:603
  27.7 0.0 collective-permute-done.2.refs_3_
  27.7 0.0 copy-start.3
  27.7 2.5 %collective-permute-start.8 = (bf16[4,64,128]{2,1,0:T(8,128)(2,1)S(1)}, bf16[4,64,128]{2,1,0:T(8,128)(2,1)S(1)}, u32[]{:S(2)}, u32[]{:S(2)}) collective-permute-start(bf16[4,64,128]{2,1,0:T(8,128)(2,1)S(1)} %get-tuple-element.20), channel_id=1, source_target_pairs={{0,24},{4,28},{8,16},{12,20},{16,8},{20,12},{24,0},{28,4},{1,25},{... | collective-permute-start | bytes 196616 | tf_op jit(solution)/shard_map/ppermute | solution.py:603
  30.2 0.5 collective-permute-start.6
  30.7 0.6 %collective-permute-start.4 = (bf16[4,64,128]{2,1,0:T(8,128)(2,1)S(1)}, bf16[4,64,128]{2,1,0:T(8,128)(2,1)S(1)}, u32[]{:S(2)}, u32[]{:S(2)}) collective-permute-start(bf16[4,64,128]{2,1,0:T(8,128)(2,1)S(1)} %get-tuple-element.19.refs_0_), channel_id=1, source_target_pairs={{0,8},{4,12},{8,0},{12,4},{16,24},{20,28},{24,16},{28,20},{1,9},{5... | collective-permute-start | bytes 196616 | tf_op jit(solution)/shard_map/ppermute | solution.py:603
  31.3 2.0 %collective-permute-done.8.refs_6_ = bf16[4,64,128]{2,1,0:T(8,128)(2,1)S(1)} collective-permute-done((bf16[4,64,128]{2,1,0:T(8,128)(2,1)S(1)}, bf16[4,64,128]{2,1,0:T(8,128)(2,1)S(1)}, u32[]{:S(2)}, u32[]{:S(2)}) %collective-permute-start.8) | collective-permute-done | bytes 65568 | tf_op jit(solution)/shard_map/ppermute | solution.py:603
  33.3 1.1 %collective-permute-done.6.refs_4_ = bf16[4,64,128]{2,1,0:T(8,128)(2,1)S(1)} collective-permute-done((bf16[4,64,128]{2,1,0:T(8,128)(2,1)S(1)}, bf16[4,64,128]{2,1,0:T(8,128)(2,1)S(1)}, u32[]{:S(2)}, u32[]{:S(2)}) %collective-permute-start.6) | collective-permute-done | bytes 65568 | tf_op jit(solution)/shard_map/ppermute | solution.py:603
  34.5 0.5 collective-permute-done.4.refs_2_
  35.0 0.7 %collective-permute-done.7.refs_5_ = bf16[4,64,128]{2,1,0:T(8,128)(2,1)S(1)} collective-permute-done((bf16[4,64,128]{2,1,0:T(8,128)(2,1)S(1)}, bf16[4,64,128]{2,1,0:T(8,128)(2,1)S(1)}, u32[]{:S(2)}, u32[]{:S(2)}) %collective-permute-start.7) | collective-permute-done | bytes 65568 | tf_op jit(solution)/shard_map/ppermute | solution.py:603
  35.7 0.5 collective-permute-done.5.refs_3_
  36.3 1.4 %shard_map.70 = (bf16[2048,128]{1,0:T(8,128)(2,1)S(1)}, f32[1,256,1024]{2,1,0:T(8,128)S(1)}, bf16[1,2,1024,128]{3,2,1,0:T(8,128)(2,1)S(1)}, f32[128,128]{1,0:T(8,128)S(1)}, f32[128,128]{1,0:T(8,128)S(1)}) custom-call(s32[16]{0:T(128)S(1)} %copy-done.3, f32[2,128,128]{2,1,0:T(8,128)S(1)} %copy-done.1, f32[8,128,128]{2,1,0:T(8,128)S(1)} %copy-done, ...), custom_call_target="tpu_custom_call" | custom-call | flops 201326592 | bytes 3145728 | tf_op jit(solution)/shard_map/pallas_call | solution.py:640
  37.7 6.7 %shard_map.71 = bf16[384,128]{1,0:T(8,128)(2,1)S(1)} custom-call(s32[16]{0:T(128)S(1)} %copy-done.3, bf16[32,64,128]{2,1,0:T(8,128)(2,1)S(1)} %all-to-all-done.arrived_ref, f32[128,128]{1,0:T(8,128)S(1)} %get-tuple-element.21.query_weights_ref, f32[128,128]{1,0:T(8,128)S(1)} %get-tuple-element.22.key_weights_ref, ...), custom_call_target="tpu_custom_call" | custom-call | tf_op jit(solution)/shard_map/pallas_call | solution.py:658
  44.4 10.4 %all-gather = bf16[3072,128]{1,0:T(8,128)(2,1)S(1)} all-gather(bf16[384,128]{1,0:T(8,128)(2,1)S(1)} %shard_map.71), channel_id=2, replica_groups=mesh['seq'=8,'head'=4] {'seq'}, dimensions={0}, use_global_device_ids=true | all-gather | bytes 884736 | tf_op jit(solution)/shard_map/all_gather | solution.py:678
  54.8 0.9 %shard_map.72 = (f32[8,128,128]{2,1,0:T(8,128)}, f32[2,128,128]{2,1,0:T(8,128)}) custom-call(bf16[8,384,128]{2,1,0:T(8,128)(2,1)S(1)} %bitcast.1), custom_call_target="tpu_custom_call" | custom-call | tf_op jit(solution)/shard_map/pallas_call | solution.py:679
  (18 shorter events, 0.0 us)
Async XLA Ops:
  2.9 7.4 %copy-start.6 = (bf16[2,64,128]{2,1,0:T(8,128)(2,1)S(1)}, bf16[2,64,128]{2,1,0:T(8,128)(2,1)}, u32[]{:S(2)}) copy-start(bf16[2,64,128]{2,1,0:T(8,128)(2,1)} %get-tuple-element.16) | copy-start | bytes 98308
  2.9 9.2 %copy-start.5 = (bf16[2,64,128]{2,1,0:T(8,128)(2,1)S(1)}, bf16[2,64,128]{2,1,0:T(8,128)(2,1)}, u32[]{:S(2)}) copy-start(bf16[2,64,128]{2,1,0:T(8,128)(2,1)} %get-tuple-element.17) | copy-start | bytes 98308
  2.9 11.7 %copy-start.4 = (bf16[2,64,128]{2,1,0:T(8,128)(2,1)S(1)}, bf16[2,64,128]{2,1,0:T(8,128)(2,1)}, u32[]{:S(2)}) copy-start(bf16[2,64,128]{2,1,0:T(8,128)(2,1)} %get-tuple-element.18) | copy-start | bytes 98308
  2.9 24.8 %copy-start.2 = (bf16[2,64,128]{2,1,0:T(8,128)(2,1)S(1)}, bf16[2,64,128]{2,1,0:T(8,128)(2,1)}, u32[]{:S(2)}) copy-start(bf16[2,64,128]{2,1,0:T(8,128)(2,1)} %get-tuple-element.15.refs_0_) | copy-start | bytes 98308
  2.9 33.3 %copy-start = (f32[8,128,128]{2,1,0:T(8,128)S(1)}, f32[8,128,128]{2,1,0:T(8,128)}, u32[]{:S(2)}) copy-start(f32[8,128,128]{2,1,0:T(8,128)} %query_map_ref.1) | copy-start | bytes 1572868
  2.9 34.7 %all-to-all-start = ((bf16[32,64,128]{2,1,0:T(8,128)(2,1)}), bf16[32,64,128]{2,1,0:T(8,128)(2,1)S(1)}, u32[]{:S(2)}, u32[]{:S(2)}) async-start(bf16[32,64,128]{2,1,0:T(8,128)(2,1)} %get-tuple-element.14), calls=%async_computation | async-start | bytes 1048576 | tf_op jit(solution)/shard_map/all_to_all | solution.py:624
  10.3 26.0 %copy-start.1 = (f32[2,128,128]{2,1,0:T(8,128)S(1)}, f32[2,128,128]{2,1,0:T(8,128)}, u32[]{:S(2)}) copy-start(f32[2,128,128]{2,1,0:T(8,128)} %key_map_ref.1) | copy-start | bytes 393220
  10.3 10.2 %collective-permute-start = (bf16[2,64,128]{2,1,0:T(8,128)(2,1)S(1)}, bf16[2,64,128]{2,1,0:T(8,128)(2,1)S(1)}, u32[]{:S(2)}, u32[]{:S(2)}) collective-permute-start(bf16[2,64,128]{2,1,0:T(8,128)(2,1)S(1)} %copy-done.6), channel_id=1, source_target_pairs={{0,1},{1,0},{2,3},{3,2},{4,5},{5,4},{6,7},{7,6},{8,9},{9,8},{10,11... | collective-permute-start | bytes 98312 | tf_op jit(solution)/shard_map/ppermute | solution.py:603
  12.1 15.6 %collective-permute-start.1 = (bf16[2,64,128]{2,1,0:T(8,128)(2,1)S(1)}, bf16[2,64,128]{2,1,0:T(8,128)(2,1)S(1)}, u32[]{:S(2)}, u32[]{:S(2)}) collective-permute-start(bf16[2,64,128]{2,1,0:T(8,128)(2,1)S(1)} %copy-done.5), channel_id=1, source_target_pairs={{0,2},{1,3},{2,0},{3,1},{4,6},{5,7},{6,4},{7,5},{8,10},{9,11},{10,... | collective-permute-start | bytes 98312 | tf_op jit(solution)/shard_map/ppermute | solution.py:603
  14.6 13.2 %collective-permute-start.2 = (bf16[2,64,128]{2,1,0:T(8,128)(2,1)S(1)}, bf16[2,64,128]{2,1,0:T(8,128)(2,1)S(1)}, u32[]{:S(2)}, u32[]{:S(2)}) collective-permute-start(bf16[2,64,128]{2,1,0:T(8,128)(2,1)S(1)} %copy-done.4), channel_id=1, source_target_pairs={{0,3},{1,2},{2,1},{3,0},{4,7},{5,6},{6,5},{7,4},{8,11},{9,10},{10,... | collective-permute-start | bytes 98312 | tf_op jit(solution)/shard_map/ppermute | solution.py:603
  27.7 8.5 %copy-start.3 = (s32[16]{0:T(128)S(1)}, s32[16]{0:T(128)}, u32[]{:S(2)}) copy-start(s32[16]{0:T(128)} %pos_ref.3) | copy-start | bytes 196
  27.7 5.6 %collective-permute-start.8 = (bf16[4,64,128]{2,1,0:T(8,128)(2,1)S(1)}, bf16[4,64,128]{2,1,0:T(8,128)(2,1)S(1)}, u32[]{:S(2)}, u32[]{:S(2)}) collective-permute-start(bf16[4,64,128]{2,1,0:T(8,128)(2,1)S(1)} %get-tuple-element.20), channel_id=1, source_target_pairs={{0,24},{4,28},{8,16},{12,20},{16,8},{20,12},{24,0},{28,4},{1,25},{... | collective-permute-start | bytes 196616 | tf_op jit(solution)/shard_map/ppermute | solution.py:603
  30.2 4.3 %collective-permute-start.6 = (bf16[4,64,128]{2,1,0:T(8,128)(2,1)S(1)}, bf16[4,64,128]{2,1,0:T(8,128)(2,1)S(1)}, u32[]{:S(2)}, u32[]{:S(2)}) collective-permute-start(bf16[4,64,128]{2,1,0:T(8,128)(2,1)S(1)} %get-tuple-element.20), channel_id=1, source_target_pairs={{0,16},{4,20},{8,24},{12,28},{16,0},{20,4},{24,8},{28,12},{1,17},{... | collective-permute-start | bytes 196616 | tf_op jit(solution)/shard_map/ppermute | solution.py:603
  30.7 4.3 %collective-permute-start.4 = (bf16[4,64,128]{2,1,0:T(8,128)(2,1)S(1)}, bf16[4,64,128]{2,1,0:T(8,128)(2,1)S(1)}, u32[]{:S(2)}, u32[]{:S(2)}) collective-permute-start(bf16[4,64,128]{2,1,0:T(8,128)(2,1)S(1)} %get-tuple-element.19.refs_0_), channel_id=1, source_target_pairs={{0,8},{4,12},{8,0},{12,4},{16,24},{20,28},{24,16},{28,20},{1,9},{5... | collective-permute-start | bytes 196616 | tf_op jit(solution)/shard_map/ppermute | solution.py:603
  31.3 3.7 %collective-permute-start.3 = (bf16[4,64,128]{2,1,0:T(8,128)(2,1)S(1)}, bf16[4,64,128]{2,1,0:T(8,128)(2,1)S(1)}, u32[]{:S(2)}, u32[]{:S(2)}) collective-permute-start(bf16[4,64,128]{2,1,0:T(8,128)(2,1)S(1)} %get-tuple-element.19.refs_0_), channel_id=1, source_target_pairs={{0,4},{4,0},{8,12},{12,8},{16,20},{20,16},{24,28},{28,24},{1,5},{5... | collective-permute-start | bytes 196616 | tf_op jit(solution)/shard_map/ppermute | solution.py:603
  33.3 1.7 %collective-permute-start.9 = (bf16[4,64,128]{2,1,0:T(8,128)(2,1)S(1)}, bf16[4,64,128]{2,1,0:T(8,128)(2,1)S(1)}, u32[]{:S(2)}, u32[]{:S(2)}) collective-permute-start(bf16[4,64,128]{2,1,0:T(8,128)(2,1)S(1)} %collective-permute-done.8.refs_6_), channel_id=1, source_target_pairs={{0,4},{4,0},{8,12},{12,8},{16,20},{20,16},{24,28},{28,24},{1,5},{5... | collective-permute-start | bytes 196616 | tf_op jit(solution)/shard_map/ppermute | solution.py:603
  34.5 1.3 %collective-permute-start.7 = (bf16[4,64,128]{2,1,0:T(8,128)(2,1)S(1)}, bf16[4,64,128]{2,1,0:T(8,128)(2,1)S(1)}, u32[]{:S(2)}, u32[]{:S(2)}) collective-permute-start(bf16[4,64,128]{2,1,0:T(8,128)(2,1)S(1)} %collective-permute-done.6.refs_4_), channel_id=1, source_target_pairs={{0,4},{4,0},{8,12},{12,8},{16,20},{20,16},{24,28},{28,24},{1,5},{5... | collective-permute-start | bytes 196616 | tf_op jit(solution)/shard_map/ppermute | solution.py:603
  35.0 1.3 %collective-permute-start.5 = (bf16[4,64,128]{2,1,0:T(8,128)(2,1)S(1)}, bf16[4,64,128]{2,1,0:T(8,128)(2,1)S(1)}, u32[]{:S(2)}, u32[]{:S(2)}) collective-permute-start(bf16[4,64,128]{2,1,0:T(8,128)(2,1)S(1)} %collective-permute-done.4.refs_2_), channel_id=1, source_target_pairs={{0,4},{4,0},{8,12},{12,8},{16,20},{20,16},{24,28},{28,24},{1,5},{5... | collective-permute-start | bytes 196616 | tf_op jit(solution)/shard_map/ppermute | solution.py:603
